TPU v7x, 32 devices: a whole 2x2x4 slice. The times are simulated.
32 devices in a mesh: drive: 2 (over y), tm: 4 (over z), mom: 2 (over x), col: 2 (over core).
Axes of the slice: x: 2, y: 2, z: 4, core: 2. Of those that a mesh axis runs over, the one named last changes fastest.
Arguments:
- propagators: float32 [8, 8, 384, 384], P(('drive', 'mom'), 'tm', None, 'col'), parts along dimension 0, as said below
- current_op: float32 [4, 384, 384], P('mom'), may hold values from -6 to 6
Outputs:
- spectrum: float32 [8, 2, 8, 384, 384], P(('drive', 'mom'), None, None, 'tm', 'col'), parts along dimension 0
There are 2 independent parts, one for each index of `drive`. A program takes and returns all parts, laid end to end along the dimension named above; an argument that names none is the same for every part. Nothing has to cross between parts.
Inputs may be any that keep to these rules, and one draw needn't show every extreme that they name: Every matrix propagators[k, t] is orthogonal to float32 rounding, with dense entries.
All inputs are finite; a program needn't handle non-finite values.
Results may differ from a plain program's by a relative error of at most 0.0003.
Values sent between devices are 32-bit elements; how exact they have to be, the bound alone decides.
No kernel may reach another device: no remote copies, remote signals or barrier semaphores. Data moves between devices by JAX's collectives and lax.ppermute only.
A program may use at most 64 MiB of HBM per device.

v0:
```python
import math

import jax
import jax.numpy as jnp
from jax import lax
from jax.experimental import pallas as pl
from jax.experimental.pallas import tpu as pltpu
from jax.sharding import PartitionSpec as P


CHUNKS = 3
GRANT = pltpu.CompilerParams(vmem_limit_bytes=20 * 2**20)


def prefix_2(value, axis, join, neutral):
    count, mine = (lax.axis_size(axis), lax.axis_index(axis))
    pieces = lax.all_gather(value, axis)
    running = jnp.full_like(value, 0) + jnp.asarray(neutral, value.dtype)

    def turn(position, running):
        longer = join(running, pieces[position])
        return jnp.where(position < mine, longer, running)

    return lax.fori_loop(0, count - 1, turn, running)


def multiply(left, right):
    return jnp.einsum("kab,kbc->kac", left, right, precision=lax.Precision.HIGHEST)


def later_first(earlier, later):
    return multiply(later, earlier)


def chain_step(carry, unit):
    nxt = multiply(unit, carry)
    return (nxt, nxt)


def spectrum_block(block):
    length = block.shape[1]
    freq = lax.broadcasted_iota(jnp.int32, (length, length), 0)
    times = lax.broadcasted_iota(jnp.int32, (length, length), 1)
    phase = 2.0 * math.pi / length * (freq * times % length).astype(jnp.float32)
    scale = 1.0 / math.sqrt(length)
    cosine = jnp.cos(phase) * scale
    sine = -jnp.sin(phase) * scale
    real = jnp.einsum("ft,ktrc->kfrc", cosine, block, precision=lax.Precision.HIGHEST)
    imag = jnp.einsum("ft,ktrc->kfrc", sine, block, precision=lax.Precision.HIGHEST)
    return jnp.stack([real, imag], axis=1)


def general_body(propagators, current_op):
    sym = 0.5 * (current_op + jnp.swapaxes(current_op, 1, 2))
    whole = lax.all_to_all(propagators, "col", split_axis=1, concat_axis=3, tiled=True)
    kdev = whole.shape[0]
    order = whole.shape[2]
    units = jnp.moveaxis(whole, 1, 0)
    total = units[0]
    identity = jnp.broadcast_to(jnp.eye(order, dtype=jnp.float32), total.shape)
    carry_in = prefix_2(total, ("tm", "col"), later_first, identity)
    _, applied = lax.scan(chain_step, carry_in, units)
    prefix = jnp.moveaxis(applied, 0, 1)
    weighted = jnp.einsum("kab,ksbc->ksac", sym, prefix, precision=lax.Precision.HIGHEST)
    n_rows = lax.axis_size("tm")
    n_cols = lax.axis_size("col")
    row_width = order // n_rows
    col_width = order // n_cols
    slices = prefix.shape[1]
    left = prefix.reshape(kdev, slices, order, n_rows, row_width)
    right = weighted.reshape(kdev, slices, order, n_cols, col_width)
    heis = jnp.einsum("ksbir,ksbjq->ksijrq", left, right, precision=lax.Precision.HIGHEST)
    heis = heis.reshape(kdev, slices, n_rows * n_cols, row_width, col_width)
    block = lax.all_to_all(heis, ("tm", "col"), split_axis=2, concat_axis=1, tiled=True)
    return spectrum_block(block[:, :, 0])


def halves(x):
    high = x.astype(jnp.bfloat16)
    return high, (x - high.astype(jnp.float32)).astype(jnp.bfloat16)


def as_left(x):
    high, low = halves(x)
    return jnp.concatenate([high, high, low], axis=1)


def as_right(x):
    high, low = halves(x)
    return jnp.concatenate([high, low, high], axis=0)


def as_right_t(x):
    high, low = halves(x)
    return jnp.concatenate([high, low, high], axis=1)


def product(left, right):
    return jnp.dot(left, right, preferred_element_type=jnp.float32)


def product_t(left, right):
    dims = (((1,), (1,)), ((), ()))
    return lax.dot_general(left, right, dims, preferred_element_type=jnp.float32)


VMEM = pl.BlockSpec(memory_space=pltpu.VMEM)


def local_call(kernel, outs, args, scratch=(), outside=()):
    near = [
        x if i in outside else pltpu.with_memory_space_constraint(x, pltpu.VMEM)
        for i, x in enumerate(args)
    ]
    return pl.pallas_call(
        kernel,
        out_shape=[pltpu.VMEM(s, jnp.float32) for s in outs],
        in_specs=[VMEM] * len(args),
        out_specs=[VMEM] * len(outs),
        scratch_shapes=list(scratch),
        compiler_params=GRANT,
    )(*near)


def pick_kernel(in_ref, mine_ref, other_ref, sems):
    core = lax.axis_index("col")
    copies = [
        pltpu.make_async_copy(in_ref.at[1 - core], other_ref, sems.at[0]),
        pltpu.make_async_copy(in_ref.at[core], mine_ref, sems.at[1]),
    ]
    for copy in copies:
        copy.start()
    for copy in copies:
        copy.wait()


def start_kernel(mine_ref, got_ref, a0_ref, *refs):
    *prod_refs, a1_ref = refs
    core = lax.axis_index("col")
    part = got_ref.shape[1]
    for s, a_ref in enumerate((a0_ref, a1_ref)):
        a_ref[pl.ds(pl.multiple_of(core * part, 8), part), :] = mine_ref[s]
        a_ref[pl.ds(pl.multiple_of((1 - core) * part, 8), part), :] = got_ref[s]
    right = as_right(a1_ref[...])
    row = 0
    for p_ref in prod_refs:
        rows = p_ref.shape[0]
        p_ref[...] = product(as_left(a0_ref[row:row + rows, :]), right)
        row += rows


def packed(x):
    third = x.shape[0] // 3
    lower = jnp.concatenate([x[third:2 * third, third:], x[2 * third:, 2 * third:]], axis=1)
    return jnp.concatenate([x[:third, :], lower], axis=0)


def unpacked(x):
    third = x.shape[0] // 2
    top = x[:third, :]
    b11, b12, b22 = (x[third:, i * third:(i + 1) * third] for i in range(3))
    middle = jnp.concatenate([top[:, third:2 * third].T, b11, b12], axis=1)
    bottom = jnp.concatenate([top[:, 2 * third:].T, b12.T, b22], axis=1)
    return jnp.concatenate([top, middle, bottom], axis=0)


def local_kernel(chunks, *refs):
    a0_ref, *prod_refs, op_ref = refs[:chunks + 2]
    sym_ref, g0_ref, g1_ref, pack_ref, own_ref, *row_refs = refs[chunks + 2:]
    place = lax.axis_index("tm")
    op = op_ref[lax.axis_index("col")]
    sym = 0.5 * (op + op.T)
    sym_ref[...] = sym
    right = as_right(sym)
    a0 = a0_ref[...]
    b = jnp.concatenate([r[...] for r in prod_refs], axis=0)
    for x, g_ref in ((a0, g0_ref), (b, g1_ref)):
        g_ref[...] = product_t(as_left(product(as_left(x), right)), as_right_t(x))
    rows = own_ref.shape[1]

    @pl.when(place >= 2)
    def _():
        pack_ref[0] = packed(g0_ref[...])
        pack_ref[1] = packed(g1_ref[...])

    @pl.when(place == 0)
    def _():
        own_ref[0] = g0_ref[:rows, :]
        own_ref[1] = g1_ref[:rows, :]
        for i, row_ref in enumerate(row_refs):
            row_ref[0] = g0_ref[(i + 1) * rows:(i + 2) * rows, :]


def hop_kernel(place, in_ref, *refs):
    *prod_refs, out_ref = refs

    @pl.when(lax.axis_index("tm") == place)
    def _():
        b = jnp.concatenate([r[...] for r in prod_refs], axis=0)
        out_ref[...] = product(as_left(in_ref[...]), as_right(b))


def joined(out_ref, parts):
    row = 0
    for part in parts:
        out_ref[row:row + part.shape[0], :] = part[...]
        row += part.shape[0]


def rows_out(outs, wanted, heis, top, rows):
    for to, position in wanted.items():
        outs[to][position] = heis[to * rows - top:(to + 1) * rows - top, :]


def heis_kernel(place, count, chunks, *refs):
    sym_ref, g0_ref, g1_ref = refs[:3]
    before = refs[3:3 + chunks]
    outs, r_ref, t_ref = refs[3 + chunks:-2], refs[-2], refs[-1]
    outs = dict(zip(heis_receivers(place, count), outs))

    @pl.when(lax.axis_index("tm") == place)
    def _():
        order = sym_ref.shape[0]
        rows = order // count
        joined(r_ref, before)
        t_ref[...] = as_right_t(r_ref[...])
        for i, middle_ref in enumerate((sym_ref, g0_ref, g1_ref)):
            t = 2 * place - 1 + i
            wanted = {to: heis_slices(place, to).index(t) for to in outs if t in heis_slices(place, to)}
            top, bottom = min(wanted) * rows, (max(wanted) + 1) * rows
            weighted = product(as_left(r_ref[top:bottom, :]), as_right(middle_ref[...]))
            rows_out(outs, wanted, product_t(as_left(weighted), t_ref[...]), top, rows)


def ahead_kernel(place, count, chunks, *refs):
    pack_ref, *after = refs[:1 + chunks]
    outs, r_ref, t_ref = refs[1 + chunks:-2], refs[-2], refs[-1]

    @pl.when(lax.axis_index("tm") == place)
    def _():
        order = pack_ref.shape[2]
        rows = order // count
        joined(r_ref, after)
        t_ref[...] = as_right_t(r_ref[...])
        left = as_left(r_ref[:(place + 1) * rows, :])
        for i in range(2):
            weighted = product(left, as_right(unpacked(pack_ref[i])))
            heis = product_t(as_left(weighted), t_ref[...])
            rows_out(outs, {to: i for to in range(place + 1)}, heis, 0, rows)


def heis_slices(place, to):
    if to > place:
        return [2 * place - 1, 2 * place]
    if to == place:
        return [2 * place - 1, 2 * place, 2 * place + 1]
    return [2 * place, 2 * place + 1]


def heis_receivers(place, count):
    return [0] * (place == 1) + list(range(place, count))


def gather_kernel(plan, *refs):
    ins, (keep_ref, send_ref) = refs[:-2], refs[-2:]
    core = lax.axis_index("col")
    width = keep_ref.shape[2]
    for to, entries in enumerate(plan):
        @pl.when(lax.axis_index("tm") == to)
        def _(entries=entries):
            for c in range(2):
                @pl.when(core == c)
                def _(c=c):
                    for source, slices in entries:
                        for i, t in enumerate(slices):
                            block = ins[source][i]
                            keep_ref[t] = block[:, c * width:(c + 1) * width]
                            send_ref[t] = block[:, (1 - c) * width:(2 - c) * width]


def spectrum_kernel(keep_ref, got_ref, out_ref):
    core = lax.axis_index("col")
    length, rows, _ = keep_ref.shape
    scale = 1.0 / math.sqrt(length)
    step = 8

    def cosine(n):
        return scale * math.cos(2.0 * math.pi * (n % length) / length)

    def sine(n):
        return scale * math.sin(2.0 * math.pi * (n % length) / length)

    def block(source, k, row):
        here = pl.ds(pl.multiple_of(row * step, step), step)
        values = [source[t, here, :] for t in range(length)]
        for f in range(length // 2 + 1):
            real = sum(cosine(f * t) * values[t] for t in range(length))
            out_ref[k, 0, f, here, :] = real
            mirrored = (length - f) % length
            if mirrored != f:
                imag = sum(-sine(f * t) * values[t] for t in range(1, length))
                out_ref[k, 0, mirrored, here, :] = real
                out_ref[k, 1, f, here, :] = imag
                out_ref[k, 1, mirrored, here, :] = -imag
            else:
                imag = sum(-sine(f * t) * values[t] for t in range(length))
                out_ref[k, 1, f, here, :] = imag

    def turn(row, carry):
        block(keep_ref, core, row)
        block(got_ref, 1 - core, row)
        return carry

    lax.fori_loop(0, rows // step, turn, 0)


def paired_body(propagators, current_op):
    count = lax.axis_size("tm")
    flipped = jnp.swapaxes(propagators, 2, 3)
    kdev, slices, part, order = flipped.shape
    rows = order // count
    step = order // CHUNKS
    square, chunk = (order, order), (step, order)
    swap = [(0, 1), (1, 0)]
    scratch = [pltpu.VMEM(square, jnp.float32), pltpu.VMEM((order, 3 * order), jnp.bfloat16)]

    mine, other = pl.pallas_call(
        pick_kernel,
        out_shape=[pltpu.VMEM((slices, part, order), jnp.float32)] * 2,
        in_specs=[pl.BlockSpec(memory_space=pltpu.HBM)],
        out_specs=[VMEM] * 2,
        scratch_shapes=[pltpu.SemaphoreType.DMA((2,))],
        compiler_params=GRANT,
        name="pick",
    )(pltpu.with_memory_space_constraint(flipped, pltpu.HBM))
    got = lax.ppermute(other, "col", swap)
    a0, *prod = local_call(
        start_kernel, [square] + [chunk] * CHUNKS, (mine, got),
        scratch=[pltpu.VMEM(square, jnp.float32)],
    )

    def along(x, hop):
        return lax.ppermute(x, "tm", [hop] if isinstance(hop, tuple) else hop)

    arrays, plan = [], [[] for _ in range(count)]

    def keep(x, to, ts):
        plan[to].append((len(arrays), ts))
        arrays.append(x)

    before = [along(x, (0, 1)) for x in prod]
    shapes = [square] * 3 + [(2, 2 * (order // 3), order), (2, rows, order)] + [(1, rows, order)] * (count - 1)
    sym, g0, g1, pack, own, *firsts = local_call(
        lambda *r: local_kernel(CHUNKS, *r), shapes, (a0, *prod, current_op),
        outside=(CHUNKS + 1,),
    )
    ahead = along(pack, [(j, j - 1) for j in range(2, count)])
    keep(own, 0, [0, 1])
    for to in range(1, count):
        keep(along(firsts[to - 1], (0, to)), to, [0])
    for place in range(1, count):
        after = []
        for x in before if place + 1 < count else ():
            after += local_call(lambda *r, p=place: hop_kernel(p, *r), [chunk], (x, *prod))
        if place + 1 < count:
            following = [along(x, (place, place + 1)) for x in after]
        receivers = heis_receivers(place, count)
        outs = local_call(
            lambda *r, p=place: heis_kernel(p, count, CHUNKS, *r),
            [(len(heis_slices(place, to)), rows, order) for to in receivers],
            (sym, g0, g1, *before), scratch=scratch,
        )
        for to, x in zip(receivers, outs):
            keep(x if to == place else along(x, (place, to)), to, heis_slices(place, to))
        if place + 1 < count:
            outs = local_call(
                lambda *r, p=place: ahead_kernel(p, count, CHUNKS, *r),
                [(2, rows, order)] * (place + 1), (ahead, *after), scratch=scratch,
            )
            for to, x in enumerate(outs):
                ts = [2 * place + 2, 2 * place + 3]
                keep(x if to == place else along(x, (place, to)), to, ts)
            before = following
    width = order // 2
    kept, give = local_call(lambda *r: gather_kernel(plan, *r), [(count * slices, rows, width)] * 2, arrays)
    taken = lax.ppermute(give, "col", swap)
    return pl.pallas_call(
        spectrum_kernel,
        out_shape=jax.ShapeDtypeStruct((kdev, 2, count * slices, rows, width), jnp.float32),
        in_specs=[VMEM] * 2,
        out_specs=VMEM,
        compiler_params=GRANT,
        name="spectrum",
    )(*(pltpu.with_memory_space_constraint(x, pltpu.VMEM) for x in (kept, taken)))


def is_paired(mesh, kdev, slices, order):
    count = mesh.shape["tm"]
    fits = kdev == 2 and mesh.shape["col"] == 2 and slices == 2 and count > 2
    return fits and order % 384 == 0 and order % (16 * CHUNKS) == 0 and order % (16 * count) == 0


def solution(mesh):
    def body(propagators, current_op):
        kdev, slices, order, _ = propagators.shape
        if is_paired(mesh, kdev, slices, order):
            return paired_body(propagators, current_op)
        return general_body(propagators, current_op)

    return jax.shard_map(
        body,
        mesh=mesh,
        in_specs=(P(("drive", "mom"), "tm", None, "col"), P("mom", None, None)),
        out_specs=P(("drive", "mom"), None, None, "tm", "col"),
        check_vma=False,
    )
```

profile of v0, /device:TPU:0, one launch (start us, length us, event | category | flops | bytes accessed | tf_op | source)
XLA Modules:
  0.0 74.5 jit_solution(10653408889707349559)
XLA Ops:
  0.0 1.4 %pick.1 = (f32[2,192,384]{2,1,0:T(8,128)S(1)}, f32[2,192,384]{2,1,0:T(8,128)S(1)}) custom-call(f32[2,2,192,384]{3,2,1,0:T(8,128)} %bitcast.1), custom_call_target="tpu_custom_call" | custom-call | tf_op jit(solution)/shard_map/pick/pallas_call | solution.py:327
  1.9 1.6 %collective-permute-done.got_ref = f32[2,192,384]{2,1,0:T(8,128)S(1)} collective-permute-done((f32[2,192,384]{2,1,0:T(8,128)S(1)}, f32[2,192,384]{2,1,0:T(8,128)S(1)}, u32[]{:S(2)}, u32[]{:S(2)}) %collective-permute-start) | collective-permute-done | bytes 589856 | tf_op jit(solution)/shard_map/ppermute | solution.py:336
  3.6 0.8 %shard_map.28 = (f32[384,384]{1,0:T(8,128)S(1)}, f32[128,384]{1,0:T(8,128)S(1)}, f32[128,384]{1,0:T(8,128)S(1)}, f32[128,384]{1,0:T(8,128)S(1)}) custom-call(f32[2,192,384]{2,1,0:T(8,128)S(1)} %get-tuple-element.32.mine_ref, f32[2,192,384]{2,1,0:T(8,128)S(1)} %collective-permute-done.got_ref), custom_call_target="tpu_custom_call" | custom-call | tf_op jit(solution)/shard_map/pallas_call | solution.py:115
  4.4 2.4 %shard_map.29 = (f32[384,384]{1,0:T(8,128)S(1)}, f32[384,384]{1,0:T(8,128)S(1)}, f32[384,384]{1,0:T(8,128)S(1)}, f32[2,256,384]{2,1,0:T(8,128)S(1)}, f32[2,96,38...) custom-call(f32[384,384]{1,0:T(8,128)S(1)} %get-tuple-element.34.r_0_, ...), custom_call_target="tpu_custom_call" | custom-call | tf_op jit(solution)/shard_map/pallas_call | solution.py:115
  6.7 0.7 collective-permute-start.10
  7.5 5.4 %collective-permute-start.6 = (f32[128,384]{1,0:T(8,128)S(1)}, f32[128,384]{1,0:T(8,128)S(1)}, u32[]{:S(2)}, u32[]{:S(2)}) collective-permute-start(f32[128,384]{1,0:T(8,128)S(1)} %get-tuple-element.37.r_3_), channel_id=1, source_target_pairs={{0,4},{1,5},{2,6},{3,7},{16,20},{17,21},{18,22},{19,23}} | collective-permute-start | bytes 589832 | tf_op jit(solution)/shard_map/ppermute | solution.py:343
  12.9 1.3 %collective-permute-start.5 = (f32[128,384]{1,0:T(8,128)S(1)}, f32[128,384]{1,0:T(8,128)S(1)}, u32[]{:S(2)}, u32[]{:S(2)}) collective-permute-start(f32[128,384]{1,0:T(8,128)S(1)} %get-tuple-element.36.r_2_), channel_id=1, source_target_pairs={{0,4},{1,5},{2,6},{3,7},{16,20},{17,21},{18,22},{19,23}} | collective-permute-start | bytes 589832 | tf_op jit(solution)/shard_map/ppermute | solution.py:343
  14.2 1.3 %collective-permute-start.1 = (f32[1,96,384]{2,1,0:T(8,128)S(1)}, f32[1,96,384]{2,1,0:T(8,128)S(1)}, u32[]{:S(2)}, u32[]{:S(2)}) collective-permute-start(f32[1,96,384]{2,1,0:T(8,128)S(1)} %get-tuple-element.39), channel_id=1, source_target_pairs={{0,4},{1,5},{2,6},{3,7},{16,20},{17,21},{18,22},{19,23}} | collective-permute-start | bytes 442376 | tf_op jit(solution)/shard_map/ppermute | solution.py:343
  15.5 1.3 %collective-permute-start.4 = (f32[128,384]{1,0:T(8,128)S(1)}, f32[128,384]{1,0:T(8,128)S(1)}, u32[]{:S(2)}, u32[]{:S(2)}) collective-permute-start(f32[128,384]{1,0:T(8,128)S(1)} %get-tuple-element.35.r_1_), channel_id=1, source_target_pairs={{0,4},{1,5},{2,6},{3,7},{16,20},{17,21},{18,22},{19,23}} | collective-permute-start | bytes 589832 | tf_op jit(solution)/shard_map/ppermute | solution.py:343
  16.8 1.3 %collective-permute-done.6.r_5_.r_0_ = f32[128,384]{1,0:T(8,128)S(1)} collective-permute-done((f32[128,384]{1,0:T(8,128)S(1)}, f32[128,384]{1,0:T(8,128)S(1)}, u32[]{:S(2)}, u32[]{:S(2)}) %collective-permute-start.6) | collective-permute-done | bytes 196640 | tf_op jit(solution)/shard_map/ppermute | solution.py:343
  18.1 1.3 %collective-permute-start.2 = (f32[1,96,384]{2,1,0:T(8,128)S(1)}, f32[1,96,384]{2,1,0:T(8,128)S(1)}, u32[]{:S(2)}, u32[]{:S(2)}) collective-permute-start(f32[1,96,384]{2,1,0:T(8,128)S(1)} %get-tuple-element.40), channel_id=1, source_target_pairs={{0,8},{1,9},{2,10},{3,11},{16,24},{17,25},{18,26},{19,27}} | collective-permute-start | bytes 442376 | tf_op jit(solution)/shard_map/ppermute | solution.py:343
  19.4 6.1 %collective-permute-done.1.r_1_ = f32[1,96,384]{2,1,0:T(8,128)S(1)} collective-permute-done((f32[1,96,384]{2,1,0:T(8,128)S(1)}, f32[1,96,384]{2,1,0:T(8,128)S(1)}, u32[]{:S(2)}, u32[]{:S(2)}) %collective-permute-start.1) | collective-permute-done | bytes 147488 | tf_op jit(solution)/shard_map/ppermute | solution.py:343
  26.2 1.3 %collective-permute-start.3 = (f32[1,96,384]{2,1,0:T(8,128)S(1)}, f32[1,96,384]{2,1,0:T(8,128)S(1)}, u32[]{:S(2)}, u32[]{:S(2)}) collective-permute-start(f32[1,96,384]{2,1,0:T(8,128)S(1)} %get-tuple-element.41), channel_id=1, source_target_pairs={{0,12},{1,13},{2,14},{3,15},{16,28},{17,29},{18,30},{19,31}} | collective-permute-start | bytes 442376 | tf_op jit(solution)/shard_map/ppermute | solution.py:343
  27.5 2.2 %collective-permute-done.4.r_3_.r_0_ = f32[128,384]{1,0:T(8,128)S(1)} collective-permute-done((f32[128,384]{1,0:T(8,128)S(1)}, f32[128,384]{1,0:T(8,128)S(1)}, u32[]{:S(2)}, u32[]{:S(2)}) %collective-permute-start.4) | collective-permute-done | bytes 196640 | tf_op jit(solution)/shard_map/ppermute | solution.py:343
  30.4 2.5 %collective-permute-done.2.r_2_ = f32[1,96,384]{2,1,0:T(8,128)S(1)} collective-permute-done((f32[1,96,384]{2,1,0:T(8,128)S(1)}, f32[1,96,384]{2,1,0:T(8,128)S(1)}, u32[]{:S(2)}, u32[]{:S(2)}) %collective-permute-start.2) | collective-permute-done | bytes 147488 | tf_op jit(solution)/shard_map/ppermute | solution.py:343
  32.9 0.7 collective-permute-start.12
  33.6 1.6 %collective-permute-done.3.r_3_ = f32[1,96,384]{2,1,0:T(8,128)S(1)} collective-permute-done((f32[1,96,384]{2,1,0:T(8,128)S(1)}, f32[1,96,384]{2,1,0:T(8,128)S(1)}, u32[]{:S(2)}, u32[]{:S(2)}) %collective-permute-start.3) | collective-permute-done | bytes 147488 | tf_op jit(solution)/shard_map/ppermute | solution.py:343
  35.2 1.3 %collective-permute-start.7 = (f32[2,96,384]{2,1,0:T(8,128)S(1)}, f32[2,96,384]{2,1,0:T(8,128)S(1)}, u32[]{:S(2)}, u32[]{:S(2)}) collective-permute-start(f32[2,96,384]{2,1,0:T(8,128)S(1)} %get-tuple-element.45), channel_id=1, source_target_pairs={{4,0},{5,1},{6,2},{7,3},{20,16},{21,17},{22,18},{23,19}} | collective-permute-start | bytes 884744 | tf_op jit(solution)/shard_map/ppermute | solution.py:343
  36.5 0.7 collective-permute-start.8
  37.3 0.7 collective-permute-start.20
  38.0 0.7 collective-permute-start.19
  38.7 0.7 collective-permute-start.18
  39.6 8.4 %collective-permute-done.7.r_4_ = f32[2,96,384]{2,1,0:T(8,128)S(1)} collective-permute-done((f32[2,96,384]{2,1,0:T(8,128)S(1)}, f32[2,96,384]{2,1,0:T(8,128)S(1)}, u32[]{:S(2)}, u32[]{:S(2)}) %collective-permute-start.7) | collective-permute-done | bytes 294944 | tf_op jit(solution)/shard_map/ppermute | solution.py:343
  48.0 0.7 collective-permute-start.9
  48.7 0.7 collective-permute-start.15
  49.4 1.3 %collective-permute-start.16 = (f32[2,96,384]{2,1,0:T(8,128)S(1)}, f32[2,96,384]{2,1,0:T(8,128)S(1)}, u32[]{:S(2)}, u32[]{:S(2)}) collective-permute-start(f32[2,96,384]{2,1,0:T(8,128)S(1)} %get-tuple-element.54), channel_id=1, source_target_pairs={{8,0},{9,1},{10,2},{11,3},{24,16},{25,17},{26,18},{27,19}} | collective-permute-start | bytes 884744 | tf_op jit(solution)/shard_map/ppermute | solution.py:343
  50.7 0.7 collective-permute-start.17
  51.4 1.3 %collective-permute-start.11 = (f32[2,96,384]{2,1,0:T(8,128)S(1)}, f32[2,96,384]{2,1,0:T(8,128)S(1)}, u32[]{:S(2)}, u32[]{:S(2)}) collective-permute-start(f32[2,96,384]{2,1,0:T(8,128)S(1)} %get-tuple-element.50), channel_id=1, source_target_pairs={{4,0},{5,1},{6,2},{7,3},{20,16},{21,17},{22,18},{23,19}} | collective-permute-start | bytes 884744 | tf_op jit(solution)/shard_map/ppermute | solution.py:343
  52.8 15.2 %collective-permute-done.16.r_12_ = f32[2,96,384]{2,1,0:T(8,128)S(1)} collective-permute-done((f32[2,96,384]{2,1,0:T(8,128)S(1)}, f32[2,96,384]{2,1,0:T(8,128)S(1)}, u32[]{:S(2)}, u32[]{:S(2)}) %collective-permute-start.16) | collective-permute-done | bytes 294944 | tf_op jit(solution)/shard_map/ppermute | solution.py:343
  68.0 1.1 %collective-permute-done.11.r_8_ = f32[2,96,384]{2,1,0:T(8,128)S(1)} collective-permute-done((f32[2,96,384]{2,1,0:T(8,128)S(1)}, f32[2,96,384]{2,1,0:T(8,128)S(1)}, u32[]{:S(2)}, u32[]{:S(2)}) %collective-permute-start.11) | collective-permute-done | bytes 294944 | tf_op jit(solution)/shard_map/ppermute | solution.py:343
  69.5 2.3 %collective-permute-done.21.got_ref = f32[8,96,192]{2,1,0:T(8,128)S(1)} collective-permute-done((f32[8,96,192]{2,1,0:T(8,128)S(1)}, f32[8,96,192]{2,1,0:T(8,128)S(1)}, u32[]{:S(2)}, u32[]{:S(2)}) %collective-permute-start.21) | collective-permute-done | bytes 589856 | tf_op jit(solution)/shard_map/ppermute | solution.py:386
  71.8 2.7 %spectrum.1 = f32[2,2,8,96,192]{4,3,2,1,0:T(8,128)} custom-call(f32[8,96,192]{2,1,0:T(8,128)S(1)} %get-tuple-element.57.keep_ref, f32[8,96,192]{2,1,0:T(8,128)S(1)} %collective-permute-done.21.got_ref), custom_call_target="tpu_custom_call" | custom-call | tf_op jit(solution)/shard_map/spectrum/pallas_call | solution.py:387
  (30 shorter events, 2.6 us)
Async XLA Ops:
  0.0 4.4 %copy-start = (f32[2,384,384]{2,1,0:T(8,128)S(1)}, f32[2,384,384]{2,1,0:T(8,128)}, u32[]{:S(2)}) copy-start(f32[2,384,384]{2,1,0:T(8,128)} %r_4_.1) | copy-start | bytes 3538948
  1.4 2.2 %collective-permute-start = (f32[2,192,384]{2,1,0:T(8,128)S(1)}, f32[2,192,384]{2,1,0:T(8,128)S(1)}, u32[]{:S(2)}, u32[]{:S(2)}) collective-permute-start(f32[2,192,384]{2,1,0:T(8,128)S(1)} %get-tuple-element.33), channel_id=1, source_target_pairs={{0,1},{1,0},{2,3},{3,2},{4,5},{5,4},{6,7},{7,6},{8,9},{9,8},{10,11... | collective-permute-start | bytes 1769480 | tf_op jit(solution)/shard_map/ppermute | solution.py:336
  6.7 31.9 %collective-permute-start.10 = (f32[2,256,384]{2,1,0:T(8,128)S(1)}, f32[2,256,384]{2,1,0:T(8,128)S(1)}, u32[]{:S(2)}, u32[]{:S(2)}) collective-permute-start(f32[2,256,384]{2,1,0:T(8,128)S(1)} %get-tuple-element.49), channel_id=1, source_target_pairs={{8,4},{12,8},{9,5},{13,9},{10,6},{14,10},{11,7},{15,11},{24,20},{2... | collective-permute-start | bytes 2359304 | tf_op jit(solution)/shard_map/ppermute | solution.py:343
  7.5 10.7 %collective-permute-start.6 = (f32[128,384]{1,0:T(8,128)S(1)}, f32[128,384]{1,0:T(8,128)S(1)}, u32[]{:S(2)}, u32[]{:S(2)}) collective-permute-start(f32[128,384]{1,0:T(8,128)S(1)} %get-tuple-element.37.r_3_), channel_id=1, source_target_pairs={{0,4},{1,5},{2,6},{3,7},{16,20},{17,21},{18,22},{19,23}} | collective-permute-start | bytes 589832 | tf_op jit(solution)/shard_map/ppermute | solution.py:343
  12.9 13.3 %collective-permute-start.5 = (f32[128,384]{1,0:T(8,128)S(1)}, f32[128,384]{1,0:T(8,128)S(1)}, u32[]{:S(2)}, u32[]{:S(2)}) collective-permute-start(f32[128,384]{1,0:T(8,128)S(1)} %get-tuple-element.36.r_2_), channel_id=1, source_target_pairs={{0,4},{1,5},{2,6},{3,7},{16,20},{17,21},{18,22},{19,23}} | collective-permute-start | bytes 589832 | tf_op jit(solution)/shard_map/ppermute | solution.py:343
  14.2 11.3 %collective-permute-start.1 = (f32[1,96,384]{2,1,0:T(8,128)S(1)}, f32[1,96,384]{2,1,0:T(8,128)S(1)}, u32[]{:S(2)}, u32[]{:S(2)}) collective-permute-start(f32[1,96,384]{2,1,0:T(8,128)S(1)} %get-tuple-element.39), channel_id=1, source_target_pairs={{0,4},{1,5},{2,6},{3,7},{16,20},{17,21},{18,22},{19,23}} | collective-permute-start | bytes 442376 | tf_op jit(solution)/shard_map/ppermute | solution.py:343
  15.5 14.2 %collective-permute-start.4 = (f32[128,384]{1,0:T(8,128)S(1)}, f32[128,384]{1,0:T(8,128)S(1)}, u32[]{:S(2)}, u32[]{:S(2)}) collective-permute-start(f32[128,384]{1,0:T(8,128)S(1)} %get-tuple-element.35.r_1_), channel_id=1, source_target_pairs={{0,4},{1,5},{2,6},{3,7},{16,20},{17,21},{18,22},{19,23}} | collective-permute-start | bytes 589832 | tf_op jit(solution)/shard_map/ppermute | solution.py:343
  18.1 14.8 %collective-permute-start.2 = (f32[1,96,384]{2,1,0:T(8,128)S(1)}, f32[1,96,384]{2,1,0:T(8,128)S(1)}, u32[]{:S(2)}, u32[]{:S(2)}) collective-permute-start(f32[1,96,384]{2,1,0:T(8,128)S(1)} %get-tuple-element.40), channel_id=1, source_target_pairs={{0,8},{1,9},{2,10},{3,11},{16,24},{17,25},{18,26},{19,27}} | collective-permute-start | bytes 442376 | tf_op jit(solution)/shard_map/ppermute | solution.py:343
  25.5 11.0 %collective-permute-start.14 = (f32[128,384]{1,0:T(8,128)S(1)}, f32[128,384]{1,0:T(8,128)S(1)}, u32[]{:S(2)}, u32[]{:S(2)}) collective-permute-start(f32[128,384]{1,0:T(8,128)S(1)} %shard_map.33.r_3_), channel_id=1, source_target_pairs={{4,8},{5,9},{6,10},{7,11},{20,24},{21,25},{22,26},{23,27}} | collective-permute-start | bytes 589832 | tf_op jit(solution)/shard_map/ppermute | solution.py:343
  26.2 9.1 %collective-permute-start.3 = (f32[1,96,384]{2,1,0:T(8,128)S(1)}, f32[1,96,384]{2,1,0:T(8,128)S(1)}, u32[]{:S(2)}, u32[]{:S(2)}) collective-permute-start(f32[1,96,384]{2,1,0:T(8,128)S(1)} %get-tuple-element.41), channel_id=1, source_target_pairs={{0,12},{1,13},{2,14},{3,15},{16,28},{17,29},{18,30},{19,31}} | collective-permute-start | bytes 442376 | tf_op jit(solution)/shard_map/ppermute | solution.py:343
  29.7 7.5 %collective-permute-start.13 = (f32[128,384]{1,0:T(8,128)S(1)}, f32[128,384]{1,0:T(8,128)S(1)}, u32[]{:S(2)}, u32[]{:S(2)}) collective-permute-start(f32[128,384]{1,0:T(8,128)S(1)} %shard_map.32.r_2_), channel_id=1, source_target_pairs={{4,8},{5,9},{6,10},{7,11},{20,24},{21,25},{22,26},{23,27}} | collective-permute-start | bytes 589832 | tf_op jit(solution)/shard_map/ppermute | solution.py:343
  32.9 5.1 %collective-permute-start.12 = (f32[128,384]{1,0:T(8,128)S(1)}, f32[128,384]{1,0:T(8,128)S(1)}, u32[]{:S(2)}, u32[]{:S(2)}) collective-permute-start(f32[128,384]{1,0:T(8,128)S(1)} %shard_map.31.r_1_), channel_id=1, source_target_pairs={{4,8},{5,9},{6,10},{7,11},{20,24},{21,25},{22,26},{23,27}} | collective-permute-start | bytes 589832 | tf_op jit(solution)/shard_map/ppermute | solution.py:343
  35.2 12.8 %collective-permute-start.7 = (f32[2,96,384]{2,1,0:T(8,128)S(1)}, f32[2,96,384]{2,1,0:T(8,128)S(1)}, u32[]{:S(2)}, u32[]{:S(2)}) collective-permute-start(f32[2,96,384]{2,1,0:T(8,128)S(1)} %get-tuple-element.45), channel_id=1, source_target_pairs={{4,0},{5,1},{6,2},{7,3},{20,16},{21,17},{22,18},{23,19}} | collective-permute-start | bytes 884744 | tf_op jit(solution)/shard_map/ppermute | solution.py:343
  36.5 12.2 %collective-permute-start.8 = (f32[2,96,384]{2,1,0:T(8,128)S(1)}, f32[2,96,384]{2,1,0:T(8,128)S(1)}, u32[]{:S(2)}, u32[]{:S(2)}) collective-permute-start(f32[2,96,384]{2,1,0:T(8,128)S(1)} %get-tuple-element.47), channel_id=1, source_target_pairs={{4,8},{5,9},{6,10},{7,11},{20,24},{21,25},{22,26},{23,27}} | collective-permute-start | bytes 884744 | tf_op jit(solution)/shard_map/ppermute | solution.py:343
  37.3 12.2 %collective-permute-start.20 = (f32[128,384]{1,0:T(8,128)S(1)}, f32[128,384]{1,0:T(8,128)S(1)}, u32[]{:S(2)}, u32[]{:S(2)}) collective-permute-start(f32[128,384]{1,0:T(8,128)S(1)} %shard_map.38.r_3_), channel_id=1, source_target_pairs={{8,12},{9,13},{10,14},{11,15},{24,28},{25,29},{26,30},{27,31}} | collective-permute-start | bytes 589832 | tf_op jit(solution)/shard_map/ppermute | solution.py:343
  38.0 12.8 %collective-permute-start.19 = (f32[128,384]{1,0:T(8,128)S(1)}, f32[128,384]{1,0:T(8,128)S(1)}, u32[]{:S(2)}, u32[]{:S(2)}) collective-permute-start(f32[128,384]{1,0:T(8,128)S(1)} %shard_map.37.r_2_), channel_id=1, source_target_pairs={{8,12},{9,13},{10,14},{11,15},{24,28},{25,29},{26,30},{27,31}} | collective-permute-start | bytes 589832 | tf_op jit(solution)/shard_map/ppermute | solution.py:343
  38.7 12.7 %collective-permute-start.18 = (f32[128,384]{1,0:T(8,128)S(1)}, f32[128,384]{1,0:T(8,128)S(1)}, u32[]{:S(2)}, u32[]{:S(2)}) collective-permute-start(f32[128,384]{1,0:T(8,128)S(1)} %shard_map.36.r_1_), channel_id=1, source_target_pairs={{8,12},{9,13},{10,14},{11,15},{24,28},{25,29},{26,30},{27,31}} | collective-permute-start | bytes 589832 | tf_op jit(solution)/shard_map/ppermute | solution.py:343
  48.0 4.7 %collective-permute-start.9 = (f32[2,96,384]{2,1,0:T(8,128)S(1)}, f32[2,96,384]{2,1,0:T(8,128)S(1)}, u32[]{:S(2)}, u32[]{:S(2)}) collective-permute-start(f32[2,96,384]{2,1,0:T(8,128)S(1)} %get-tuple-element.48), channel_id=1, source_target_pairs={{4,12},{5,13},{6,14},{7,15},{20,28},{21,29},{22,30},{23,31}} | collective-permute-start | bytes 884744 | tf_op jit(solution)/shard_map/ppermute | solution.py:343
  48.7 4.0 %collective-permute-start.15 = (f32[2,96,384]{2,1,0:T(8,128)S(1)}, f32[2,96,384]{2,1,0:T(8,128)S(1)}, u32[]{:S(2)}, u32[]{:S(2)}) collective-permute-start(f32[2,96,384]{2,1,0:T(8,128)S(1)} %get-tuple-element.53), channel_id=1, source_target_pairs={{8,12},{9,13},{10,14},{11,15},{24,28},{25,29},{26,30},{27,31}} | collective-permute-start | bytes 884744 | tf_op jit(solution)/shard_map/ppermute | solution.py:343
  49.4 18.6 %collective-permute-start.16 = (f32[2,96,384]{2,1,0:T(8,128)S(1)}, f32[2,96,384]{2,1,0:T(8,128)S(1)}, u32[]{:S(2)}, u32[]{:S(2)}) collective-permute-start(f32[2,96,384]{2,1,0:T(8,128)S(1)} %get-tuple-element.54), channel_id=1, source_target_pairs={{8,0},{9,1},{10,2},{11,3},{24,16},{25,17},{26,18},{27,19}} | collective-permute-start | bytes 884744 | tf_op jit(solution)/shard_map/ppermute | solution.py:343
  50.7 17.3 %collective-permute-start.17 = (f32[2,96,384]{2,1,0:T(8,128)S(1)}, f32[2,96,384]{2,1,0:T(8,128)S(1)}, u32[]{:S(2)}, u32[]{:S(2)}) collective-permute-start(f32[2,96,384]{2,1,0:T(8,128)S(1)} %get-tuple-element.55), channel_id=1, source_target_pairs={{8,4},{9,5},{10,6},{11,7},{24,20},{25,21},{26,22},{27,23}} | collective-permute-start | bytes 884744 | tf_op jit(solution)/shard_map/ppermute | solution.py:343
  51.4 17.7 %collective-permute-start.11 = (f32[2,96,384]{2,1,0:T(8,128)S(1)}, f32[2,96,384]{2,1,0:T(8,128)S(1)}, u32[]{:S(2)}, u32[]{:S(2)}) collective-permute-start(f32[2,96,384]{2,1,0:T(8,128)S(1)} %get-tuple-element.50), channel_id=1, source_target_pairs={{4,0},{5,1},{6,2},{7,3},{20,16},{21,17},{22,18},{23,19}} | collective-permute-start | bytes 884744 | tf_op jit(solution)/shard_map/ppermute | solution.py:343
  69.4 2.4 %collective-permute-start.21 = (f32[8,96,192]{2,1,0:T(8,128)S(1)}, f32[8,96,192]{2,1,0:T(8,128)S(1)}, u32[]{:S(2)}, u32[]{:S(2)}) collective-permute-start(f32[8,96,192]{2,1,0:T(8,128)S(1)} %get-tuple-element.58), channel_id=1, source_target_pairs={{0,1},{1,0},{2,3},{3,2},{4,5},{5,4},{6,7},{7,6},{8,9},{9,8},{10,11... | collective-permute-start | bytes 1769480 | tf_op jit(solution)/shard_map/ppermute | solution.py:386
where the time goes:
time: 75 us; the launch traced here: 74.5 us
  waiting for transfers between devices  42.4 us (57%)
  starting transfers between devices  23.8 us (32%)
  Pallas kernels  7.89 us (11%)
    ppermute x20, waiting for transfers between devices, along(): return lax.ppermute(x, 'tm', [hop] if isinstance(hop, tuple) else hop)  38.5 us
    ppermute x20, starting transfers between devices, along(): return lax.ppermute(x, 'tm', [hop] if isinstance(hop, tuple) else hop)  23.2 us
    pallas_call x14, Pallas kernels, local_call(): pl.pallas_call(kernel, out_shape=[pltpu.VMEM(s, jnp.float32) for s in out...  3.82 us
    pallas_call x1, Pallas kernels, paired_body(): pl.pallas_call(spectrum_kernel, out_shape=jax.ShapeDtypeStruct((kdev, 2,...  2.72 us
    ppermute x1, waiting for transfers between devices, paired_body(): taken = lax.ppermute(give, 'col', swap)  2.27 us
    ppermute x1, waiting for transfers between devices, paired_body(): got = lax.ppermute(other, 'col', swap)  1.63 us
  transfers between devices with their start and end apart: 22, of which 10 were waited for; matrix products, arithmetic and copies ran while one was open for 0% of the time, Pallas kernels for 0%

commit v1 on v0

--- a/solution.py
+++ b/solution.py
@@ -122,16 +122,11 @@
     )(*near)
 
 
-def pick_kernel(in_ref, mine_ref, other_ref, sems):
+def pick_kernel(own, in_ref, out_ref, sem):
     core = lax.axis_index("col")
-    copies = [
-        pltpu.make_async_copy(in_ref.at[1 - core], other_ref, sems.at[0]),
-        pltpu.make_async_copy(in_ref.at[core], mine_ref, sems.at[1]),
-    ]
-    for copy in copies:
-        copy.start()
-    for copy in copies:
-        copy.wait()
+    copy = pltpu.make_async_copy(in_ref.at[core if own else 1 - core], out_ref, sem)
+    copy.start()
+    copy.wait()
 
 
 def start_kernel(mine_ref, got_ref, a0_ref, *refs):
@@ -324,16 +319,18 @@
     swap = [(0, 1), (1, 0)]
     scratch = [pltpu.VMEM(square, jnp.float32), pltpu.VMEM((order, 3 * order), jnp.bfloat16)]
 
-    mine, other = pl.pallas_call(
-        pick_kernel,
-        out_shape=[pltpu.VMEM((slices, part, order), jnp.float32)] * 2,
-        in_specs=[pl.BlockSpec(memory_space=pltpu.HBM)],
-        out_specs=[VMEM] * 2,
-        scratch_shapes=[pltpu.SemaphoreType.DMA((2,))],
-        compiler_params=GRANT,
-        name="pick",
-    )(pltpu.with_memory_space_constraint(flipped, pltpu.HBM))
-    got = lax.ppermute(other, "col", swap)
+    def pick(own):
+        return pl.pallas_call(
+            lambda *r: pick_kernel(own, *r),
+            out_shape=pltpu.VMEM((slices, part, order), jnp.float32),
+            in_specs=[pl.BlockSpec(memory_space=pltpu.HBM)],
+            out_specs=VMEM,
+            scratch_shapes=[pltpu.SemaphoreType.DMA],
+            compiler_params=GRANT,
+        )(pltpu.with_memory_space_constraint(flipped, pltpu.HBM))
+
+    got = lax.ppermute(pick(False), "col", swap)
+    mine = pick(True)
     a0, *prod = local_call(
         start_kernel, [square] + [chunk] * CHUNKS, (mine, got),
         scratch=[pltpu.VMEM(square, jnp.float32)],

time: 75 us -> 74.8 us (level)
  waiting for transfers between devices: 42.4 us -> 41.3 us
  Pallas kernels: 7.89 us -> 8.68 us
    ppermute x1, waiting for transfers between devices: 1.63 us -> 0.55 us  [paired_body(): got = lax.ppermute(pick(False), 'col', swap)]
    pallas_call x1 -> x2, Pallas kernels: 1.35 us -> 2.14 us  [pick(): pl.pallas_call(lambda *r: pick_kernel(own, *r), out_shape=pltpu.VMEM((sli...]
  transfers between devices with their start and end apart: 22 -> 22, of which waited for: 10 -> 10; matrix products, arithmetic and copies ran while one was open for 0% -> 0% of each run, Pallas kernels for 0% -> 2%
where the time goes in v1:
time: 74.8 us; the launch traced here: 74.2 us
  waiting for transfers between devices  41.3 us (55%)
  starting transfers between devices  23.8 us (32%)
  Pallas kernels  8.68 us (12%)
    ppermute x20, waiting for transfers between devices, along(): return lax.ppermute(x, 'tm', [hop] if isinstance(hop, tuple) else hop)  38.5 us
    ppermute x20, starting transfers between devices, along(): return lax.ppermute(x, 'tm', [hop] if isinstance(hop, tuple) else hop)  23.2 us
    pallas_call x14, Pallas kernels, local_call(): pl.pallas_call(kernel, out_shape=[pltpu.VMEM(s, jnp.float32) for s in out...  3.82 us
    pallas_call x1, Pallas kernels, paired_body(): pl.pallas_call(spectrum_kernel, out_shape=jax.ShapeDtypeStruct((kdev, 2,...  2.72 us
    ppermute x1, waiting for transfers between devices, paired_body(): taken = lax.ppermute(give, 'col', swap)  2.27 us
    pallas_call x2, Pallas kernels, pick(): pl.pallas_call(lambda *r: pick_kernel(own, *r), out_shape=pltpu.VMEM((sli...  2.14 us
  transfers between devices with their start and end apart: 22, of which 10 were waited for; matrix products, arithmetic and copies ran while one was open for 0% of the time, Pallas kernels for 2%

profile of v1, /device:TPU:0, one launch (start us, length us, event | category | flops | bytes accessed | tf_op | source)
XLA Modules:
  0.0 74.2 jit_solution(17266343771967531467)
XLA Ops:
  0.0 1.1 %shard_map.29 = f32[2,192,384]{2,1,0:T(8,128)S(1)} custom-call(f32[2,2,192,384]{3,2,1,0:T(8,128)} %bitcast.1), custom_call_target="tpu_custom_call" | custom-call | tf_op jit(solution)/shard_map/pallas_call | solution.py:323
  1.7 1.1 %shard_map.28.mine_ref = f32[2,192,384]{2,1,0:T(8,128)S(1)} custom-call(f32[2,2,192,384]{3,2,1,0:T(8,128)} %bitcast.2), custom_call_target="tpu_custom_call" | custom-call | tf_op jit(solution)/shard_map/pallas_call | solution.py:323
  3.3 0.8 %shard_map.30 = (f32[384,384]{1,0:T(8,128)S(1)}, f32[128,384]{1,0:T(8,128)S(1)}, f32[128,384]{1,0:T(8,128)S(1)}, f32[128,384]{1,0:T(8,128)S(1)}) custom-call(f32[2,192,384]{2,1,0:T(8,128)S(1)} %shard_map.28.mine_ref, f32[2,192,384]{2,1,0:T(8,128)S(1)} %collective-permute-done.got_ref), custom_call_target="tpu_custom_call" | custom-call | tf_op jit(solution)/shard_map/pallas_call | solution.py:115
  4.1 2.4 %shard_map.31 = (f32[384,384]{1,0:T(8,128)S(1)}, f32[384,384]{1,0:T(8,128)S(1)}, f32[384,384]{1,0:T(8,128)S(1)}, f32[2,256,384]{2,1,0:T(8,128)S(1)}, f32[2,96,38...) custom-call(f32[384,384]{1,0:T(8,128)S(1)} %get-tuple-element.30.r_0_, ...), custom_call_target="tpu_custom_call" | custom-call | tf_op jit(solution)/shard_map/pallas_call | solution.py:115
  6.5 0.7 collective-permute-start.10
  7.2 5.4 %collective-permute-start.6 = (f32[128,384]{1,0:T(8,128)S(1)}, f32[128,384]{1,0:T(8,128)S(1)}, u32[]{:S(2)}, u32[]{:S(2)}) collective-permute-start(f32[128,384]{1,0:T(8,128)S(1)} %get-tuple-element.33.r_3_), channel_id=1, source_target_pairs={{0,4},{1,5},{2,6},{3,7},{16,20},{17,21},{18,22},{19,23}} | collective-permute-start | bytes 589832 | tf_op jit(solution)/shard_map/ppermute | solution.py:340
  12.6 1.3 %collective-permute-start.5 = (f32[128,384]{1,0:T(8,128)S(1)}, f32[128,384]{1,0:T(8,128)S(1)}, u32[]{:S(2)}, u32[]{:S(2)}) collective-permute-start(f32[128,384]{1,0:T(8,128)S(1)} %get-tuple-element.32.r_2_), channel_id=1, source_target_pairs={{0,4},{1,5},{2,6},{3,7},{16,20},{17,21},{18,22},{19,23}} | collective-permute-start | bytes 589832 | tf_op jit(solution)/shard_map/ppermute | solution.py:340
  13.9 1.3 %collective-permute-start.1 = (f32[1,96,384]{2,1,0:T(8,128)S(1)}, f32[1,96,384]{2,1,0:T(8,128)S(1)}, u32[]{:S(2)}, u32[]{:S(2)}) collective-permute-start(f32[1,96,384]{2,1,0:T(8,128)S(1)} %get-tuple-element.35), channel_id=1, source_target_pairs={{0,4},{1,5},{2,6},{3,7},{16,20},{17,21},{18,22},{19,23}} | collective-permute-start | bytes 442376 | tf_op jit(solution)/shard_map/ppermute | solution.py:340
  15.2 1.3 %collective-permute-start.4 = (f32[128,384]{1,0:T(8,128)S(1)}, f32[128,384]{1,0:T(8,128)S(1)}, u32[]{:S(2)}, u32[]{:S(2)}) collective-permute-start(f32[128,384]{1,0:T(8,128)S(1)} %get-tuple-element.31.r_1_), channel_id=1, source_target_pairs={{0,4},{1,5},{2,6},{3,7},{16,20},{17,21},{18,22},{19,23}} | collective-permute-start | bytes 589832 | tf_op jit(solution)/shard_map/ppermute | solution.py:340
  16.5 1.3 %collective-permute-done.6.r_5_.r_0_ = f32[128,384]{1,0:T(8,128)S(1)} collective-permute-done((f32[128,384]{1,0:T(8,128)S(1)}, f32[128,384]{1,0:T(8,128)S(1)}, u32[]{:S(2)}, u32[]{:S(2)}) %collective-permute-start.6) | collective-permute-done | bytes 196640 | tf_op jit(solution)/shard_map/ppermute | solution.py:340
  17.8 1.3 %collective-permute-start.2 = (f32[1,96,384]{2,1,0:T(8,128)S(1)}, f32[1,96,384]{2,1,0:T(8,128)S(1)}, u32[]{:S(2)}, u32[]{:S(2)}) collective-permute-start(f32[1,96,384]{2,1,0:T(8,128)S(1)} %get-tuple-element.36), channel_id=1, source_target_pairs={{0,8},{1,9},{2,10},{3,11},{16,24},{17,25},{18,26},{19,27}} | collective-permute-start | bytes 442376 | tf_op jit(solution)/shard_map/ppermute | solution.py:340
  19.2 6.1 %collective-permute-done.1.r_1_ = f32[1,96,384]{2,1,0:T(8,128)S(1)} collective-permute-done((f32[1,96,384]{2,1,0:T(8,128)S(1)}, f32[1,96,384]{2,1,0:T(8,128)S(1)}, u32[]{:S(2)}, u32[]{:S(2)}) %collective-permute-start.1) | collective-permute-done | bytes 147488 | tf_op jit(solution)/shard_map/ppermute | solution.py:340
  25.2 0.7 collective-permute-start.14
  25.9 1.3 %collective-permute-start.3 = (f32[1,96,384]{2,1,0:T(8,128)S(1)}, f32[1,96,384]{2,1,0:T(8,128)S(1)}, u32[]{:S(2)}, u32[]{:S(2)}) collective-permute-start(f32[1,96,384]{2,1,0:T(8,128)S(1)} %get-tuple-element.37), channel_id=1, source_target_pairs={{0,12},{1,13},{2,14},{3,15},{16,28},{17,29},{18,30},{19,31}} | collective-permute-start | bytes 442376 | tf_op jit(solution)/shard_map/ppermute | solution.py:340
  27.2 2.2 %collective-permute-done.4.r_3_.r_0_ = f32[128,384]{1,0:T(8,128)S(1)} collective-permute-done((f32[128,384]{1,0:T(8,128)S(1)}, f32[128,384]{1,0:T(8,128)S(1)}, u32[]{:S(2)}, u32[]{:S(2)}) %collective-permute-start.4) | collective-permute-done | bytes 196640 | tf_op jit(solution)/shard_map/ppermute | solution.py:340
  30.1 2.5 %collective-permute-done.2.r_2_ = f32[1,96,384]{2,1,0:T(8,128)S(1)} collective-permute-done((f32[1,96,384]{2,1,0:T(8,128)S(1)}, f32[1,96,384]{2,1,0:T(8,128)S(1)}, u32[]{:S(2)}, u32[]{:S(2)}) %collective-permute-start.2) | collective-permute-done | bytes 147488 | tf_op jit(solution)/shard_map/ppermute | solution.py:340
  33.3 1.6 %collective-permute-done.3.r_3_ = f32[1,96,384]{2,1,0:T(8,128)S(1)} collective-permute-done((f32[1,96,384]{2,1,0:T(8,128)S(1)}, f32[1,96,384]{2,1,0:T(8,128)S(1)}, u32[]{:S(2)}, u32[]{:S(2)}) %collective-permute-start.3) | collective-permute-done | bytes 147488 | tf_op jit(solution)/shard_map/ppermute | solution.py:340
  35.0 1.3 %collective-permute-start.7 = (f32[2,96,384]{2,1,0:T(8,128)S(1)}, f32[2,96,384]{2,1,0:T(8,128)S(1)}, u32[]{:S(2)}, u32[]{:S(2)}) collective-permute-start(f32[2,96,384]{2,1,0:T(8,128)S(1)} %get-tuple-element.41), channel_id=1, source_target_pairs={{4,0},{5,1},{6,2},{7,3},{20,16},{21,17},{22,18},{23,19}} | collective-permute-start | bytes 884744 | tf_op jit(solution)/shard_map/ppermute | solution.py:340
  36.3 0.7 collective-permute-start.8
  37.0 0.7 collective-permute-start.20
  37.7 0.7 collective-permute-start.19
  38.4 0.7 collective-permute-start.18
  39.4 8.4 %collective-permute-done.7.r_4_ = f32[2,96,384]{2,1,0:T(8,128)S(1)} collective-permute-done((f32[2,96,384]{2,1,0:T(8,128)S(1)}, f32[2,96,384]{2,1,0:T(8,128)S(1)}, u32[]{:S(2)}, u32[]{:S(2)}) %collective-permute-start.7) | collective-permute-done | bytes 294944 | tf_op jit(solution)/shard_map/ppermute | solution.py:340
  47.8 0.7 collective-permute-start.9
  48.5 0.7 collective-permute-start.15
  49.2 1.3 %collective-permute-start.16 = (f32[2,96,384]{2,1,0:T(8,128)S(1)}, f32[2,96,384]{2,1,0:T(8,128)S(1)}, u32[]{:S(2)}, u32[]{:S(2)}) collective-permute-start(f32[2,96,384]{2,1,0:T(8,128)S(1)} %get-tuple-element.50), channel_id=1, source_target_pairs={{8,0},{9,1},{10,2},{11,3},{24,16},{25,17},{26,18},{27,19}} | collective-permute-start | bytes 884744 | tf_op jit(solution)/shard_map/ppermute | solution.py:340
  50.5 0.7 collective-permute-start.17
  51.2 1.3 %collective-permute-start.11 = (f32[2,96,384]{2,1,0:T(8,128)S(1)}, f32[2,96,384]{2,1,0:T(8,128)S(1)}, u32[]{:S(2)}, u32[]{:S(2)}) collective-permute-start(f32[2,96,384]{2,1,0:T(8,128)S(1)} %get-tuple-element.46), channel_id=1, source_target_pairs={{4,0},{5,1},{6,2},{7,3},{20,16},{21,17},{22,18},{23,19}} | collective-permute-start | bytes 884744 | tf_op jit(solution)/shard_map/ppermute | solution.py:340
  52.5 15.2 %collective-permute-done.16.r_12_ = f32[2,96,384]{2,1,0:T(8,128)S(1)} collective-permute-done((f32[2,96,384]{2,1,0:T(8,128)S(1)}, f32[2,96,384]{2,1,0:T(8,128)S(1)}, u32[]{:S(2)}, u32[]{:S(2)}) %collective-permute-start.16) | collective-permute-done | bytes 294944 | tf_op jit(solution)/shard_map/ppermute | solution.py:340
  67.7 1.1 %collective-permute-done.11.r_8_ = f32[2,96,384]{2,1,0:T(8,128)S(1)} collective-permute-done((f32[2,96,384]{2,1,0:T(8,128)S(1)}, f32[2,96,384]{2,1,0:T(8,128)S(1)}, u32[]{:S(2)}, u32[]{:S(2)}) %collective-permute-start.11) | collective-permute-done | bytes 294944 | tf_op jit(solution)/shard_map/ppermute | solution.py:340
  69.2 2.3 %collective-permute-done.21.got_ref = f32[8,96,192]{2,1,0:T(8,128)S(1)} collective-permute-done((f32[8,96,192]{2,1,0:T(8,128)S(1)}, f32[8,96,192]{2,1,0:T(8,128)S(1)}, u32[]{:S(2)}, u32[]{:S(2)}) %collective-permute-start.21) | collective-permute-done | bytes 589856 | tf_op jit(solution)/shard_map/ppermute | solution.py:383
  71.5 2.7 %spectrum.1 = f32[2,2,8,96,192]{4,3,2,1,0:T(8,128)} custom-call(f32[8,96,192]{2,1,0:T(8,128)S(1)} %get-tuple-element.53.keep_ref, f32[8,96,192]{2,1,0:T(8,128)S(1)} %collective-permute-done.21.got_ref), custom_call_target="tpu_custom_call" | custom-call | tf_op jit(solution)/shard_map/spectrum/pallas_call | solution.py:384
  (31 shorter events, 3.2 us)
Async XLA Ops:
  1.1 3.0 %copy-start = (f32[2,384,384]{2,1,0:T(8,128)S(1)}, f32[2,384,384]{2,1,0:T(8,128)}, u32[]{:S(2)}) copy-start(f32[2,384,384]{2,1,0:T(8,128)} %r_4_.1) | copy-start | bytes 3538948
  1.1 2.2 %collective-permute-start = (f32[2,192,384]{2,1,0:T(8,128)S(1)}, f32[2,192,384]{2,1,0:T(8,128)S(1)}, u32[]{:S(2)}, u32[]{:S(2)}) collective-permute-start(f32[2,192,384]{2,1,0:T(8,128)S(1)} %shard_map.29), channel_id=1, source_target_pairs={{0,1},{1,0},{2,3},{3,2},{4,5},{5,4},{6,7},{7,6},{8,9},{9,8},{10,11... | collective-permute-start | bytes 1769480 | tf_op jit(solution)/shard_map/ppermute | solution.py:332
  6.5 31.9 %collective-permute-start.10 = (f32[2,256,384]{2,1,0:T(8,128)S(1)}, f32[2,256,384]{2,1,0:T(8,128)S(1)}, u32[]{:S(2)}, u32[]{:S(2)}) collective-permute-start(f32[2,256,384]{2,1,0:T(8,128)S(1)} %get-tuple-element.45), channel_id=1, source_target_pairs={{8,4},{12,8},{9,5},{13,9},{10,6},{14,10},{11,7},{15,11},{24,20},{2... | collective-permute-start | bytes 2359304 | tf_op jit(solution)/shard_map/ppermute | solution.py:340
  7.2 10.7 %collective-permute-start.6 = (f32[128,384]{1,0:T(8,128)S(1)}, f32[128,384]{1,0:T(8,128)S(1)}, u32[]{:S(2)}, u32[]{:S(2)}) collective-permute-start(f32[128,384]{1,0:T(8,128)S(1)} %get-tuple-element.33.r_3_), channel_id=1, source_target_pairs={{0,4},{1,5},{2,6},{3,7},{16,20},{17,21},{18,22},{19,23}} | collective-permute-start | bytes 589832 | tf_op jit(solution)/shard_map/ppermute | solution.py:340
  12.6 13.3 %collective-permute-start.5 = (f32[128,384]{1,0:T(8,128)S(1)}, f32[128,384]{1,0:T(8,128)S(1)}, u32[]{:S(2)}, u32[]{:S(2)}) collective-permute-start(f32[128,384]{1,0:T(8,128)S(1)} %get-tuple-element.32.r_2_), channel_id=1, source_target_pairs={{0,4},{1,5},{2,6},{3,7},{16,20},{17,21},{18,22},{19,23}} | collective-permute-start | bytes 589832 | tf_op jit(solution)/shard_map/ppermute | solution.py:340
  13.9 11.3 %collective-permute-start.1 = (f32[1,96,384]{2,1,0:T(8,128)S(1)}, f32[1,96,384]{2,1,0:T(8,128)S(1)}, u32[]{:S(2)}, u32[]{:S(2)}) collective-permute-start(f32[1,96,384]{2,1,0:T(8,128)S(1)} %get-tuple-element.35), channel_id=1, source_target_pairs={{0,4},{1,5},{2,6},{3,7},{16,20},{17,21},{18,22},{19,23}} | collective-permute-start | bytes 442376 | tf_op jit(solution)/shard_map/ppermute | solution.py:340
  15.2 14.2 %collective-permute-start.4 = (f32[128,384]{1,0:T(8,128)S(1)}, f32[128,384]{1,0:T(8,128)S(1)}, u32[]{:S(2)}, u32[]{:S(2)}) collective-permute-start(f32[128,384]{1,0:T(8,128)S(1)} %get-tuple-element.31.r_1_), channel_id=1, source_target_pairs={{0,4},{1,5},{2,6},{3,7},{16,20},{17,21},{18,22},{19,23}} | collective-permute-start | bytes 589832 | tf_op jit(solution)/shard_map/ppermute | solution.py:340
  17.8 14.8 %collective-permute-start.2 = (f32[1,96,384]{2,1,0:T(8,128)S(1)}, f32[1,96,384]{2,1,0:T(8,128)S(1)}, u32[]{:S(2)}, u32[]{:S(2)}) collective-permute-start(f32[1,96,384]{2,1,0:T(8,128)S(1)} %get-tuple-element.36), channel_id=1, source_target_pairs={{0,8},{1,9},{2,10},{3,11},{16,24},{17,25},{18,26},{19,27}} | collective-permute-start | bytes 442376 | tf_op jit(solution)/shard_map/ppermute | solution.py:340
  25.2 11.0 %collective-permute-start.14 = (f32[128,384]{1,0:T(8,128)S(1)}, f32[128,384]{1,0:T(8,128)S(1)}, u32[]{:S(2)}, u32[]{:S(2)}) collective-permute-start(f32[128,384]{1,0:T(8,128)S(1)} %shard_map.35.r_3_), channel_id=1, source_target_pairs={{4,8},{5,9},{6,10},{7,11},{20,24},{21,25},{22,26},{23,27}} | collective-permute-start | bytes 589832 | tf_op jit(solution)/shard_map/ppermute | solution.py:340
  25.9 9.1 %collective-permute-start.3 = (f32[1,96,384]{2,1,0:T(8,128)S(1)}, f32[1,96,384]{2,1,0:T(8,128)S(1)}, u32[]{:S(2)}, u32[]{:S(2)}) collective-permute-start(f32[1,96,384]{2,1,0:T(8,128)S(1)} %get-tuple-element.37), channel_id=1, source_target_pairs={{0,12},{1,13},{2,14},{3,15},{16,28},{17,29},{18,30},{19,31}} | collective-permute-start | bytes 442376 | tf_op jit(solution)/shard_map/ppermute | solution.py:340
  29.4 7.5 %collective-permute-start.13 = (f32[128,384]{1,0:T(8,128)S(1)}, f32[128,384]{1,0:T(8,128)S(1)}, u32[]{:S(2)}, u32[]{:S(2)}) collective-permute-start(f32[128,384]{1,0:T(8,128)S(1)} %shard_map.34.r_2_), channel_id=1, source_target_pairs={{4,8},{5,9},{6,10},{7,11},{20,24},{21,25},{22,26},{23,27}} | collective-permute-start | bytes 589832 | tf_op jit(solution)/shard_map/ppermute | solution.py:340
  32.6 5.1 %collective-permute-start.12 = (f32[128,384]{1,0:T(8,128)S(1)}, f32[128,384]{1,0:T(8,128)S(1)}, u32[]{:S(2)}, u32[]{:S(2)}) collective-permute-start(f32[128,384]{1,0:T(8,128)S(1)} %shard_map.33.r_1_), channel_id=1, source_target_pairs={{4,8},{5,9},{6,10},{7,11},{20,24},{21,25},{22,26},{23,27}} | collective-permute-start | bytes 589832 | tf_op jit(solution)/shard_map/ppermute | solution.py:340
  35.0 12.8 %collective-permute-start.7 = (f32[2,96,384]{2,1,0:T(8,128)S(1)}, f32[2,96,384]{2,1,0:T(8,128)S(1)}, u32[]{:S(2)}, u32[]{:S(2)}) collective-permute-start(f32[2,96,384]{2,1,0:T(8,128)S(1)} %get-tuple-element.41), channel_id=1, source_target_pairs={{4,0},{5,1},{6,2},{7,3},{20,16},{21,17},{22,18},{23,19}} | collective-permute-start | bytes 884744 | tf_op jit(solution)/shard_map/ppermute | solution.py:340
  36.3 12.2 %collective-permute-start.8 = (f32[2,96,384]{2,1,0:T(8,128)S(1)}, f32[2,96,384]{2,1,0:T(8,128)S(1)}, u32[]{:S(2)}, u32[]{:S(2)}) collective-permute-start(f32[2,96,384]{2,1,0:T(8,128)S(1)} %get-tuple-element.43), channel_id=1, source_target_pairs={{4,8},{5,9},{6,10},{7,11},{20,24},{21,25},{22,26},{23,27}} | collective-permute-start | bytes 884744 | tf_op jit(solution)/shard_map/ppermute | solution.py:340
  37.0 12.2 %collective-permute-start.20 = (f32[128,384]{1,0:T(8,128)S(1)}, f32[128,384]{1,0:T(8,128)S(1)}, u32[]{:S(2)}, u32[]{:S(2)}) collective-permute-start(f32[128,384]{1,0:T(8,128)S(1)} %shard_map.40.r_3_), channel_id=1, source_target_pairs={{8,12},{9,13},{10,14},{11,15},{24,28},{25,29},{26,30},{27,31}} | collective-permute-start | bytes 589832 | tf_op jit(solution)/shard_map/ppermute | solution.py:340
  37.7 12.8 %collective-permute-start.19 = (f32[128,384]{1,0:T(8,128)S(1)}, f32[128,384]{1,0:T(8,128)S(1)}, u32[]{:S(2)}, u32[]{:S(2)}) collective-permute-start(f32[128,384]{1,0:T(8,128)S(1)} %shard_map.39.r_2_), channel_id=1, source_target_pairs={{8,12},{9,13},{10,14},{11,15},{24,28},{25,29},{26,30},{27,31}} | collective-permute-start | bytes 589832 | tf_op jit(solution)/shard_map/ppermute | solution.py:340
  38.4 12.7 %collective-permute-start.18 = (f32[128,384]{1,0:T(8,128)S(1)}, f32[128,384]{1,0:T(8,128)S(1)}, u32[]{:S(2)}, u32[]{:S(2)}) collective-permute-start(f32[128,384]{1,0:T(8,128)S(1)} %shard_map.38.r_1_), channel_id=1, source_target_pairs={{8,12},{9,13},{10,14},{11,15},{24,28},{25,29},{26,30},{27,31}} | collective-permute-start | bytes 589832 | tf_op jit(solution)/shard_map/ppermute | solution.py:340
  47.8 4.7 %collective-permute-start.9 = (f32[2,96,384]{2,1,0:T(8,128)S(1)}, f32[2,96,384]{2,1,0:T(8,128)S(1)}, u32[]{:S(2)}, u32[]{:S(2)}) collective-permute-start(f32[2,96,384]{2,1,0:T(8,128)S(1)} %get-tuple-element.44), channel_id=1, source_target_pairs={{4,12},{5,13},{6,14},{7,15},{20,28},{21,29},{22,30},{23,31}} | collective-permute-start | bytes 884744 | tf_op jit(solution)/shard_map/ppermute | solution.py:340
  48.5 4.0 %collective-permute-start.15 = (f32[2,96,384]{2,1,0:T(8,128)S(1)}, f32[2,96,384]{2,1,0:T(8,128)S(1)}, u32[]{:S(2)}, u32[]{:S(2)}) collective-permute-start(f32[2,96,384]{2,1,0:T(8,128)S(1)} %get-tuple-element.49), channel_id=1, source_target_pairs={{8,12},{9,13},{10,14},{11,15},{24,28},{25,29},{26,30},{27,31}} | collective-permute-start | bytes 884744 | tf_op jit(solution)/shard_map/ppermute | solution.py:340
  49.2 18.6 %collective-permute-start.16 = (f32[2,96,384]{2,1,0:T(8,128)S(1)}, f32[2,96,384]{2,1,0:T(8,128)S(1)}, u32[]{:S(2)}, u32[]{:S(2)}) collective-permute-start(f32[2,96,384]{2,1,0:T(8,128)S(1)} %get-tuple-element.50), channel_id=1, source_target_pairs={{8,0},{9,1},{10,2},{11,3},{24,16},{25,17},{26,18},{27,19}} | collective-permute-start | bytes 884744 | tf_op jit(solution)/shard_map/ppermute | solution.py:340
  50.5 17.3 %collective-permute-start.17 = (f32[2,96,384]{2,1,0:T(8,128)S(1)}, f32[2,96,384]{2,1,0:T(8,128)S(1)}, u32[]{:S(2)}, u32[]{:S(2)}) collective-permute-start(f32[2,96,384]{2,1,0:T(8,128)S(1)} %get-tuple-element.51), channel_id=1, source_target_pairs={{8,4},{9,5},{10,6},{11,7},{24,20},{25,21},{26,22},{27,23}} | collective-permute-start | bytes 884744 | tf_op jit(solution)/shard_map/ppermute | solution.py:340
  51.2 17.7 %collective-permute-start.11 = (f32[2,96,384]{2,1,0:T(8,128)S(1)}, f32[2,96,384]{2,1,0:T(8,128)S(1)}, u32[]{:S(2)}, u32[]{:S(2)}) collective-permute-start(f32[2,96,384]{2,1,0:T(8,128)S(1)} %get-tuple-element.46), channel_id=1, source_target_pairs={{4,0},{5,1},{6,2},{7,3},{20,16},{21,17},{22,18},{23,19}} | collective-permute-start | bytes 884744 | tf_op jit(solution)/shard_map/ppermute | solution.py:340
  69.1 2.4 %collective-permute-start.21 = (f32[8,96,192]{2,1,0:T(8,128)S(1)}, f32[8,96,192]{2,1,0:T(8,128)S(1)}, u32[]{:S(2)}, u32[]{:S(2)}) collective-permute-start(f32[8,96,192]{2,1,0:T(8,128)S(1)} %get-tuple-element.54), channel_id=1, source_target_pairs={{0,1},{1,0},{2,3},{3,2},{4,5},{5,4},{6,7},{7,6},{8,9},{9,8},{10,11... | collective-permute-start | bytes 1769480 | tf_op jit(solution)/shard_map/ppermute | solution.py:383

commit v2 on v1

--- a/solution.py
+++ b/solution.py
@@ -256,28 +256,34 @@
     return [0] * (place == 1) + list(range(place, count))
 
 
-def gather_kernel(plan, *refs):
+def gather_kernel(chosen, *refs):
     ins, (keep_ref, send_ref) = refs[:-2], refs[-2:]
     core = lax.axis_index("col")
     width = keep_ref.shape[2]
-    for to, entries in enumerate(plan):
+    for to, entries in enumerate(chosen):
         @pl.when(lax.axis_index("tm") == to)
         def _(entries=entries):
             for c in range(2):
                 @pl.when(core == c)
                 def _(c=c):
-                    for source, slices in entries:
-                        for i, t in enumerate(slices):
-                            block = ins[source][i]
-                            keep_ref[t] = block[:, c * width:(c + 1) * width]
-                            send_ref[t] = block[:, (1 - c) * width:(2 - c) * width]
-
-
-def spectrum_kernel(keep_ref, got_ref, out_ref):
-    core = lax.axis_index("col")
-    length, rows, _ = keep_ref.shape
+                    for slot, (_, source, i) in enumerate(entries):
+                        block = ins[source][i]
+                        keep_ref[slot] = block[:, c * width:(c + 1) * width]
+                        send_ref[slot] = block[:, (1 - c) * width:(2 - c) * width]
+
+
+def spectrum_kernel(own, tables, *refs):
+    parts, (out_ref, all_ref, done_ref, sems) = refs[:2], refs[-4:]
+    place, core = lax.axis_index("tm"), lax.axis_index("col")
+    length, rows, _ = all_ref.shape
+    for part, table in zip(parts, tables):
+        for slot in range(part.shape[0]):
+            t = sum(jnp.where(place == to, ts[slot], 0) for to, ts in enumerate(table))
+            all_ref[t] = part[slot]
     scale = 1.0 / math.sqrt(length)
     step = 8
+    groups = 3 if rows % (3 * step) == 0 else 1
+    size = rows // groups
 
     def cosine(n):
         return scale * math.cos(2.0 * math.pi * (n % length) / length)
@@ -285,28 +291,31 @@
     def sine(n):
         return scale * math.sin(2.0 * math.pi * (n % length) / length)
 
-    def block(source, k, row):
+    def turn(row, carry):
         here = pl.ds(pl.multiple_of(row * step, step), step)
-        values = [source[t, here, :] for t in range(length)]
+        values = [all_ref[t, here, :] for t in range(length)]
         for f in range(length // 2 + 1):
             real = sum(cosine(f * t) * values[t] for t in range(length))
-            out_ref[k, 0, f, here, :] = real
+            imag = sum(-sine(f * t) * values[t] for t in range(length))
+            done_ref[0, f, here, :] = real
+            done_ref[1, f, here, :] = imag
             mirrored = (length - f) % length
             if mirrored != f:
-                imag = sum(-sine(f * t) * values[t] for t in range(1, length))
-                out_ref[k, 0, mirrored, here, :] = real
-                out_ref[k, 1, f, here, :] = imag
-                out_ref[k, 1, mirrored, here, :] = -imag
-            else:
-                imag = sum(-sine(f * t) * values[t] for t in range(length))
-                out_ref[k, 1, f, here, :] = imag
-
-    def turn(row, carry):
-        block(keep_ref, core, row)
-        block(got_ref, 1 - core, row)
+                done_ref[0, mirrored, here, :] = real
+                done_ref[1, mirrored, here, :] = -imag
         return carry
 
-    lax.fori_loop(0, rows // step, turn, 0)
+    copies = []
+    for g in range(groups):
+        lax.fori_loop(g * size // step, (g + 1) * size // step, turn, 0)
+        span = pl.ds(g * size, size)
+        copy = pltpu.make_async_copy(
+            done_ref.at[:, :, span, :], out_ref.at[core if own else 1 - core, :, :, span, :], sems.at[g]
+        )
+        copy.start()
+        copies.append(copy)
+    for copy in copies:
+        copy.wait()
 
 
 def paired_body(propagators, current_op):
@@ -341,10 +350,11 @@
 
     arrays, plan = [], [[] for _ in range(count)]
 
-    def keep(x, to, ts):
-        plan[to].append((len(arrays), ts))
+    def keep(x, to, ts, rank):
+        plan[to].extend((rank, t, len(arrays), i) for i, t in enumerate(ts))
         arrays.append(x)
 
+    soon = [(1, 0), (1, count - 1)]
     before = [along(x, (0, 1)) for x in prod]
     shapes = [square] * 3 + [(2, 2 * (order // 3), order), (2, rows, order)] + [(1, rows, order)] * (count - 1)
     sym, g0, g1, pack, own, *firsts = local_call(
@@ -352,9 +362,9 @@
         outside=(CHUNKS + 1,),
     )
     ahead = along(pack, [(j, j - 1) for j in range(2, count)])
-    keep(own, 0, [0, 1])
+    keep(own, 0, [0, 1], 0)
     for to in range(1, count):
-        keep(along(firsts[to - 1], (0, to)), to, [0])
+        keep(along(firsts[to - 1], (0, to)), to, [0], 1 if to == 1 else 5)
     for place in range(1, count):
         after = []
         for x in before if place + 1 < count else ():
@@ -368,7 +378,11 @@
             (sym, g0, g1, *before), scratch=scratch,
         )
         for to, x in zip(receivers, outs):
-            keep(x if to == place else along(x, (place, to)), to, heis_slices(place, to))
+            ts = heis_slices(place, to)
+            if to == place:
+                keep(x, to, ts, 0)
+            else:
+                keep(along(x, (place, to)), to, ts, 1 if (place, to) in soon else 3)
         if place + 1 < count:
             outs = local_call(
                 lambda *r, p=place: ahead_kernel(p, count, CHUNKS, *r),
@@ -376,19 +390,44 @@
             )
             for to, x in enumerate(outs):
                 ts = [2 * place + 2, 2 * place + 3]
-                keep(x if to == place else along(x, (place, to)), to, ts)
+                if to == place:
+                    keep(x, to, ts, 2)
+                else:
+                    keep(along(x, (place, to)), to, ts, 4)
             before = following
     width = order // 2
-    kept, give = local_call(lambda *r: gather_kernel(plan, *r), [(count * slices, rows, width)] * 2, arrays)
-    taken = lax.ppermute(give, "col", swap)
-    return pl.pallas_call(
-        spectrum_kernel,
-        out_shape=jax.ShapeDtypeStruct((kdev, 2, count * slices, rows, width), jnp.float32),
-        in_specs=[VMEM] * 2,
-        out_specs=VMEM,
-        compiler_params=GRANT,
-        name="spectrum",
-    )(*(pltpu.with_memory_space_constraint(x, pltpu.VMEM) for x in (kept, taken)))
+    length = count * slices
+    half = length // 2
+    ordered = [[entry[1:] for entry in sorted(entries)] for entries in plan]
+    kept, taken, tables = [], [], []
+    for chosen in ([o[:half] for o in ordered], [o[half:] for o in ordered]):
+        used = sorted({source for entries in chosen for _, source, _ in entries})
+        local = [[(t, used.index(source), i) for t, source, i in entries] for entries in chosen]
+        mine_part, give = local_call(
+            lambda *r, c=local: gather_kernel(c, *r), [(half, rows, width)] * 2,
+            [arrays[source] for source in used],
+        )
+        taken.append(lax.ppermute(give, "col", swap))
+        kept.append(mine_part)
+        tables.append([[t for t, _, _ in entries] for entries in chosen])
+
+    def spectrum(own, parts, so_far):
+        return pl.pallas_call(
+            lambda *r: spectrum_kernel(own, tables, *r),
+            out_shape=jax.ShapeDtypeStruct((kdev, 2, length, rows, width), jnp.float32),
+            in_specs=[VMEM] * 2 + [pl.BlockSpec(memory_space=pl.ANY)] * len(so_far),
+            out_specs=pl.BlockSpec(memory_space=pl.ANY),
+            scratch_shapes=[
+                pltpu.VMEM((length, rows, width), jnp.float32),
+                pltpu.VMEM((2, length, rows, width), jnp.float32),
+                pltpu.SemaphoreType.DMA((3,)),
+            ],
+            input_output_aliases={2: 0} if so_far else {},
+            compiler_params=GRANT,
+            name="spectrum",
+        )(*(pltpu.with_memory_space_constraint(x, pltpu.VMEM) for x in parts), *so_far)
+
+    return spectrum(False, taken, [spectrum(True, kept, [])])
 
 
 def is_paired(mesh, kdev, slices, order):

time: 74.8 us -> 75.3 us (level)
  starting transfers between devices: 23.8 us -> 30.5 us
  waiting for transfers between devices: 41.3 us -> 34.8 us
    ppermute x20, starting transfers between devices: 23.2 us -> 29.8 us  [along(): return lax.ppermute(x, 'tm', [hop] if isinstance(hop, tuple) else hop)]
    ppermute x20, waiting for transfers between devices: 38.5 us -> 33.9 us  [along(): return lax.ppermute(x, 'tm', [hop] if isinstance(hop, tuple) else hop)]
    ppermute x1 -> x2, waiting for transfers between devices: 2.27 us -> 0.28 us  [paired_body(): taken.append(lax.ppermute(give, 'col', swap))]
    pallas_call x1 -> x2, Pallas kernels: 2.72 us -> 2.82 us  [spectrum(): pl.pallas_call(lambda *r: spectrum_kernel(own, tables, *r), out_shape=jax...]
    pallas_call x14 -> x15, Pallas kernels: 3.82 us -> 3.92 us  [local_call(): pl.pallas_call(kernel, out_shape=[pltpu.VMEM(s, jnp.float32) for s in out...]
  transfers between devices with their start and end apart: 22 -> 23, of which waited for: 10 -> 7; matrix products, arithmetic and copies ran while one was open for 0% -> 0% of each run, Pallas kernels for 2% -> 4%
where the time goes in v2:
time: 75.3 us; the launch traced here: 74.8 us
  waiting for transfers between devices  34.8 us (46%)
  starting transfers between devices  30.5 us (41%)
  Pallas kernels  8.98 us (12%)
    ppermute x20, waiting for transfers between devices, along(): return lax.ppermute(x, 'tm', [hop] if isinstance(hop, tuple) else hop)  33.9 us
    ppermute x20, starting transfers between devices, along(): return lax.ppermute(x, 'tm', [hop] if isinstance(hop, tuple) else hop)  29.8 us
    pallas_call x15, Pallas kernels, local_call(): pl.pallas_call(kernel, out_shape=[pltpu.VMEM(s, jnp.float32) for s in out...  3.92 us
    pallas_call x2, Pallas kernels, spectrum(): pl.pallas_call(lambda *r: spectrum_kernel(own, tables, *r), out_shape=jax...  2.82 us
    pallas_call x2, Pallas kernels, pick(): pl.pallas_call(lambda *r: pick_kernel(own, *r), out_shape=pltpu.VMEM((sli...  2.24 us
  transfers between devices with their start and end apart: 23, of which 7 were waited for; matrix products, arithmetic and copies ran while one was open for 0% of the time, Pallas kernels for 4%

profile of v2, /device:TPU:0, one launch (start us, length us, event | category | flops | bytes accessed | tf_op | source)
XLA Modules:
  0.0 74.8 jit_solution(6984293972729684196)
XLA Ops:
  0.0 1.2 %shard_map.29 = f32[2,192,384]{2,1,0:T(8,128)S(1)} custom-call(f32[2,2,192,384]{3,2,1,0:T(8,128)} %bitcast.1), custom_call_target="tpu_custom_call" | custom-call | tf_op jit(solution)/shard_map/pallas_call | solution.py:332
  1.2 0.6 collective-permute-start
  1.7 1.1 %shard_map.28.mine_ref = f32[2,192,384]{2,1,0:T(8,128)S(1)} custom-call(f32[2,2,192,384]{3,2,1,0:T(8,128)} %bitcast.2), custom_call_target="tpu_custom_call" | custom-call | tf_op jit(solution)/shard_map/pallas_call | solution.py:332
  2.8 0.6 collective-permute-done.got_ref
  3.4 0.8 %shard_map.30 = (f32[384,384]{1,0:T(8,128)S(1)}, f32[128,384]{1,0:T(8,128)S(1)}, f32[128,384]{1,0:T(8,128)S(1)}, f32[128,384]{1,0:T(8,128)S(1)}) custom-call(f32[2,192,384]{2,1,0:T(8,128)S(1)} %shard_map.28.mine_ref, f32[2,192,384]{2,1,0:T(8,128)S(1)} %collective-permute-done.got_ref), custom_call_target="tpu_custom_call" | custom-call | tf_op jit(solution)/shard_map/pallas_call | solution.py:115
  4.2 2.4 %shard_map.31 = (f32[384,384]{1,0:T(8,128)S(1)}, f32[384,384]{1,0:T(8,128)S(1)}, f32[384,384]{1,0:T(8,128)S(1)}, f32[2,256,384]{2,1,0:T(8,128)S(1)}, f32[2,96,38...) custom-call(f32[384,384]{1,0:T(8,128)S(1)} %get-tuple-element.32.r_0_, ...), custom_call_target="tpu_custom_call" | custom-call | tf_op jit(solution)/shard_map/pallas_call | solution.py:115
  6.6 0.7 collective-permute-start.10
  7.3 5.4 %collective-permute-start.4 = (f32[128,384]{1,0:T(8,128)S(1)}, f32[128,384]{1,0:T(8,128)S(1)}, u32[]{:S(2)}, u32[]{:S(2)}) collective-permute-start(f32[128,384]{1,0:T(8,128)S(1)} %get-tuple-element.35.r_3_), channel_id=1, source_target_pairs={{0,4},{1,5},{2,6},{3,7},{16,20},{17,21},{18,22},{19,23}} | collective-permute-start | bytes 589832 | tf_op jit(solution)/shard_map/ppermute | solution.py:349
  12.7 1.3 %collective-permute-start.3 = (f32[128,384]{1,0:T(8,128)S(1)}, f32[128,384]{1,0:T(8,128)S(1)}, u32[]{:S(2)}, u32[]{:S(2)}) collective-permute-start(f32[128,384]{1,0:T(8,128)S(1)} %get-tuple-element.34.r_2_), channel_id=1, source_target_pairs={{0,4},{1,5},{2,6},{3,7},{16,20},{17,21},{18,22},{19,23}} | collective-permute-start | bytes 589832 | tf_op jit(solution)/shard_map/ppermute | solution.py:349
  14.0 2.1 %collective-permute-start.15 = (f32[1,96,384]{2,1,0:T(8,128)S(1)}, f32[1,96,384]{2,1,0:T(8,128)S(1)}, u32[]{:S(2)}, u32[]{:S(2)}) collective-permute-start(f32[1,96,384]{2,1,0:T(8,128)S(1)} %get-tuple-element.48), channel_id=1, source_target_pairs={{0,8},{1,9},{2,10},{3,11},{16,24},{17,25},{18,26},{19,27}} | collective-permute-start | bytes 442376 | tf_op jit(solution)/shard_map/ppermute | solution.py:349
  16.1 1.3 %collective-permute-start.2 = (f32[128,384]{1,0:T(8,128)S(1)}, f32[128,384]{1,0:T(8,128)S(1)}, u32[]{:S(2)}, u32[]{:S(2)}) collective-permute-start(f32[128,384]{1,0:T(8,128)S(1)} %get-tuple-element.33.r_1_), channel_id=1, source_target_pairs={{0,4},{1,5},{2,6},{3,7},{16,20},{17,21},{18,22},{19,23}} | collective-permute-start | bytes 589832 | tf_op jit(solution)/shard_map/ppermute | solution.py:349
  17.9 1.3 %collective-permute-start.16 = (f32[1,96,384]{2,1,0:T(8,128)S(1)}, f32[1,96,384]{2,1,0:T(8,128)S(1)}, u32[]{:S(2)}, u32[]{:S(2)}) collective-permute-start(f32[1,96,384]{2,1,0:T(8,128)S(1)} %get-tuple-element.49), channel_id=1, source_target_pairs={{0,12},{1,13},{2,14},{3,15},{16,28},{17,29},{18,30},{19,31}} | collective-permute-start | bytes 442376 | tf_op jit(solution)/shard_map/ppermute | solution.py:349
  19.3 6.1 %collective-permute-done.15.r_0_ = f32[1,96,384]{2,1,0:T(8,128)S(1)} collective-permute-done((f32[1,96,384]{2,1,0:T(8,128)S(1)}, f32[1,96,384]{2,1,0:T(8,128)S(1)}, u32[]{:S(2)}, u32[]{:S(2)}) %collective-permute-start.15) | collective-permute-done | bytes 147488 | tf_op jit(solution)/shard_map/ppermute | solution.py:349
  25.3 0.7 collective-permute-start.9
  26.0 7.1 %collective-permute-start.1 = (f32[1,96,384]{2,1,0:T(8,128)S(1)}, f32[1,96,384]{2,1,0:T(8,128)S(1)}, u32[]{:S(2)}, u32[]{:S(2)}) collective-permute-start(f32[1,96,384]{2,1,0:T(8,128)S(1)} %get-tuple-element.37), channel_id=1, source_target_pairs={{0,4},{1,5},{2,6},{3,7},{16,20},{17,21},{18,22},{19,23}} | collective-permute-start | bytes 442376 | tf_op jit(solution)/shard_map/ppermute | solution.py:349
  33.1 0.7 collective-permute-start.8
  33.8 0.7 collective-permute-start.7
  34.6 1.2 %collective-permute-done.1.r_1_ = f32[1,96,384]{2,1,0:T(8,128)S(1)} collective-permute-done((f32[1,96,384]{2,1,0:T(8,128)S(1)}, f32[1,96,384]{2,1,0:T(8,128)S(1)}, u32[]{:S(2)}, u32[]{:S(2)}) %collective-permute-start.1) | collective-permute-done | bytes 147488 | tf_op jit(solution)/shard_map/ppermute | solution.py:349
  35.7 0.7 collective-permute-start.6
  36.4 1.3 %collective-permute-start.5 = (f32[2,96,384]{2,1,0:T(8,128)S(1)}, f32[2,96,384]{2,1,0:T(8,128)S(1)}, u32[]{:S(2)}, u32[]{:S(2)}) collective-permute-start(f32[2,96,384]{2,1,0:T(8,128)S(1)} %get-tuple-element.41), channel_id=1, source_target_pairs={{4,0},{5,1},{6,2},{7,3},{20,16},{21,17},{22,18},{23,19}} | collective-permute-start | bytes 884744 | tf_op jit(solution)/shard_map/ppermute | solution.py:349
  37.8 0.7 collective-permute-start.13
  38.5 0.7 collective-permute-start.12
  39.2 0.7 collective-permute-start.11
  40.1 0.7 collective-permute-start.17
  40.8 6.0 %collective-permute-done.5.r_2_ = f32[2,96,384]{2,1,0:T(8,128)S(1)} collective-permute-done((f32[2,96,384]{2,1,0:T(8,128)S(1)}, f32[2,96,384]{2,1,0:T(8,128)S(1)}, u32[]{:S(2)}, u32[]{:S(2)}) %collective-permute-start.5) | collective-permute-done | bytes 294944 | tf_op jit(solution)/shard_map/ppermute | solution.py:349
  46.8 0.7 collective-permute-start.19
  47.5 1.3 %collective-permute-start.18 = (f32[2,96,384]{2,1,0:T(8,128)S(1)}, f32[2,96,384]{2,1,0:T(8,128)S(1)}, u32[]{:S(2)}, u32[]{:S(2)}) collective-permute-start(f32[2,96,384]{2,1,0:T(8,128)S(1)} %get-tuple-element.51), channel_id=1, source_target_pairs={{4,0},{5,1},{6,2},{7,3},{20,16},{21,17},{22,18},{23,19}} | collective-permute-start | bytes 884744 | tf_op jit(solution)/shard_map/ppermute | solution.py:349
  48.8 1.3 %collective-permute-start.20 = (f32[2,96,384]{2,1,0:T(8,128)S(1)}, f32[2,96,384]{2,1,0:T(8,128)S(1)}, u32[]{:S(2)}, u32[]{:S(2)}) collective-permute-start(f32[2,96,384]{2,1,0:T(8,128)S(1)} %get-tuple-element.54), channel_id=1, source_target_pairs={{8,0},{9,1},{10,2},{11,3},{24,16},{25,17},{26,18},{27,19}} | collective-permute-start | bytes 884744 | tf_op jit(solution)/shard_map/ppermute | solution.py:349
  50.1 0.7 collective-permute-start.21
  51.2 20.1 %collective-permute-done.18.r_4_ = f32[2,96,384]{2,1,0:T(8,128)S(1)} collective-permute-done((f32[2,96,384]{2,1,0:T(8,128)S(1)}, f32[2,96,384]{2,1,0:T(8,128)S(1)}, u32[]{:S(2)}, u32[]{:S(2)}) %collective-permute-start.18) | collective-permute-done | bytes 294944 | tf_op jit(solution)/shard_map/ppermute | solution.py:349
  71.6 1.4 %spectrum.2.r_2_ = f32[2,2,8,96,192]{4,3,2,1,0:T(8,128)} custom-call(f32[4,96,192]{2,1,0:T(8,128)S(1)} %get-tuple-element.57.r_0_, f32[4,96,192]{2,1,0:T(8,128)S(1)} %get-tuple-element.58.r_1_), custom_call_target="tpu_custom_call" | custom-call | tf_op jit(solution)/shard_map/spectrum/pallas_call | solution.py:415
  73.3 1.4 %spectrum.3 = f32[2,2,8,96,192]{4,3,2,1,0:T(8,128)} custom-call(f32[4,96,192]{2,1,0:T(8,128)S(1)} %collective-permute-done.14.r_0_, f32[4,96,192]{2,1,0:T(8,128)S(1)} %collective-permute-done.22.r_1_, f32[2,2,8,96,192]{4,3,2,1,0:T(8,128)} %spectrum.2.r_2_), custom_call_target="tpu_custom_call", output_to_operand_aliasing={{}: (2, {})} | custom-call | tf_op jit(solution)/shard_map/spectrum/pallas_call | solution.py:415
  (35 shorter events, 1.7 us)
Async XLA Ops:
  0.0 4.2 %copy-start = (f32[2,384,384]{2,1,0:T(8,128)S(1)}, f32[2,384,384]{2,1,0:T(8,128)}, u32[]{:S(2)}) copy-start(f32[2,384,384]{2,1,0:T(8,128)} %r_4_.1) | copy-start | bytes 3538948
  1.2 2.2 %collective-permute-start = (f32[2,192,384]{2,1,0:T(8,128)S(1)}, f32[2,192,384]{2,1,0:T(8,128)S(1)}, u32[]{:S(2)}, u32[]{:S(2)}) collective-permute-start(f32[2,192,384]{2,1,0:T(8,128)S(1)} %shard_map.29), channel_id=1, source_target_pairs={{0,1},{1,0},{2,3},{3,2},{4,5},{5,4},{6,7},{7,6},{8,9},{9,8},{10,11... | collective-permute-start | bytes 1769480 | tf_op jit(solution)/shard_map/ppermute | solution.py:341
  6.6 32.6 %collective-permute-start.10 = (f32[2,256,384]{2,1,0:T(8,128)S(1)}, f32[2,256,384]{2,1,0:T(8,128)S(1)}, u32[]{:S(2)}, u32[]{:S(2)}) collective-permute-start(f32[2,256,384]{2,1,0:T(8,128)S(1)} %get-tuple-element.45), channel_id=1, source_target_pairs={{8,4},{12,8},{9,5},{13,9},{10,6},{14,10},{11,7},{15,11},{24,20},{2... | collective-permute-start | bytes 2359304 | tf_op jit(solution)/shard_map/ppermute | solution.py:349
  7.3 10.7 %collective-permute-start.4 = (f32[128,384]{1,0:T(8,128)S(1)}, f32[128,384]{1,0:T(8,128)S(1)}, u32[]{:S(2)}, u32[]{:S(2)}) collective-permute-start(f32[128,384]{1,0:T(8,128)S(1)} %get-tuple-element.35.r_3_), channel_id=1, source_target_pairs={{0,4},{1,5},{2,6},{3,7},{16,20},{17,21},{18,22},{19,23}} | collective-permute-start | bytes 589832 | tf_op jit(solution)/shard_map/ppermute | solution.py:349
  12.7 13.3 %collective-permute-start.3 = (f32[128,384]{1,0:T(8,128)S(1)}, f32[128,384]{1,0:T(8,128)S(1)}, u32[]{:S(2)}, u32[]{:S(2)}) collective-permute-start(f32[128,384]{1,0:T(8,128)S(1)} %get-tuple-element.34.r_2_), channel_id=1, source_target_pairs={{0,4},{1,5},{2,6},{3,7},{16,20},{17,21},{18,22},{19,23}} | collective-permute-start | bytes 589832 | tf_op jit(solution)/shard_map/ppermute | solution.py:349
  14.0 11.3 %collective-permute-start.15 = (f32[1,96,384]{2,1,0:T(8,128)S(1)}, f32[1,96,384]{2,1,0:T(8,128)S(1)}, u32[]{:S(2)}, u32[]{:S(2)}) collective-permute-start(f32[1,96,384]{2,1,0:T(8,128)S(1)} %get-tuple-element.48), channel_id=1, source_target_pairs={{0,8},{1,9},{2,10},{3,11},{16,24},{17,25},{18,26},{19,27}} | collective-permute-start | bytes 442376 | tf_op jit(solution)/shard_map/ppermute | solution.py:349
  16.1 17.0 %collective-permute-start.2 = (f32[128,384]{1,0:T(8,128)S(1)}, f32[128,384]{1,0:T(8,128)S(1)}, u32[]{:S(2)}, u32[]{:S(2)}) collective-permute-start(f32[128,384]{1,0:T(8,128)S(1)} %get-tuple-element.33.r_1_), channel_id=1, source_target_pairs={{0,4},{1,5},{2,6},{3,7},{16,20},{17,21},{18,22},{19,23}} | collective-permute-start | bytes 589832 | tf_op jit(solution)/shard_map/ppermute | solution.py:349
  17.9 15.9 %collective-permute-start.16 = (f32[1,96,384]{2,1,0:T(8,128)S(1)}, f32[1,96,384]{2,1,0:T(8,128)S(1)}, u32[]{:S(2)}, u32[]{:S(2)}) collective-permute-start(f32[1,96,384]{2,1,0:T(8,128)S(1)} %get-tuple-element.49), channel_id=1, source_target_pairs={{0,12},{1,13},{2,14},{3,15},{16,28},{17,29},{18,30},{19,31}} | collective-permute-start | bytes 442376 | tf_op jit(solution)/shard_map/ppermute | solution.py:349
  25.3 11.1 %collective-permute-start.9 = (f32[128,384]{1,0:T(8,128)S(1)}, f32[128,384]{1,0:T(8,128)S(1)}, u32[]{:S(2)}, u32[]{:S(2)}) collective-permute-start(f32[128,384]{1,0:T(8,128)S(1)} %shard_map.35.r_3_), channel_id=1, source_target_pairs={{4,8},{5,9},{6,10},{7,11},{20,24},{21,25},{22,26},{23,27}} | collective-permute-start | bytes 589832 | tf_op jit(solution)/shard_map/ppermute | solution.py:349
  26.0 9.8 %collective-permute-start.1 = (f32[1,96,384]{2,1,0:T(8,128)S(1)}, f32[1,96,384]{2,1,0:T(8,128)S(1)}, u32[]{:S(2)}, u32[]{:S(2)}) collective-permute-start(f32[1,96,384]{2,1,0:T(8,128)S(1)} %get-tuple-element.37), channel_id=1, source_target_pairs={{0,4},{1,5},{2,6},{3,7},{16,20},{17,21},{18,22},{19,23}} | collective-permute-start | bytes 442376 | tf_op jit(solution)/shard_map/ppermute | solution.py:349
  33.1 4.6 %collective-permute-start.8 = (f32[128,384]{1,0:T(8,128)S(1)}, f32[128,384]{1,0:T(8,128)S(1)}, u32[]{:S(2)}, u32[]{:S(2)}) collective-permute-start(f32[128,384]{1,0:T(8,128)S(1)} %shard_map.34.r_2_), channel_id=1, source_target_pairs={{4,8},{5,9},{6,10},{7,11},{20,24},{21,25},{22,26},{23,27}} | collective-permute-start | bytes 589832 | tf_op jit(solution)/shard_map/ppermute | solution.py:349
  33.8 4.6 %collective-permute-start.7 = (f32[128,384]{1,0:T(8,128)S(1)}, f32[128,384]{1,0:T(8,128)S(1)}, u32[]{:S(2)}, u32[]{:S(2)}) collective-permute-start(f32[128,384]{1,0:T(8,128)S(1)} %shard_map.33.r_1_), channel_id=1, source_target_pairs={{4,8},{5,9},{6,10},{7,11},{20,24},{21,25},{22,26},{23,27}} | collective-permute-start | bytes 589832 | tf_op jit(solution)/shard_map/ppermute | solution.py:349
  35.7 4.4 %collective-permute-start.6 = (f32[2,96,384]{2,1,0:T(8,128)S(1)}, f32[2,96,384]{2,1,0:T(8,128)S(1)}, u32[]{:S(2)}, u32[]{:S(2)}) collective-permute-start(f32[2,96,384]{2,1,0:T(8,128)S(1)} %get-tuple-element.43), channel_id=1, source_target_pairs={{4,12},{5,13},{6,14},{7,15},{20,28},{21,29},{22,30},{23,31}} | collective-permute-start | bytes 884744 | tf_op jit(solution)/shard_map/ppermute | solution.py:349
  36.4 10.4 %collective-permute-start.5 = (f32[2,96,384]{2,1,0:T(8,128)S(1)}, f32[2,96,384]{2,1,0:T(8,128)S(1)}, u32[]{:S(2)}, u32[]{:S(2)}) collective-permute-start(f32[2,96,384]{2,1,0:T(8,128)S(1)} %get-tuple-element.41), channel_id=1, source_target_pairs={{4,0},{5,1},{6,2},{7,3},{20,16},{21,17},{22,18},{23,19}} | collective-permute-start | bytes 884744 | tf_op jit(solution)/shard_map/ppermute | solution.py:349
  37.8 9.8 %collective-permute-start.13 = (f32[128,384]{1,0:T(8,128)S(1)}, f32[128,384]{1,0:T(8,128)S(1)}, u32[]{:S(2)}, u32[]{:S(2)}) collective-permute-start(f32[128,384]{1,0:T(8,128)S(1)} %shard_map.39.r_3_), channel_id=1, source_target_pairs={{8,12},{9,13},{10,14},{11,15},{24,28},{25,29},{26,30},{27,31}} | collective-permute-start | bytes 589832 | tf_op jit(solution)/shard_map/ppermute | solution.py:349
  38.5 10.3 %collective-permute-start.12 = (f32[128,384]{1,0:T(8,128)S(1)}, f32[128,384]{1,0:T(8,128)S(1)}, u32[]{:S(2)}, u32[]{:S(2)}) collective-permute-start(f32[128,384]{1,0:T(8,128)S(1)} %shard_map.38.r_2_), channel_id=1, source_target_pairs={{8,12},{9,13},{10,14},{11,15},{24,28},{25,29},{26,30},{27,31}} | collective-permute-start | bytes 589832 | tf_op jit(solution)/shard_map/ppermute | solution.py:349
  39.2 10.9 %collective-permute-start.11 = (f32[128,384]{1,0:T(8,128)S(1)}, f32[128,384]{1,0:T(8,128)S(1)}, u32[]{:S(2)}, u32[]{:S(2)}) collective-permute-start(f32[128,384]{1,0:T(8,128)S(1)} %shard_map.37.r_1_), channel_id=1, source_target_pairs={{8,12},{9,13},{10,14},{11,15},{24,28},{25,29},{26,30},{27,31}} | collective-permute-start | bytes 589832 | tf_op jit(solution)/shard_map/ppermute | solution.py:349
  40.1 10.9 %collective-permute-start.17 = (f32[2,96,384]{2,1,0:T(8,128)S(1)}, f32[2,96,384]{2,1,0:T(8,128)S(1)}, u32[]{:S(2)}, u32[]{:S(2)}) collective-permute-start(f32[2,96,384]{2,1,0:T(8,128)S(1)} %get-tuple-element.50), channel_id=1, source_target_pairs={{4,8},{5,9},{6,10},{7,11},{20,24},{21,25},{22,26},{23,27}} | collective-permute-start | bytes 884744 | tf_op jit(solution)/shard_map/ppermute | solution.py:349
  46.8 4.3 %collective-permute-start.19 = (f32[2,96,384]{2,1,0:T(8,128)S(1)}, f32[2,96,384]{2,1,0:T(8,128)S(1)}, u32[]{:S(2)}, u32[]{:S(2)}) collective-permute-start(f32[2,96,384]{2,1,0:T(8,128)S(1)} %get-tuple-element.53), channel_id=1, source_target_pairs={{8,12},{9,13},{10,14},{11,15},{24,28},{25,29},{26,30},{27,31}} | collective-permute-start | bytes 884744 | tf_op jit(solution)/shard_map/ppermute | solution.py:349
  47.5 23.8 %collective-permute-start.18 = (f32[2,96,384]{2,1,0:T(8,128)S(1)}, f32[2,96,384]{2,1,0:T(8,128)S(1)}, u32[]{:S(2)}, u32[]{:S(2)}) collective-permute-start(f32[2,96,384]{2,1,0:T(8,128)S(1)} %get-tuple-element.51), channel_id=1, source_target_pairs={{4,0},{5,1},{6,2},{7,3},{20,16},{21,17},{22,18},{23,19}} | collective-permute-start | bytes 884744 | tf_op jit(solution)/shard_map/ppermute | solution.py:349
  48.8 22.5 %collective-permute-start.20 = (f32[2,96,384]{2,1,0:T(8,128)S(1)}, f32[2,96,384]{2,1,0:T(8,128)S(1)}, u32[]{:S(2)}, u32[]{:S(2)}) collective-permute-start(f32[2,96,384]{2,1,0:T(8,128)S(1)} %get-tuple-element.54), channel_id=1, source_target_pairs={{8,0},{9,1},{10,2},{11,3},{24,16},{25,17},{26,18},{27,19}} | collective-permute-start | bytes 884744 | tf_op jit(solution)/shard_map/ppermute | solution.py:349
  50.1 21.1 %collective-permute-start.21 = (f32[2,96,384]{2,1,0:T(8,128)S(1)}, f32[2,96,384]{2,1,0:T(8,128)S(1)}, u32[]{:S(2)}, u32[]{:S(2)}) collective-permute-start(f32[2,96,384]{2,1,0:T(8,128)S(1)} %get-tuple-element.55), channel_id=1, source_target_pairs={{8,4},{9,5},{10,6},{11,7},{24,20},{25,21},{26,22},{27,23}} | collective-permute-start | bytes 884744 | tf_op jit(solution)/shard_map/ppermute | solution.py:349
  51.1 21.9 %collective-permute-start.14 = (f32[4,96,192]{2,1,0:T(8,128)S(1)}, f32[4,96,192]{2,1,0:T(8,128)S(1)}, u32[]{:S(2)}, u32[]{:S(2)}) collective-permute-start(f32[4,96,192]{2,1,0:T(8,128)S(1)} %get-tuple-element.47), channel_id=1, source_target_pairs={{0,1},{1,0},{2,3},{3,2},{4,5},{5,4},{6,7},{7,6},{8,9},{9,8},{10,11... | collective-permute-start | bytes 884744 | tf_op jit(solution)/shard_map/ppermute | solution.py:410
  71.5 1.8 %collective-permute-start.22 = (f32[4,96,192]{2,1,0:T(8,128)S(1)}, f32[4,96,192]{2,1,0:T(8,128)S(1)}, u32[]{:S(2)}, u32[]{:S(2)}) collective-permute-start(f32[4,96,192]{2,1,0:T(8,128)S(1)} %get-tuple-element.56), channel_id=1, source_target_pairs={{0,1},{1,0},{2,3},{3,2},{4,5},{5,4},{6,7},{7,6},{8,9},{9,8},{10,11... | collective-permute-start | bytes 884744 | tf_op jit(solution)/shard_map/ppermute | solution.py:410

commit v3 on v2

--- a/solution.py
+++ b/solution.py
@@ -207,11 +207,11 @@
         outs[to][position] = heis[to * rows - top:(to + 1) * rows - top, :]
 
 
-def heis_kernel(place, count, chunks, *refs):
+def heis_kernel(place, receivers, count, chunks, *refs):
     sym_ref, g0_ref, g1_ref = refs[:3]
     before = refs[3:3 + chunks]
     outs, r_ref, t_ref = refs[3 + chunks:-2], refs[-2], refs[-1]
-    outs = dict(zip(heis_receivers(place, count), outs))
+    outs = dict(zip(receivers, outs))
 
     @pl.when(lax.axis_index("tm") == place)
     def _():
@@ -222,6 +222,8 @@
         for i, middle_ref in enumerate((sym_ref, g0_ref, g1_ref)):
             t = 2 * place - 1 + i
             wanted = {to: heis_slices(place, to).index(t) for to in outs if t in heis_slices(place, to)}
+            if not wanted:
+                continue
             top, bottom = min(wanted) * rows, (max(wanted) + 1) * rows
             weighted = product(as_left(r_ref[top:bottom, :]), as_right(middle_ref[...]))
             rows_out(outs, wanted, product_t(as_left(weighted), t_ref[...]), top, rows)
@@ -252,8 +254,10 @@
     return [2 * place, 2 * place + 1]
 
 
-def heis_receivers(place, count):
-    return [0] * (place == 1) + list(range(place, count))
+def heis_groups(place, count):
+    if place == 1:
+        return [[0], list(range(1, count))]
+    return [list(range(place + 1, count)), [place]] if place + 1 < count else [[place]]
 
 
 def gather_kernel(chosen, *refs):
@@ -371,18 +375,18 @@
             after += local_call(lambda *r, p=place: hop_kernel(p, *r), [chunk], (x, *prod))
         if place + 1 < count:
             following = [along(x, (place, place + 1)) for x in after]
-        receivers = heis_receivers(place, count)
-        outs = local_call(
-            lambda *r, p=place: heis_kernel(p, count, CHUNKS, *r),
-            [(len(heis_slices(place, to)), rows, order) for to in receivers],
-            (sym, g0, g1, *before), scratch=scratch,
-        )
-        for to, x in zip(receivers, outs):
-            ts = heis_slices(place, to)
-            if to == place:
-                keep(x, to, ts, 0)
-            else:
-                keep(along(x, (place, to)), to, ts, 1 if (place, to) in soon else 3)
+        for receivers in heis_groups(place, count):
+            outs = local_call(
+                lambda *r, p=place, w=receivers: heis_kernel(p, w, count, CHUNKS, *r),
+                [(len(heis_slices(place, to)), rows, order) for to in receivers],
+                (sym, g0, g1, *before), scratch=scratch,
+            )
+            for to, x in zip(receivers, outs):
+                ts = heis_slices(place, to)
+                if to == place:
+                    keep(x, to, ts, 0)
+                else:
+                    keep(along(x, (place, to)), to, ts, 1 if (place, to) in soon else 3)
         if place + 1 < count:
             outs = local_call(
                 lambda *r, p=place: ahead_kernel(p, count, CHUNKS, *r),

time: 75.3 us -> 75.7 us (level)
  starting transfers between devices: 30.5 us -> 23.9 us
  waiting for transfers between devices: 34.8 us -> 41.1 us
    ppermute x20, starting transfers between devices: 29.8 us -> 23.2 us  [along(): return lax.ppermute(x, 'tm', [hop] if isinstance(hop, tuple) else hop)]
    ppermute x20, waiting for transfers between devices: 33.9 us -> 40.2 us  [along(): return lax.ppermute(x, 'tm', [hop] if isinstance(hop, tuple) else hop)]
    pallas_call x15 -> x17, Pallas kernels: 3.92 us -> 3.95 us  [local_call(): pl.pallas_call(kernel, out_shape=[pltpu.VMEM(s, jnp.float32) for s in out...]
  transfers between devices with their start and end apart: 23 -> 23, of which waited for: 7 -> 9; matrix products, arithmetic and copies ran while one was open for 0% -> 0% of each run, Pallas kernels for 4% -> 4%
where the time goes in v3:
time: 75.7 us; the launch traced here: 74.5 us
  waiting for transfers between devices  41.1 us (54%)
  starting transfers between devices  23.9 us (32%)
  Pallas kernels  9.01 us (12%)
    ppermute x20, waiting for transfers between devices, along(): return lax.ppermute(x, 'tm', [hop] if isinstance(hop, tuple) else hop)  40.2 us
    ppermute x20, starting transfers between devices, along(): return lax.ppermute(x, 'tm', [hop] if isinstance(hop, tuple) else hop)  23.2 us
    pallas_call x17, Pallas kernels, local_call(): pl.pallas_call(kernel, out_shape=[pltpu.VMEM(s, jnp.float32) for s in out...  3.95 us
    pallas_call x2, Pallas kernels, spectrum(): pl.pallas_call(lambda *r: spectrum_kernel(own, tables, *r), out_shape=jax...  2.82 us
    pallas_call x2, Pallas kernels, pick(): pl.pallas_call(lambda *r: pick_kernel(own, *r), out_shape=pltpu.VMEM((sli...  2.24 us
  transfers between devices with their start and end apart: 23, of which 9 were waited for; matrix products, arithmetic and copies ran while one was open for 0% of the time, Pallas kernels for 4%

profile of v3, /device:TPU:0, one launch (start us, length us, event | category | flops | bytes accessed | tf_op | source)
XLA Modules:
  0.0 74.5 jit_solution(7929495501473209919)
XLA Ops:
  0.0 1.2 %shard_map.29 = f32[2,192,384]{2,1,0:T(8,128)S(1)} custom-call(f32[2,2,192,384]{3,2,1,0:T(8,128)} %bitcast.1), custom_call_target="tpu_custom_call" | custom-call | tf_op jit(solution)/shard_map/pallas_call | solution.py:336
  1.7 1.1 %shard_map.28.mine_ref = f32[2,192,384]{2,1,0:T(8,128)S(1)} custom-call(f32[2,2,192,384]{3,2,1,0:T(8,128)} %bitcast.2), custom_call_target="tpu_custom_call" | custom-call | tf_op jit(solution)/shard_map/pallas_call | solution.py:336
  3.4 0.8 %shard_map.30 = (f32[384,384]{1,0:T(8,128)S(1)}, f32[128,384]{1,0:T(8,128)S(1)}, f32[128,384]{1,0:T(8,128)S(1)}, f32[128,384]{1,0:T(8,128)S(1)}) custom-call(f32[2,192,384]{2,1,0:T(8,128)S(1)} %shard_map.28.mine_ref, f32[2,192,384]{2,1,0:T(8,128)S(1)} %collective-permute-done.got_ref), custom_call_target="tpu_custom_call" | custom-call | tf_op jit(solution)/shard_map/pallas_call | solution.py:115
  4.2 2.4 %shard_map.31 = (f32[384,384]{1,0:T(8,128)S(1)}, f32[384,384]{1,0:T(8,128)S(1)}, f32[384,384]{1,0:T(8,128)S(1)}, f32[2,256,384]{2,1,0:T(8,128)S(1)}, f32[2,96,38...) custom-call(f32[384,384]{1,0:T(8,128)S(1)} %get-tuple-element.29.r_0_, ...), custom_call_target="tpu_custom_call" | custom-call | tf_op jit(solution)/shard_map/pallas_call | solution.py:115
  6.6 0.7 collective-permute-start.10
  7.3 5.4 %collective-permute-start.2 = (f32[128,384]{1,0:T(8,128)S(1)}, f32[128,384]{1,0:T(8,128)S(1)}, u32[]{:S(2)}, u32[]{:S(2)}) collective-permute-start(f32[128,384]{1,0:T(8,128)S(1)} %get-tuple-element.30.r_1_), channel_id=1, source_target_pairs={{0,4},{1,5},{2,6},{3,7},{16,20},{17,21},{18,22},{19,23}} | collective-permute-start | bytes 589832 | tf_op jit(solution)/shard_map/ppermute | solution.py:353
  12.7 1.3 %collective-permute-start.3 = (f32[128,384]{1,0:T(8,128)S(1)}, f32[128,384]{1,0:T(8,128)S(1)}, u32[]{:S(2)}, u32[]{:S(2)}) collective-permute-start(f32[128,384]{1,0:T(8,128)S(1)} %get-tuple-element.31.r_2_), channel_id=1, source_target_pairs={{0,4},{1,5},{2,6},{3,7},{16,20},{17,21},{18,22},{19,23}} | collective-permute-start | bytes 589832 | tf_op jit(solution)/shard_map/ppermute | solution.py:353
  14.0 1.3 %collective-permute-start.1 = (f32[1,96,384]{2,1,0:T(8,128)S(1)}, f32[1,96,384]{2,1,0:T(8,128)S(1)}, u32[]{:S(2)}, u32[]{:S(2)}) collective-permute-start(f32[1,96,384]{2,1,0:T(8,128)S(1)} %get-tuple-element.34), channel_id=1, source_target_pairs={{0,4},{1,5},{2,6},{3,7},{16,20},{17,21},{18,22},{19,23}} | collective-permute-start | bytes 442376 | tf_op jit(solution)/shard_map/ppermute | solution.py:353
  15.3 1.3 %collective-permute-start.4 = (f32[128,384]{1,0:T(8,128)S(1)}, f32[128,384]{1,0:T(8,128)S(1)}, u32[]{:S(2)}, u32[]{:S(2)}) collective-permute-start(f32[128,384]{1,0:T(8,128)S(1)} %get-tuple-element.32.r_3_), channel_id=1, source_target_pairs={{0,4},{1,5},{2,6},{3,7},{16,20},{17,21},{18,22},{19,23}} | collective-permute-start | bytes 589832 | tf_op jit(solution)/shard_map/ppermute | solution.py:353
  16.6 1.3 %collective-permute-done.2.r_3_.r_0_ = f32[128,384]{1,0:T(8,128)S(1)} collective-permute-done((f32[128,384]{1,0:T(8,128)S(1)}, f32[128,384]{1,0:T(8,128)S(1)}, u32[]{:S(2)}, u32[]{:S(2)}) %collective-permute-start.2) | collective-permute-done | bytes 196640 | tf_op jit(solution)/shard_map/ppermute | solution.py:353
  17.9 1.3 %collective-permute-start.15 = (f32[1,96,384]{2,1,0:T(8,128)S(1)}, f32[1,96,384]{2,1,0:T(8,128)S(1)}, u32[]{:S(2)}, u32[]{:S(2)}) collective-permute-start(f32[1,96,384]{2,1,0:T(8,128)S(1)} %get-tuple-element.43), channel_id=1, source_target_pairs={{0,8},{1,9},{2,10},{3,11},{16,24},{17,25},{18,26},{19,27}} | collective-permute-start | bytes 442376 | tf_op jit(solution)/shard_map/ppermute | solution.py:353
  19.3 6.1 %collective-permute-done.1.r_1_ = f32[1,96,384]{2,1,0:T(8,128)S(1)} collective-permute-done((f32[1,96,384]{2,1,0:T(8,128)S(1)}, f32[1,96,384]{2,1,0:T(8,128)S(1)}, u32[]{:S(2)}, u32[]{:S(2)}) %collective-permute-start.1) | collective-permute-done | bytes 147488 | tf_op jit(solution)/shard_map/ppermute | solution.py:353
  26.0 1.3 %collective-permute-start.16 = (f32[1,96,384]{2,1,0:T(8,128)S(1)}, f32[1,96,384]{2,1,0:T(8,128)S(1)}, u32[]{:S(2)}, u32[]{:S(2)}) collective-permute-start(f32[1,96,384]{2,1,0:T(8,128)S(1)} %get-tuple-element.44), channel_id=1, source_target_pairs={{0,12},{1,13},{2,14},{3,15},{16,28},{17,29},{18,30},{19,31}} | collective-permute-start | bytes 442376 | tf_op jit(solution)/shard_map/ppermute | solution.py:353
  27.3 2.2 %collective-permute-done.4.r_5_.r_0_ = f32[128,384]{1,0:T(8,128)S(1)} collective-permute-done((f32[128,384]{1,0:T(8,128)S(1)}, f32[128,384]{1,0:T(8,128)S(1)}, u32[]{:S(2)}, u32[]{:S(2)}) %collective-permute-start.4) | collective-permute-done | bytes 196640 | tf_op jit(solution)/shard_map/ppermute | solution.py:353
  29.5 0.7 collective-permute-start.8
  30.2 2.5 %collective-permute-done.15.r_0_ = f32[1,96,384]{2,1,0:T(8,128)S(1)} collective-permute-done((f32[1,96,384]{2,1,0:T(8,128)S(1)}, f32[1,96,384]{2,1,0:T(8,128)S(1)}, u32[]{:S(2)}, u32[]{:S(2)}) %collective-permute-start.15) | collective-permute-done | bytes 147488 | tf_op jit(solution)/shard_map/ppermute | solution.py:353
  32.7 0.7 collective-permute-start.9
  33.4 1.6 %collective-permute-done.16.r_1_ = f32[1,96,384]{2,1,0:T(8,128)S(1)} collective-permute-done((f32[1,96,384]{2,1,0:T(8,128)S(1)}, f32[1,96,384]{2,1,0:T(8,128)S(1)}, u32[]{:S(2)}, u32[]{:S(2)}) %collective-permute-start.16) | collective-permute-done | bytes 147488 | tf_op jit(solution)/shard_map/ppermute | solution.py:353
  35.1 0.7 collective-permute-start.6
  35.8 1.3 %collective-permute-start.5 = (f32[2,96,384]{2,1,0:T(8,128)S(1)}, f32[2,96,384]{2,1,0:T(8,128)S(1)}, u32[]{:S(2)}, u32[]{:S(2)}) collective-permute-start(f32[2,96,384]{2,1,0:T(8,128)S(1)} %shard_map.32), channel_id=1, source_target_pairs={{4,0},{5,1},{6,2},{7,3},{20,16},{21,17},{22,18},{23,19}} | collective-permute-start | bytes 884744 | tf_op jit(solution)/shard_map/ppermute | solution.py:353
  37.1 0.7 collective-permute-start.11
  37.8 0.7 collective-permute-start.12
  38.5 0.7 collective-permute-start.13
  39.5 0.7 collective-permute-start.17
  40.2 10.3 %collective-permute-done.5.r_2_ = f32[2,96,384]{2,1,0:T(8,128)S(1)} collective-permute-done((f32[2,96,384]{2,1,0:T(8,128)S(1)}, f32[2,96,384]{2,1,0:T(8,128)S(1)}, u32[]{:S(2)}, u32[]{:S(2)}) %collective-permute-start.5) | collective-permute-done | bytes 294944 | tf_op jit(solution)/shard_map/ppermute | solution.py:353
  50.5 0.7 collective-permute-start.19
  51.1 1.3 %collective-permute-start.18 = (f32[2,96,384]{2,1,0:T(8,128)S(1)}, f32[2,96,384]{2,1,0:T(8,128)S(1)}, u32[]{:S(2)}, u32[]{:S(2)}) collective-permute-start(f32[2,96,384]{2,1,0:T(8,128)S(1)} %get-tuple-element.46), channel_id=1, source_target_pairs={{4,0},{5,1},{6,2},{7,3},{20,16},{21,17},{22,18},{23,19}} | collective-permute-start | bytes 884744 | tf_op jit(solution)/shard_map/ppermute | solution.py:353
  52.4 1.3 %collective-permute-start.20 = (f32[2,96,384]{2,1,0:T(8,128)S(1)}, f32[2,96,384]{2,1,0:T(8,128)S(1)}, u32[]{:S(2)}, u32[]{:S(2)}) collective-permute-start(f32[2,96,384]{2,1,0:T(8,128)S(1)} %get-tuple-element.48), channel_id=1, source_target_pairs={{8,0},{9,1},{10,2},{11,3},{24,16},{25,17},{26,18},{27,19}} | collective-permute-start | bytes 884744 | tf_op jit(solution)/shard_map/ppermute | solution.py:353
  53.8 0.7 collective-permute-start.21
  54.8 16.2 %collective-permute-done.18.r_4_ = f32[2,96,384]{2,1,0:T(8,128)S(1)} collective-permute-done((f32[2,96,384]{2,1,0:T(8,128)S(1)}, f32[2,96,384]{2,1,0:T(8,128)S(1)}, u32[]{:S(2)}, u32[]{:S(2)}) %collective-permute-start.18) | collective-permute-done | bytes 294944 | tf_op jit(solution)/shard_map/ppermute | solution.py:353
  71.2 1.4 %spectrum.2.r_2_ = f32[2,2,8,96,192]{4,3,2,1,0:T(8,128)} custom-call(f32[4,96,192]{2,1,0:T(8,128)S(1)} %get-tuple-element.51.r_0_, f32[4,96,192]{2,1,0:T(8,128)S(1)} %get-tuple-element.52.r_1_), custom_call_target="tpu_custom_call" | custom-call | tf_op jit(solution)/shard_map/spectrum/pallas_call | solution.py:419
  73.0 1.4 %spectrum.3 = f32[2,2,8,96,192]{4,3,2,1,0:T(8,128)} custom-call(f32[4,96,192]{2,1,0:T(8,128)S(1)} %collective-permute-done.14.r_0_, f32[4,96,192]{2,1,0:T(8,128)S(1)} %collective-permute-done.22.r_1_, f32[2,2,8,96,192]{4,3,2,1,0:T(8,128)} %spectrum.2.r_2_), custom_call_target="tpu_custom_call", output_to_operand_aliasing={{}: (2, {})} | custom-call | tf_op jit(solution)/shard_map/spectrum/pallas_call | solution.py:419
  (37 shorter events, 3.0 us)
Async XLA Ops:
  0.0 4.2 %copy-start = (f32[2,384,384]{2,1,0:T(8,128)S(1)}, f32[2,384,384]{2,1,0:T(8,128)}, u32[]{:S(2)}) copy-start(f32[2,384,384]{2,1,0:T(8,128)} %r_4_.1) | copy-start | bytes 3538948
  1.2 2.2 %collective-permute-start = (f32[2,192,384]{2,1,0:T(8,128)S(1)}, f32[2,192,384]{2,1,0:T(8,128)S(1)}, u32[]{:S(2)}, u32[]{:S(2)}) collective-permute-start(f32[2,192,384]{2,1,0:T(8,128)S(1)} %shard_map.29), channel_id=1, source_target_pairs={{0,1},{1,0},{2,3},{3,2},{4,5},{5,4},{6,7},{7,6},{8,9},{9,8},{10,11... | collective-permute-start | bytes 1769480 | tf_op jit(solution)/shard_map/ppermute | solution.py:345
  6.6 32.0 %collective-permute-start.10 = (f32[2,256,384]{2,1,0:T(8,128)S(1)}, f32[2,256,384]{2,1,0:T(8,128)S(1)}, u32[]{:S(2)}, u32[]{:S(2)}) collective-permute-start(f32[2,256,384]{2,1,0:T(8,128)S(1)} %get-tuple-element.40), channel_id=1, source_target_pairs={{8,4},{12,8},{9,5},{13,9},{10,6},{14,10},{11,7},{15,11},{24,20},{2... | collective-permute-start | bytes 2359304 | tf_op jit(solution)/shard_map/ppermute | solution.py:353
  7.3 10.7 %collective-permute-start.2 = (f32[128,384]{1,0:T(8,128)S(1)}, f32[128,384]{1,0:T(8,128)S(1)}, u32[]{:S(2)}, u32[]{:S(2)}) collective-permute-start(f32[128,384]{1,0:T(8,128)S(1)} %get-tuple-element.30.r_1_), channel_id=1, source_target_pairs={{0,4},{1,5},{2,6},{3,7},{16,20},{17,21},{18,22},{19,23}} | collective-permute-start | bytes 589832 | tf_op jit(solution)/shard_map/ppermute | solution.py:353
  12.7 13.3 %collective-permute-start.3 = (f32[128,384]{1,0:T(8,128)S(1)}, f32[128,384]{1,0:T(8,128)S(1)}, u32[]{:S(2)}, u32[]{:S(2)}) collective-permute-start(f32[128,384]{1,0:T(8,128)S(1)} %get-tuple-element.31.r_2_), channel_id=1, source_target_pairs={{0,4},{1,5},{2,6},{3,7},{16,20},{17,21},{18,22},{19,23}} | collective-permute-start | bytes 589832 | tf_op jit(solution)/shard_map/ppermute | solution.py:353
  14.0 11.3 %collective-permute-start.1 = (f32[1,96,384]{2,1,0:T(8,128)S(1)}, f32[1,96,384]{2,1,0:T(8,128)S(1)}, u32[]{:S(2)}, u32[]{:S(2)}) collective-permute-start(f32[1,96,384]{2,1,0:T(8,128)S(1)} %get-tuple-element.34), channel_id=1, source_target_pairs={{0,4},{1,5},{2,6},{3,7},{16,20},{17,21},{18,22},{19,23}} | collective-permute-start | bytes 442376 | tf_op jit(solution)/shard_map/ppermute | solution.py:353
  15.3 14.2 %collective-permute-start.4 = (f32[128,384]{1,0:T(8,128)S(1)}, f32[128,384]{1,0:T(8,128)S(1)}, u32[]{:S(2)}, u32[]{:S(2)}) collective-permute-start(f32[128,384]{1,0:T(8,128)S(1)} %get-tuple-element.32.r_3_), channel_id=1, source_target_pairs={{0,4},{1,5},{2,6},{3,7},{16,20},{17,21},{18,22},{19,23}} | collective-permute-start | bytes 589832 | tf_op jit(solution)/shard_map/ppermute | solution.py:353
  17.9 14.8 %collective-permute-start.15 = (f32[1,96,384]{2,1,0:T(8,128)S(1)}, f32[1,96,384]{2,1,0:T(8,128)S(1)}, u32[]{:S(2)}, u32[]{:S(2)}) collective-permute-start(f32[1,96,384]{2,1,0:T(8,128)S(1)} %get-tuple-element.43), channel_id=1, source_target_pairs={{0,8},{1,9},{2,10},{3,11},{16,24},{17,25},{18,26},{19,27}} | collective-permute-start | bytes 442376 | tf_op jit(solution)/shard_map/ppermute | solution.py:353
  25.3 10.5 %collective-permute-start.7 = (f32[128,384]{1,0:T(8,128)S(1)}, f32[128,384]{1,0:T(8,128)S(1)}, u32[]{:S(2)}, u32[]{:S(2)}) collective-permute-start(f32[128,384]{1,0:T(8,128)S(1)} %shard_map.34.r_1_), channel_id=1, source_target_pairs={{4,8},{5,9},{6,10},{7,11},{20,24},{21,25},{22,26},{23,27}} | collective-permute-start | bytes 589832 | tf_op jit(solution)/shard_map/ppermute | solution.py:353
  26.0 9.1 %collective-permute-start.16 = (f32[1,96,384]{2,1,0:T(8,128)S(1)}, f32[1,96,384]{2,1,0:T(8,128)S(1)}, u32[]{:S(2)}, u32[]{:S(2)}) collective-permute-start(f32[1,96,384]{2,1,0:T(8,128)S(1)} %get-tuple-element.44), channel_id=1, source_target_pairs={{0,12},{1,13},{2,14},{3,15},{16,28},{17,29},{18,30},{19,31}} | collective-permute-start | bytes 442376 | tf_op jit(solution)/shard_map/ppermute | solution.py:353
  29.5 7.6 %collective-permute-start.8 = (f32[128,384]{1,0:T(8,128)S(1)}, f32[128,384]{1,0:T(8,128)S(1)}, u32[]{:S(2)}, u32[]{:S(2)}) collective-permute-start(f32[128,384]{1,0:T(8,128)S(1)} %shard_map.35.r_2_), channel_id=1, source_target_pairs={{4,8},{5,9},{6,10},{7,11},{20,24},{21,25},{22,26},{23,27}} | collective-permute-start | bytes 589832 | tf_op jit(solution)/shard_map/ppermute | solution.py:353
  32.7 5.1 %collective-permute-start.9 = (f32[128,384]{1,0:T(8,128)S(1)}, f32[128,384]{1,0:T(8,128)S(1)}, u32[]{:S(2)}, u32[]{:S(2)}) collective-permute-start(f32[128,384]{1,0:T(8,128)S(1)} %shard_map.36.r_3_), channel_id=1, source_target_pairs={{4,8},{5,9},{6,10},{7,11},{20,24},{21,25},{22,26},{23,27}} | collective-permute-start | bytes 589832 | tf_op jit(solution)/shard_map/ppermute | solution.py:353
  35.1 4.4 %collective-permute-start.6 = (f32[2,96,384]{2,1,0:T(8,128)S(1)}, f32[2,96,384]{2,1,0:T(8,128)S(1)}, u32[]{:S(2)}, u32[]{:S(2)}) collective-permute-start(f32[2,96,384]{2,1,0:T(8,128)S(1)} %get-tuple-element.39), channel_id=1, source_target_pairs={{4,12},{5,13},{6,14},{7,15},{20,28},{21,29},{22,30},{23,31}} | collective-permute-start | bytes 884744 | tf_op jit(solution)/shard_map/ppermute | solution.py:353
  35.8 14.7 %collective-permute-start.5 = (f32[2,96,384]{2,1,0:T(8,128)S(1)}, f32[2,96,384]{2,1,0:T(8,128)S(1)}, u32[]{:S(2)}, u32[]{:S(2)}) collective-permute-start(f32[2,96,384]{2,1,0:T(8,128)S(1)} %shard_map.32), channel_id=1, source_target_pairs={{4,0},{5,1},{6,2},{7,3},{20,16},{21,17},{22,18},{23,19}} | collective-permute-start | bytes 884744 | tf_op jit(solution)/shard_map/ppermute | solution.py:353
  37.1 14.0 %collective-permute-start.11 = (f32[128,384]{1,0:T(8,128)S(1)}, f32[128,384]{1,0:T(8,128)S(1)}, u32[]{:S(2)}, u32[]{:S(2)}) collective-permute-start(f32[128,384]{1,0:T(8,128)S(1)} %shard_map.38.r_1_), channel_id=1, source_target_pairs={{8,12},{9,13},{10,14},{11,15},{24,28},{25,29},{26,30},{27,31}} | collective-permute-start | bytes 589832 | tf_op jit(solution)/shard_map/ppermute | solution.py:353
  37.8 14.6 %collective-permute-start.12 = (f32[128,384]{1,0:T(8,128)S(1)}, f32[128,384]{1,0:T(8,128)S(1)}, u32[]{:S(2)}, u32[]{:S(2)}) collective-permute-start(f32[128,384]{1,0:T(8,128)S(1)} %shard_map.39.r_2_), channel_id=1, source_target_pairs={{8,12},{9,13},{10,14},{11,15},{24,28},{25,29},{26,30},{27,31}} | collective-permute-start | bytes 589832 | tf_op jit(solution)/shard_map/ppermute | solution.py:353
  38.5 15.2 %collective-permute-start.13 = (f32[128,384]{1,0:T(8,128)S(1)}, f32[128,384]{1,0:T(8,128)S(1)}, u32[]{:S(2)}, u32[]{:S(2)}) collective-permute-start(f32[128,384]{1,0:T(8,128)S(1)} %shard_map.40.r_3_), channel_id=1, source_target_pairs={{8,12},{9,13},{10,14},{11,15},{24,28},{25,29},{26,30},{27,31}} | collective-permute-start | bytes 589832 | tf_op jit(solution)/shard_map/ppermute | solution.py:353
  39.5 15.2 %collective-permute-start.17 = (f32[2,96,384]{2,1,0:T(8,128)S(1)}, f32[2,96,384]{2,1,0:T(8,128)S(1)}, u32[]{:S(2)}, u32[]{:S(2)}) collective-permute-start(f32[2,96,384]{2,1,0:T(8,128)S(1)} %get-tuple-element.45), channel_id=1, source_target_pairs={{4,8},{5,9},{6,10},{7,11},{20,24},{21,25},{22,26},{23,27}} | collective-permute-start | bytes 884744 | tf_op jit(solution)/shard_map/ppermute | solution.py:353
  50.5 4.3 %collective-permute-start.19 = (f32[2,96,384]{2,1,0:T(8,128)S(1)}, f32[2,96,384]{2,1,0:T(8,128)S(1)}, u32[]{:S(2)}, u32[]{:S(2)}) collective-permute-start(f32[2,96,384]{2,1,0:T(8,128)S(1)} %shard_map.45), channel_id=1, source_target_pairs={{8,12},{9,13},{10,14},{11,15},{24,28},{25,29},{26,30},{27,31}} | collective-permute-start | bytes 884744 | tf_op jit(solution)/shard_map/ppermute | solution.py:353
  51.1 19.8 %collective-permute-start.18 = (f32[2,96,384]{2,1,0:T(8,128)S(1)}, f32[2,96,384]{2,1,0:T(8,128)S(1)}, u32[]{:S(2)}, u32[]{:S(2)}) collective-permute-start(f32[2,96,384]{2,1,0:T(8,128)S(1)} %get-tuple-element.46), channel_id=1, source_target_pairs={{4,0},{5,1},{6,2},{7,3},{20,16},{21,17},{22,18},{23,19}} | collective-permute-start | bytes 884744 | tf_op jit(solution)/shard_map/ppermute | solution.py:353
  52.4 18.5 %collective-permute-start.20 = (f32[2,96,384]{2,1,0:T(8,128)S(1)}, f32[2,96,384]{2,1,0:T(8,128)S(1)}, u32[]{:S(2)}, u32[]{:S(2)}) collective-permute-start(f32[2,96,384]{2,1,0:T(8,128)S(1)} %get-tuple-element.48), channel_id=1, source_target_pairs={{8,0},{9,1},{10,2},{11,3},{24,16},{25,17},{26,18},{27,19}} | collective-permute-start | bytes 884744 | tf_op jit(solution)/shard_map/ppermute | solution.py:353
  53.8 17.2 %collective-permute-start.21 = (f32[2,96,384]{2,1,0:T(8,128)S(1)}, f32[2,96,384]{2,1,0:T(8,128)S(1)}, u32[]{:S(2)}, u32[]{:S(2)}) collective-permute-start(f32[2,96,384]{2,1,0:T(8,128)S(1)} %get-tuple-element.49), channel_id=1, source_target_pairs={{8,4},{9,5},{10,6},{11,7},{24,20},{25,21},{26,22},{27,23}} | collective-permute-start | bytes 884744 | tf_op jit(solution)/shard_map/ppermute | solution.py:353
  54.7 18.0 %collective-permute-start.14 = (f32[4,96,192]{2,1,0:T(8,128)S(1)}, f32[4,96,192]{2,1,0:T(8,128)S(1)}, u32[]{:S(2)}, u32[]{:S(2)}) collective-permute-start(f32[4,96,192]{2,1,0:T(8,128)S(1)} %get-tuple-element.42), channel_id=1, source_target_pairs={{0,1},{1,0},{2,3},{3,2},{4,5},{5,4},{6,7},{7,6},{8,9},{9,8},{10,11... | collective-permute-start | bytes 884744 | tf_op jit(solution)/shard_map/ppermute | solution.py:414
  71.2 1.8 %collective-permute-start.22 = (f32[4,96,192]{2,1,0:T(8,128)S(1)}, f32[4,96,192]{2,1,0:T(8,128)S(1)}, u32[]{:S(2)}, u32[]{:S(2)}) collective-permute-start(f32[4,96,192]{2,1,0:T(8,128)S(1)} %get-tuple-element.50), channel_id=1, source_target_pairs={{0,1},{1,0},{2,3},{3,2},{4,5},{5,4},{6,7},{7,6},{8,9},{9,8},{10,11... | collective-permute-start | bytes 884744 | tf_op jit(solution)/shard_map/ppermute | solution.py:414

commit v4 on v3

--- a/solution.py
+++ b/solution.py
@@ -8,7 +8,7 @@
 from jax.sharding import PartitionSpec as P
 
 
-CHUNKS = 3
+CHUNKS = 4
 GRANT = pltpu.CompilerParams(vmem_limit_bytes=20 * 2**20)
 
 
@@ -122,11 +122,20 @@
     )(*near)
 
 
-def pick_kernel(own, in_ref, out_ref, sem):
+def pick_kernel(own, in_ref, out_ref, sems):
     core = lax.axis_index("col")
-    copy = pltpu.make_async_copy(in_ref.at[core if own else 1 - core], out_ref, sem)
-    copy.start()
-    copy.wait()
+    source = in_ref.at[core if own else 1 - core]
+    slices, part, _ = out_ref.shape
+    copies = []
+    for s in range(slices):
+        for h in range(2):
+            span = pl.ds(h * (part // 2), part // 2)
+            copies.append(
+                pltpu.make_async_copy(source.at[s, span, :], out_ref.at[s, span, :], sems.at[2 * s + h])
+            )
+            copies[-1].start()
+    for copy in copies:
+        copy.wait()
 
 
 def start_kernel(mine_ref, got_ref, a0_ref, *refs):
@@ -338,7 +347,7 @@
             out_shape=pltpu.VMEM((slices, part, order), jnp.float32),
             in_specs=[pl.BlockSpec(memory_space=pltpu.HBM)],
             out_specs=VMEM,
-            scratch_shapes=[pltpu.SemaphoreType.DMA],
+            scratch_shapes=[pltpu.SemaphoreType.DMA((2 * slices,))],
             compiler_params=GRANT,
         )(pltpu.with_memory_space_constraint(flipped, pltpu.HBM))
 

time: 75.7 us -> 81.2 us (1.073)
  the two profiles are of different devices: /device:TPU:0 before, /device:TPU:11 now
where the time goes in v4:
time: 81.2 us; the launch traced here: 80.8 us
  starting transfers between devices  38.6 us (48%)
  waiting for transfers between devices  26.2 us (32%)
  Pallas kernels  15.3 us (19%)
    ppermute x23, starting transfers between devices, along(): return lax.ppermute(x, 'tm', [hop] if isinstance(hop, tuple) else hop)  35 us
    ppermute x23, waiting for transfers between devices, along(): return lax.ppermute(x, 'tm', [hop] if isinstance(hop, tuple) else hop)  25.8 us
    pallas_call x19, Pallas kernels, local_call(): pl.pallas_call(kernel, out_shape=[pltpu.VMEM(s, jnp.float32) for s in out...  10.1 us
    pallas_call x2, Pallas kernels, spectrum(): pl.pallas_call(lambda *r: spectrum_kernel(own, tables, *r), out_shape=jax...  2.83 us
    ppermute x2, starting transfers between devices, paired_body(): taken.append(lax.ppermute(give, 'col', swap))  2.82 us
    pallas_call x2, Pallas kernels, pick(): pl.pallas_call(lambda *r: pick_kernel(own, *r), out_shape=pltpu.VMEM((sli...  2.41 us
  transfers between devices with their start and end apart: 26, of which 10 were waited for; matrix products, arithmetic and copies ran while one was open for 0% of the time, Pallas kernels for 12%

profile of v4, /device:TPU:11, one launch (start us, length us, event | category | flops | bytes accessed | tf_op | source)
XLA Modules:
  0.0 80.8 jit_solution(18366240226730668164)
XLA Ops:
  0.0 1.3 %shard_map.29 = f32[2,192,384]{2,1,0:T(8,128)S(1)} custom-call(f32[2,2,192,384]{3,2,1,0:T(8,128)} %bitcast.1), custom_call_target="tpu_custom_call" | custom-call | tf_op jit(solution)/shard_map/pallas_call | solution.py:345
  4.5 2.3 %shard_map.31 = (f32[384,384]{1,0:T(8,128)S(1)}, f32[384,384]{1,0:T(8,128)S(1)}, f32[384,384]{1,0:T(8,128)S(1)}, f32[2,256,384]{2,1,0:T(8,128)S(1)}, f32[2,96,38...) custom-call(f32[384,384]{1,0:T(8,128)S(1)} %get-tuple-element.30.r_0_, ...), custom_call_target="tpu_custom_call" | custom-call | tf_op jit(solution)/shard_map/pallas_call | solution.py:115
  6.8 1.3 %collective-permute-start.12 = (f32[2,256,384]{2,1,0:T(8,128)S(1)}, f32[2,256,384]{2,1,0:T(8,128)S(1)}, u32[]{:S(2)}, u32[]{:S(2)}) collective-permute-start(f32[2,256,384]{2,1,0:T(8,128)S(1)} %get-tuple-element.42), channel_id=1, source_target_pairs={{8,4},{12,8},{9,5},{13,9},{10,6},{14,10},{11,7},{15,11},{24,20},{2... | collective-permute-start | bytes 2359304 | tf_op jit(solution)/shard_map/ppermute | solution.py:362
  8.1 1.3 %collective-permute-start.2 = (f32[96,384]{1,0:T(8,128)S(1)}, f32[96,384]{1,0:T(8,128)S(1)}, u32[]{:S(2)}, u32[]{:S(2)}) collective-permute-start(f32[96,384]{1,0:T(8,128)S(1)} %get-tuple-element.31.r_1_), channel_id=1, source_target_pairs={{0,4},{1,5},{2,6},{3,7},{16,20},{17,21},{18,22},{19,23}} | collective-permute-start | bytes 442376 | tf_op jit(solution)/shard_map/ppermute | solution.py:362
  9.4 1.3 %collective-permute-start.3 = (f32[96,384]{1,0:T(8,128)S(1)}, f32[96,384]{1,0:T(8,128)S(1)}, u32[]{:S(2)}, u32[]{:S(2)}) collective-permute-start(f32[96,384]{1,0:T(8,128)S(1)} %get-tuple-element.32.r_2_), channel_id=1, source_target_pairs={{0,4},{1,5},{2,6},{3,7},{16,20},{17,21},{18,22},{19,23}} | collective-permute-start | bytes 442376 | tf_op jit(solution)/shard_map/ppermute | solution.py:362
  10.7 1.3 %collective-permute-start.4 = (f32[96,384]{1,0:T(8,128)S(1)}, f32[96,384]{1,0:T(8,128)S(1)}, u32[]{:S(2)}, u32[]{:S(2)}) collective-permute-start(f32[96,384]{1,0:T(8,128)S(1)} %get-tuple-element.33.r_3_), channel_id=1, source_target_pairs={{0,4},{1,5},{2,6},{3,7},{16,20},{17,21},{18,22},{19,23}} | collective-permute-start | bytes 442376 | tf_op jit(solution)/shard_map/ppermute | solution.py:362
  12.0 1.3 %collective-permute-start.5 = (f32[96,384]{1,0:T(8,128)S(1)}, f32[96,384]{1,0:T(8,128)S(1)}, u32[]{:S(2)}, u32[]{:S(2)}) collective-permute-start(f32[96,384]{1,0:T(8,128)S(1)} %get-tuple-element.34.r_4_), channel_id=1, source_target_pairs={{0,4},{1,5},{2,6},{3,7},{16,20},{17,21},{18,22},{19,23}} | collective-permute-start | bytes 442376 | tf_op jit(solution)/shard_map/ppermute | solution.py:362
  13.3 1.7 %collective-permute-done.2.r_3_.r_0_ = f32[96,384]{1,0:T(8,128)S(1)} collective-permute-done((f32[96,384]{1,0:T(8,128)S(1)}, f32[96,384]{1,0:T(8,128)S(1)}, u32[]{:S(2)}, u32[]{:S(2)}) %collective-permute-start.2) | collective-permute-done | bytes 147488 | tf_op jit(solution)/shard_map/ppermute | solution.py:362
  15.1 1.3 %collective-permute-start.1 = (f32[1,96,384]{2,1,0:T(8,128)S(1)}, f32[1,96,384]{2,1,0:T(8,128)S(1)}, u32[]{:S(2)}, u32[]{:S(2)}) collective-permute-start(f32[1,96,384]{2,1,0:T(8,128)S(1)} %get-tuple-element.36), channel_id=1, source_target_pairs={{0,4},{1,5},{2,6},{3,7},{16,20},{17,21},{18,22},{19,23}} | collective-permute-start | bytes 442376 | tf_op jit(solution)/shard_map/ppermute | solution.py:362
  16.7 1.6 %collective-permute-done.3.r_4_.r_0_ = f32[96,384]{1,0:T(8,128)S(1)} collective-permute-done((f32[96,384]{1,0:T(8,128)S(1)}, f32[96,384]{1,0:T(8,128)S(1)}, u32[]{:S(2)}, u32[]{:S(2)}) %collective-permute-start.3) | collective-permute-done | bytes 147488 | tf_op jit(solution)/shard_map/ppermute | solution.py:362
  18.2 1.3 %collective-permute-start.8 = (f32[96,384]{1,0:T(8,128)S(1)}, f32[96,384]{1,0:T(8,128)S(1)}, u32[]{:S(2)}, u32[]{:S(2)}) collective-permute-start(f32[96,384]{1,0:T(8,128)S(1)} %shard_map.34.r_1_), channel_id=1, source_target_pairs={{4,8},{5,9},{6,10},{7,11},{20,24},{21,25},{22,26},{23,27}} | collective-permute-start | bytes 442376 | tf_op jit(solution)/shard_map/ppermute | solution.py:362
  19.5 1.9 %collective-permute-done.4.r_5_.r_0_ = f32[96,384]{1,0:T(8,128)S(1)} collective-permute-done((f32[96,384]{1,0:T(8,128)S(1)}, f32[96,384]{1,0:T(8,128)S(1)}, u32[]{:S(2)}, u32[]{:S(2)}) %collective-permute-start.4) | collective-permute-done | bytes 147488 | tf_op jit(solution)/shard_map/ppermute | solution.py:362
  22.1 2.5 %collective-permute-done.5.r_6_.r_0_ = f32[96,384]{1,0:T(8,128)S(1)} collective-permute-done((f32[96,384]{1,0:T(8,128)S(1)}, f32[96,384]{1,0:T(8,128)S(1)}, u32[]{:S(2)}, u32[]{:S(2)}) %collective-permute-start.5) | collective-permute-done | bytes 147488 | tf_op jit(solution)/shard_map/ppermute | solution.py:362
  25.5 2.2 %collective-permute-done.1.r_1_ = f32[1,96,384]{2,1,0:T(8,128)S(1)} collective-permute-done((f32[1,96,384]{2,1,0:T(8,128)S(1)}, f32[1,96,384]{2,1,0:T(8,128)S(1)}, u32[]{:S(2)}, u32[]{:S(2)}) %collective-permute-start.1) | collective-permute-done | bytes 147488 | tf_op jit(solution)/shard_map/ppermute | solution.py:362
  27.7 1.3 %collective-permute-start.9 = (f32[96,384]{1,0:T(8,128)S(1)}, f32[96,384]{1,0:T(8,128)S(1)}, u32[]{:S(2)}, u32[]{:S(2)}) collective-permute-start(f32[96,384]{1,0:T(8,128)S(1)} %shard_map.35.r_2_), channel_id=1, source_target_pairs={{4,8},{5,9},{6,10},{7,11},{20,24},{21,25},{22,26},{23,27}} | collective-permute-start | bytes 442376 | tf_op jit(solution)/shard_map/ppermute | solution.py:362
  29.3 1.3 %collective-permute-start.10 = (f32[96,384]{1,0:T(8,128)S(1)}, f32[96,384]{1,0:T(8,128)S(1)}, u32[]{:S(2)}, u32[]{:S(2)}) collective-permute-start(f32[96,384]{1,0:T(8,128)S(1)} %shard_map.36.r_3_), channel_id=1, source_target_pairs={{4,8},{5,9},{6,10},{7,11},{20,24},{21,25},{22,26},{23,27}} | collective-permute-start | bytes 442376 | tf_op jit(solution)/shard_map/ppermute | solution.py:362
  31.0 3.0 %collective-permute-start.11 = (f32[96,384]{1,0:T(8,128)S(1)}, f32[96,384]{1,0:T(8,128)S(1)}, u32[]{:S(2)}, u32[]{:S(2)}) collective-permute-start(f32[96,384]{1,0:T(8,128)S(1)} %shard_map.37.r_4_), channel_id=1, source_target_pairs={{4,8},{5,9},{6,10},{7,11},{20,24},{21,25},{22,26},{23,27}} | collective-permute-start | bytes 442376 | tf_op jit(solution)/shard_map/ppermute | solution.py:362
  34.6 2.3 %shard_map.33 = (f32[3,96,384]{2,1,0:T(8,128)S(1)}, f32[2,96,384]{2,1,0:T(8,128)S(1)}, f32[2,96,384]{2,1,0:T(8,128)S(1)}) custom-call(f32[384,384]{1,0:T(8,128)S(1)} %get-tuple-element.37.r_0_, f32[384,384]{1,0:T(8,128)S(1)} %get-tuple-element.38.r_1_, f32[384,384]{1,0:T(8,128)S(1)} %get-tuple-element.39.r_2_, ...), custom_call_target="tpu_custom_call" | custom-call | tf_op jit(solution)/shard_map/pallas_call | solution.py:115
  37.0 2.4 %collective-permute-start.7 = (f32[2,96,384]{2,1,0:T(8,128)S(1)}, f32[2,96,384]{2,1,0:T(8,128)S(1)}, u32[]{:S(2)}, u32[]{:S(2)}) collective-permute-start(f32[2,96,384]{2,1,0:T(8,128)S(1)} %get-tuple-element.41), channel_id=1, source_target_pairs={{4,12},{5,13},{6,14},{7,15},{20,28},{21,29},{22,30},{23,31}} | collective-permute-start | bytes 884744 | tf_op jit(solution)/shard_map/ppermute | solution.py:362
  39.4 1.2 %shard_map.32 = f32[2,96,384]{2,1,0:T(8,128)S(1)} custom-call(f32[384,384]{1,0:T(8,128)S(1)} %get-tuple-element.37.r_0_, f32[384,384]{1,0:T(8,128)S(1)} %get-tuple-element.38.r_1_, f32[384,384]{1,0:T(8,128)S(1)} %get-tuple-element.39.r_2_, f32[96,384]{1,0:T(8,128)S(1)} %collective-permute-done.2.r_3_.r_0_, f32[96,384]{1,0:T(8,128)S(1)} %collective-permute-done.3.r_4_.r_0_, ...), custom_call_target="tpu_custom_call" | custom-call | tf_op jit(solution)/shard_map/pallas_call | solution.py:115
  40.6 1.3 %collective-permute-start.6 = (f32[2,96,384]{2,1,0:T(8,128)S(1)}, f32[2,96,384]{2,1,0:T(8,128)S(1)}, u32[]{:S(2)}, u32[]{:S(2)}) collective-permute-start(f32[2,96,384]{2,1,0:T(8,128)S(1)} %shard_map.32), channel_id=1, source_target_pairs={{4,0},{5,1},{6,2},{7,3},{20,16},{21,17},{22,18},{23,19}} | collective-permute-start | bytes 884744 | tf_op jit(solution)/shard_map/ppermute | solution.py:362
  42.0 1.3 %collective-permute-done.11.r_6_.r_0_ = f32[96,384]{1,0:T(8,128)S(1)} collective-permute-done((f32[96,384]{1,0:T(8,128)S(1)}, f32[96,384]{1,0:T(8,128)S(1)}, u32[]{:S(2)}, u32[]{:S(2)}) %collective-permute-start.11) | collective-permute-done | bytes 147488 | tf_op jit(solution)/shard_map/ppermute | solution.py:362
  45.3 1.5 %shard_map.46 = (f32[2,96,384]{2,1,0:T(8,128)S(1)}, f32[2,96,384]{2,1,0:T(8,128)S(1)}) custom-call(f32[2,256,384]{2,1,0:T(8,128)S(1)} %collective-permute-done.12.r_0_, f32[96,384]{1,0:T(8,128)S(1)} %shard_map.34.r_1_, f32[96,384]{1,0:T(8,128)S(1)} %shard_map.35.r_2_, f32[96,384]{1,0:T(8,128)S(1)} %shard_map.36.r_3_, f32[96,384]{1,0:T(8,128)S(1)} %shard_map.37.r_4_), custom_call_target="tpu_custom_call" | custom-call | tf_op jit(solution)/shard_map/pallas_call | solution.py:115
  47.0 8.8 %collective-permute-start.20 = (f32[2,96,384]{2,1,0:T(8,128)S(1)}, f32[2,96,384]{2,1,0:T(8,128)S(1)}, u32[]{:S(2)}, u32[]{:S(2)}) collective-permute-start(f32[2,96,384]{2,1,0:T(8,128)S(1)} %get-tuple-element.47), channel_id=1, source_target_pairs={{4,8},{5,9},{6,10},{7,11},{20,24},{21,25},{22,26},{23,27}} | collective-permute-start | bytes 884744 | tf_op jit(solution)/shard_map/ppermute | solution.py:362
  56.5 1.3 %collective-permute-start.21 = (f32[2,96,384]{2,1,0:T(8,128)S(1)}, f32[2,96,384]{2,1,0:T(8,128)S(1)}, u32[]{:S(2)}, u32[]{:S(2)}) collective-permute-start(f32[2,96,384]{2,1,0:T(8,128)S(1)} %get-tuple-element.48), channel_id=1, source_target_pairs={{4,0},{5,1},{6,2},{7,3},{20,16},{21,17},{22,18},{23,19}} | collective-permute-start | bytes 884744 | tf_op jit(solution)/shard_map/ppermute | solution.py:362
  58.6 1.3 %collective-permute-start.24 = (f32[2,96,384]{2,1,0:T(8,128)S(1)}, f32[2,96,384]{2,1,0:T(8,128)S(1)}, u32[]{:S(2)}, u32[]{:S(2)}) collective-permute-start(f32[2,96,384]{2,1,0:T(8,128)S(1)} %get-tuple-element.51), channel_id=1, source_target_pairs={{8,4},{9,5},{10,6},{11,7},{24,20},{25,21},{26,22},{27,23}} | collective-permute-start | bytes 884744 | tf_op jit(solution)/shard_map/ppermute | solution.py:362
  60.1 1.5 %collective-permute-done.20.r_2_ = f32[2,96,384]{2,1,0:T(8,128)S(1)} collective-permute-done((f32[2,96,384]{2,1,0:T(8,128)S(1)}, f32[2,96,384]{2,1,0:T(8,128)S(1)}, u32[]{:S(2)}, u32[]{:S(2)}) %collective-permute-start.20) | collective-permute-done | bytes 294944 | tf_op jit(solution)/shard_map/ppermute | solution.py:362
  61.6 1.4 %collective-permute-start.17 = (f32[4,96,192]{2,1,0:T(8,128)S(1)}, f32[4,96,192]{2,1,0:T(8,128)S(1)}, u32[]{:S(2)}, u32[]{:S(2)}) collective-permute-start(f32[4,96,192]{2,1,0:T(8,128)S(1)} %get-tuple-element.44), channel_id=1, source_target_pairs={{0,1},{1,0},{2,3},{3,2},{4,5},{5,4},{6,7},{7,6},{8,9},{9,8},{10,11... | collective-permute-start | bytes 884744 | tf_op jit(solution)/shard_map/ppermute | solution.py:423
  63.6 12.5 %collective-permute-done.24.r_8_ = f32[2,96,384]{2,1,0:T(8,128)S(1)} collective-permute-done((f32[2,96,384]{2,1,0:T(8,128)S(1)}, f32[2,96,384]{2,1,0:T(8,128)S(1)}, u32[]{:S(2)}, u32[]{:S(2)}) %collective-permute-start.24) | collective-permute-done | bytes 294944 | tf_op jit(solution)/shard_map/ppermute | solution.py:362
  76.3 1.4 %collective-permute-start.25 = (f32[4,96,192]{2,1,0:T(8,128)S(1)}, f32[4,96,192]{2,1,0:T(8,128)S(1)}, u32[]{:S(2)}, u32[]{:S(2)}) collective-permute-start(f32[4,96,192]{2,1,0:T(8,128)S(1)} %get-tuple-element.52), channel_id=1, source_target_pairs={{0,1},{1,0},{2,3},{3,2},{4,5},{5,4},{6,7},{7,6},{8,9},{9,8},{10,11... | collective-permute-start | bytes 884744 | tf_op jit(solution)/shard_map/ppermute | solution.py:423
  77.8 1.4 %spectrum.2.r_2_ = f32[2,2,8,96,192]{4,3,2,1,0:T(8,128)} custom-call(f32[4,96,192]{2,1,0:T(8,128)S(1)} %get-tuple-element.53.r_0_, f32[4,96,192]{2,1,0:T(8,128)S(1)} %get-tuple-element.54.r_1_), custom_call_target="tpu_custom_call" | custom-call | tf_op jit(solution)/shard_map/spectrum/pallas_call | solution.py:428
  79.2 1.4 %spectrum.3 = f32[2,2,8,96,192]{4,3,2,1,0:T(8,128)} custom-call(f32[4,96,192]{2,1,0:T(8,128)S(1)} %collective-permute-done.17.r_0_, f32[4,96,192]{2,1,0:T(8,128)S(1)} %collective-permute-done.25.r_1_, f32[2,2,8,96,192]{4,3,2,1,0:T(8,128)} %spectrum.2.r_2_), custom_call_target="tpu_custom_call", output_to_operand_aliasing={{}: (2, {})} | custom-call | tf_op jit(solution)/shard_map/spectrum/pallas_call | solution.py:428
  (45 shorter events, 11.1 us)
Async XLA Ops:
  0.0 4.5 %copy-start = (f32[2,384,384]{2,1,0:T(8,128)S(1)}, f32[2,384,384]{2,1,0:T(8,128)}, u32[]{:S(2)}) copy-start(f32[2,384,384]{2,1,0:T(8,128)} %r_5_.1) | copy-start | bytes 3538948
  1.3 2.4 %collective-permute-start = (f32[2,192,384]{2,1,0:T(8,128)S(1)}, f32[2,192,384]{2,1,0:T(8,128)S(1)}, u32[]{:S(2)}, u32[]{:S(2)}) collective-permute-start(f32[2,192,384]{2,1,0:T(8,128)S(1)} %shard_map.29), channel_id=1, source_target_pairs={{0,1},{1,0},{2,3},{3,2},{4,5},{5,4},{6,7},{7,6},{8,9},{9,8},{10,11... | collective-permute-start | bytes 1769480 | tf_op jit(solution)/shard_map/ppermute | solution.py:354
  6.8 37.8 %collective-permute-start.12 = (f32[2,256,384]{2,1,0:T(8,128)S(1)}, f32[2,256,384]{2,1,0:T(8,128)S(1)}, u32[]{:S(2)}, u32[]{:S(2)}) collective-permute-start(f32[2,256,384]{2,1,0:T(8,128)S(1)} %get-tuple-element.42), channel_id=1, source_target_pairs={{8,4},{12,8},{9,5},{13,9},{10,6},{14,10},{11,7},{15,11},{24,20},{2... | collective-permute-start | bytes 2359304 | tf_op jit(solution)/shard_map/ppermute | solution.py:362
  8.1 6.9 %collective-permute-start.2 = (f32[96,384]{1,0:T(8,128)S(1)}, f32[96,384]{1,0:T(8,128)S(1)}, u32[]{:S(2)}, u32[]{:S(2)}) collective-permute-start(f32[96,384]{1,0:T(8,128)S(1)} %get-tuple-element.31.r_1_), channel_id=1, source_target_pairs={{0,4},{1,5},{2,6},{3,7},{16,20},{17,21},{18,22},{19,23}} | collective-permute-start | bytes 442376 | tf_op jit(solution)/shard_map/ppermute | solution.py:362
  9.4 8.8 %collective-permute-start.3 = (f32[96,384]{1,0:T(8,128)S(1)}, f32[96,384]{1,0:T(8,128)S(1)}, u32[]{:S(2)}, u32[]{:S(2)}) collective-permute-start(f32[96,384]{1,0:T(8,128)S(1)} %get-tuple-element.32.r_2_), channel_id=1, source_target_pairs={{0,4},{1,5},{2,6},{3,7},{16,20},{17,21},{18,22},{19,23}} | collective-permute-start | bytes 442376 | tf_op jit(solution)/shard_map/ppermute | solution.py:362
  10.7 10.6 %collective-permute-start.4 = (f32[96,384]{1,0:T(8,128)S(1)}, f32[96,384]{1,0:T(8,128)S(1)}, u32[]{:S(2)}, u32[]{:S(2)}) collective-permute-start(f32[96,384]{1,0:T(8,128)S(1)} %get-tuple-element.33.r_3_), channel_id=1, source_target_pairs={{0,4},{1,5},{2,6},{3,7},{16,20},{17,21},{18,22},{19,23}} | collective-permute-start | bytes 442376 | tf_op jit(solution)/shard_map/ppermute | solution.py:362
  12.0 12.5 %collective-permute-start.5 = (f32[96,384]{1,0:T(8,128)S(1)}, f32[96,384]{1,0:T(8,128)S(1)}, u32[]{:S(2)}, u32[]{:S(2)}) collective-permute-start(f32[96,384]{1,0:T(8,128)S(1)} %get-tuple-element.34.r_4_), channel_id=1, source_target_pairs={{0,4},{1,5},{2,6},{3,7},{16,20},{17,21},{18,22},{19,23}} | collective-permute-start | bytes 442376 | tf_op jit(solution)/shard_map/ppermute | solution.py:362
  15.1 12.6 %collective-permute-start.1 = (f32[1,96,384]{2,1,0:T(8,128)S(1)}, f32[1,96,384]{2,1,0:T(8,128)S(1)}, u32[]{:S(2)}, u32[]{:S(2)}) collective-permute-start(f32[1,96,384]{2,1,0:T(8,128)S(1)} %get-tuple-element.36), channel_id=1, source_target_pairs={{0,4},{1,5},{2,6},{3,7},{16,20},{17,21},{18,22},{19,23}} | collective-permute-start | bytes 442376 | tf_op jit(solution)/shard_map/ppermute | solution.py:362
  18.2 11.1 %collective-permute-start.8 = (f32[96,384]{1,0:T(8,128)S(1)}, f32[96,384]{1,0:T(8,128)S(1)}, u32[]{:S(2)}, u32[]{:S(2)}) collective-permute-start(f32[96,384]{1,0:T(8,128)S(1)} %shard_map.34.r_1_), channel_id=1, source_target_pairs={{4,8},{5,9},{6,10},{7,11},{20,24},{21,25},{22,26},{23,27}} | collective-permute-start | bytes 442376 | tf_op jit(solution)/shard_map/ppermute | solution.py:362
  21.4 9.6 %collective-permute-start.18 = (f32[1,96,384]{2,1,0:T(8,128)S(1)}, f32[1,96,384]{2,1,0:T(8,128)S(1)}, u32[]{:S(2)}, u32[]{:S(2)}) collective-permute-start(f32[1,96,384]{2,1,0:T(8,128)S(1)} %get-tuple-element.45), channel_id=1, source_target_pairs={{0,8},{1,9},{2,10},{3,11},{16,24},{17,25},{18,26},{19,27}} | collective-permute-start | bytes 442376 | tf_op jit(solution)/shard_map/ppermute | solution.py:362
  24.5 9.4 %collective-permute-start.19 = (f32[1,96,384]{2,1,0:T(8,128)S(1)}, f32[1,96,384]{2,1,0:T(8,128)S(1)}, u32[]{:S(2)}, u32[]{:S(2)}) collective-permute-start(f32[1,96,384]{2,1,0:T(8,128)S(1)} %get-tuple-element.46), channel_id=1, source_target_pairs={{0,12},{1,13},{2,14},{3,15},{16,28},{17,29},{18,30},{19,31}} | collective-permute-start | bytes 442376 | tf_op jit(solution)/shard_map/ppermute | solution.py:362
  27.7 9.3 %collective-permute-start.9 = (f32[96,384]{1,0:T(8,128)S(1)}, f32[96,384]{1,0:T(8,128)S(1)}, u32[]{:S(2)}, u32[]{:S(2)}) collective-permute-start(f32[96,384]{1,0:T(8,128)S(1)} %shard_map.35.r_2_), channel_id=1, source_target_pairs={{4,8},{5,9},{6,10},{7,11},{20,24},{21,25},{22,26},{23,27}} | collective-permute-start | bytes 442376 | tf_op jit(solution)/shard_map/ppermute | solution.py:362
  29.3 11.3 %collective-permute-start.10 = (f32[96,384]{1,0:T(8,128)S(1)}, f32[96,384]{1,0:T(8,128)S(1)}, u32[]{:S(2)}, u32[]{:S(2)}) collective-permute-start(f32[96,384]{1,0:T(8,128)S(1)} %shard_map.36.r_3_), channel_id=1, source_target_pairs={{4,8},{5,9},{6,10},{7,11},{20,24},{21,25},{22,26},{23,27}} | collective-permute-start | bytes 442376 | tf_op jit(solution)/shard_map/ppermute | solution.py:362
  31.0 12.2 %collective-permute-start.11 = (f32[96,384]{1,0:T(8,128)S(1)}, f32[96,384]{1,0:T(8,128)S(1)}, u32[]{:S(2)}, u32[]{:S(2)}) collective-permute-start(f32[96,384]{1,0:T(8,128)S(1)} %shard_map.37.r_4_), channel_id=1, source_target_pairs={{4,8},{5,9},{6,10},{7,11},{20,24},{21,25},{22,26},{23,27}} | collective-permute-start | bytes 442376 | tf_op jit(solution)/shard_map/ppermute | solution.py:362
  34.0 9.9 %collective-permute-start.13 = (f32[96,384]{1,0:T(8,128)S(1)}, f32[96,384]{1,0:T(8,128)S(1)}, u32[]{:S(2)}, u32[]{:S(2)}) collective-permute-start(f32[96,384]{1,0:T(8,128)S(1)} %shard_map.39.r_1_), channel_id=1, source_target_pairs={{8,12},{9,13},{10,14},{11,15},{24,28},{25,29},{26,30},{27,31}} | collective-permute-start | bytes 442376 | tf_op jit(solution)/shard_map/ppermute | solution.py:362
  37.0 20.9 %collective-permute-start.7 = (f32[2,96,384]{2,1,0:T(8,128)S(1)}, f32[2,96,384]{2,1,0:T(8,128)S(1)}, u32[]{:S(2)}, u32[]{:S(2)}) collective-permute-start(f32[2,96,384]{2,1,0:T(8,128)S(1)} %get-tuple-element.41), channel_id=1, source_target_pairs={{4,12},{5,13},{6,14},{7,15},{20,28},{21,29},{22,30},{23,31}} | collective-permute-start | bytes 884744 | tf_op jit(solution)/shard_map/ppermute | solution.py:362
  40.6 18.0 %collective-permute-start.6 = (f32[2,96,384]{2,1,0:T(8,128)S(1)}, f32[2,96,384]{2,1,0:T(8,128)S(1)}, u32[]{:S(2)}, u32[]{:S(2)}) collective-permute-start(f32[2,96,384]{2,1,0:T(8,128)S(1)} %shard_map.32), channel_id=1, source_target_pairs={{4,0},{5,1},{6,2},{7,3},{20,16},{21,17},{22,18},{23,19}} | collective-permute-start | bytes 884744 | tf_op jit(solution)/shard_map/ppermute | solution.py:362
  43.2 3.8 %collective-permute-start.14 = (f32[96,384]{1,0:T(8,128)S(1)}, f32[96,384]{1,0:T(8,128)S(1)}, u32[]{:S(2)}, u32[]{:S(2)}) collective-permute-start(f32[96,384]{1,0:T(8,128)S(1)} %shard_map.40.r_2_), channel_id=1, source_target_pairs={{8,12},{9,13},{10,14},{11,15},{24,28},{25,29},{26,30},{27,31}} | collective-permute-start | bytes 442376 | tf_op jit(solution)/shard_map/ppermute | solution.py:362
  43.9 11.9 %collective-permute-start.15 = (f32[96,384]{1,0:T(8,128)S(1)}, f32[96,384]{1,0:T(8,128)S(1)}, u32[]{:S(2)}, u32[]{:S(2)}) collective-permute-start(f32[96,384]{1,0:T(8,128)S(1)} %shard_map.41.r_3_), channel_id=1, source_target_pairs={{8,12},{9,13},{10,14},{11,15},{24,28},{25,29},{26,30},{27,31}} | collective-permute-start | bytes 442376 | tf_op jit(solution)/shard_map/ppermute | solution.py:362
  44.6 11.9 %collective-permute-start.16 = (f32[96,384]{1,0:T(8,128)S(1)}, f32[96,384]{1,0:T(8,128)S(1)}, u32[]{:S(2)}, u32[]{:S(2)}) collective-permute-start(f32[96,384]{1,0:T(8,128)S(1)} %shard_map.42.r_4_), channel_id=1, source_target_pairs={{8,12},{9,13},{10,14},{11,15},{24,28},{25,29},{26,30},{27,31}} | collective-permute-start | bytes 442376 | tf_op jit(solution)/shard_map/ppermute | solution.py:362
  47.0 14.6 %collective-permute-start.20 = (f32[2,96,384]{2,1,0:T(8,128)S(1)}, f32[2,96,384]{2,1,0:T(8,128)S(1)}, u32[]{:S(2)}, u32[]{:S(2)}) collective-permute-start(f32[2,96,384]{2,1,0:T(8,128)S(1)} %get-tuple-element.47), channel_id=1, source_target_pairs={{4,8},{5,9},{6,10},{7,11},{20,24},{21,25},{22,26},{23,27}} | collective-permute-start | bytes 884744 | tf_op jit(solution)/shard_map/ppermute | solution.py:362
  55.8 7.2 %collective-permute-start.22 = (f32[2,96,384]{2,1,0:T(8,128)S(1)}, f32[2,96,384]{2,1,0:T(8,128)S(1)}, u32[]{:S(2)}, u32[]{:S(2)}) collective-permute-start(f32[2,96,384]{2,1,0:T(8,128)S(1)} %shard_map.47), channel_id=1, source_target_pairs={{8,12},{9,13},{10,14},{11,15},{24,28},{25,29},{26,30},{27,31}} | collective-permute-start | bytes 884744 | tf_op jit(solution)/shard_map/ppermute | solution.py:362
  56.5 7.1 %collective-permute-start.21 = (f32[2,96,384]{2,1,0:T(8,128)S(1)}, f32[2,96,384]{2,1,0:T(8,128)S(1)}, u32[]{:S(2)}, u32[]{:S(2)}) collective-permute-start(f32[2,96,384]{2,1,0:T(8,128)S(1)} %get-tuple-element.48), channel_id=1, source_target_pairs={{4,0},{5,1},{6,2},{7,3},{20,16},{21,17},{22,18},{23,19}} | collective-permute-start | bytes 884744 | tf_op jit(solution)/shard_map/ppermute | solution.py:362
  57.9 5.8 %collective-permute-start.23 = (f32[2,96,384]{2,1,0:T(8,128)S(1)}, f32[2,96,384]{2,1,0:T(8,128)S(1)}, u32[]{:S(2)}, u32[]{:S(2)}) collective-permute-start(f32[2,96,384]{2,1,0:T(8,128)S(1)} %get-tuple-element.50), channel_id=1, source_target_pairs={{8,0},{9,1},{10,2},{11,3},{24,16},{25,17},{26,18},{27,19}} | collective-permute-start | bytes 884744 | tf_op jit(solution)/shard_map/ppermute | solution.py:362
  58.6 17.6 %collective-permute-start.24 = (f32[2,96,384]{2,1,0:T(8,128)S(1)}, f32[2,96,384]{2,1,0:T(8,128)S(1)}, u32[]{:S(2)}, u32[]{:S(2)}) collective-permute-start(f32[2,96,384]{2,1,0:T(8,128)S(1)} %get-tuple-element.51), channel_id=1, source_target_pairs={{8,4},{9,5},{10,6},{11,7},{24,20},{25,21},{26,22},{27,23}} | collective-permute-start | bytes 884744 | tf_op jit(solution)/shard_map/ppermute | solution.py:362
  61.6 17.5 %collective-permute-start.17 = (f32[4,96,192]{2,1,0:T(8,128)S(1)}, f32[4,96,192]{2,1,0:T(8,128)S(1)}, u32[]{:S(2)}, u32[]{:S(2)}) collective-permute-start(f32[4,96,192]{2,1,0:T(8,128)S(1)} %get-tuple-element.44), channel_id=1, source_target_pairs={{0,1},{1,0},{2,3},{3,2},{4,5},{5,4},{6,7},{7,6},{8,9},{9,8},{10,11... | collective-permute-start | bytes 884744 | tf_op jit(solution)/shard_map/ppermute | solution.py:423
  76.3 2.9 %collective-permute-start.25 = (f32[4,96,192]{2,1,0:T(8,128)S(1)}, f32[4,96,192]{2,1,0:T(8,128)S(1)}, u32[]{:S(2)}, u32[]{:S(2)}) collective-permute-start(f32[4,96,192]{2,1,0:T(8,128)S(1)} %get-tuple-element.52), channel_id=1, source_target_pairs={{0,1},{1,0},{2,3},{3,2},{4,5},{5,4},{6,7},{7,6},{8,9},{9,8},{10,11... | collective-permute-start | bytes 884744 | tf_op jit(solution)/shard_map/ppermute | solution.py:423

commit v5 on v4

--- a/solution.py
+++ b/solution.py
@@ -8,7 +8,7 @@
 from jax.sharding import PartitionSpec as P
 
 
-CHUNKS = 4
+CHUNKS = 3
 GRANT = pltpu.CompilerParams(vmem_limit_bytes=20 * 2**20)
 
 
@@ -170,7 +170,7 @@
 
 def local_kernel(chunks, *refs):
     a0_ref, *prod_refs, op_ref = refs[:chunks + 2]
-    sym_ref, g0_ref, g1_ref, pack_ref, own_ref, *row_refs = refs[chunks + 2:]
+    sym_ref, g0_ref, g1_ref, b_ref, pack_ref, own_ref, *row_refs = refs[chunks + 2:]
     place = lax.axis_index("tm")
     op = op_ref[lax.axis_index("col")]
     sym = 0.5 * (op + op.T)
@@ -178,6 +178,7 @@
     right = as_right(sym)
     a0 = a0_ref[...]
     b = jnp.concatenate([r[...] for r in prod_refs], axis=0)
+    b_ref[...] = b
     for x, g_ref in ((a0, g0_ref), (b, g1_ref)):
         g_ref[...] = product_t(as_left(product(as_left(x), right)), as_right_t(x))
     rows = own_ref.shape[1]
@@ -230,12 +231,36 @@
         t_ref[...] = as_right_t(r_ref[...])
         for i, middle_ref in enumerate((sym_ref, g0_ref, g1_ref)):
             t = 2 * place - 1 + i
-            wanted = {to: heis_slices(place, to).index(t) for to in outs if t in heis_slices(place, to)}
+            known = {to: heis_slices(place, to, count) for to in outs}
+            wanted = {to: ts.index(t) for to, ts in known.items() if t in ts}
             if not wanted:
                 continue
             top, bottom = min(wanted) * rows, (max(wanted) + 1) * rows
             weighted = product(as_left(r_ref[top:bottom, :]), as_right(middle_ref[...]))
             rows_out(outs, wanted, product_t(as_left(weighted), t_ref[...]), top, rows)
+
+
+def last_kernel(count, chunks, *refs):
+    sym_ref, g0_ref, g1_ref, step_ref = refs[:4]
+    before = refs[4:4 + chunks]
+    out_ref, r_ref, t_ref = refs[4 + chunks:]
+
+    @pl.when(lax.axis_index("tm") == count - 1)
+    def _():
+        rows = out_ref.shape[1]
+        top = (count - 1) * rows
+
+        def own_rows(position, middle_ref):
+            weighted = product(as_left(r_ref[top:, :]), as_right(middle_ref[...]))
+            out_ref[position] = product_t(as_left(weighted), t_ref[...])
+
+        joined(r_ref, before)
+        t_ref[...] = as_right_t(r_ref[...])
+        own_rows(0, sym_ref)
+        r_ref[...] = product(as_left(r_ref[...]), as_right(step_ref[...]))
+        t_ref[...] = as_right_t(r_ref[...])
+        for i, middle_ref in enumerate((sym_ref, g0_ref, g1_ref)):
+            own_rows(1 + i, middle_ref)
 
 
 def ahead_kernel(place, count, chunks, *refs):
@@ -255,18 +280,18 @@
             rows_out(outs, {to: i for to in range(place + 1)}, heis, 0, rows)
 
 
-def heis_slices(place, to):
+def heis_slices(place, to, count):
     if to > place:
-        return [2 * place - 1, 2 * place]
+        return [2 * place] if place == count - 2 else [2 * place - 1, 2 * place]
     if to == place:
-        return [2 * place - 1, 2 * place, 2 * place + 1]
+        return [2 * place - 3] * (place == count - 1) + [2 * place - 1, 2 * place, 2 * place + 1]
     return [2 * place, 2 * place + 1]
 
 
 def heis_groups(place, count):
     if place == 1:
         return [[0], list(range(1, count))]
-    return [list(range(place + 1, count)), [place]] if place + 1 < count else [[place]]
+    return [list(range(place + 1, count)), [place]] if place + 1 < count else []
 
 
 def gather_kernel(chosen, *refs):
@@ -367,47 +392,53 @@
         plan[to].extend((rank, t, len(arrays), i) for i, t in enumerate(ts))
         arrays.append(x)
 
-    soon = [(1, 0), (1, count - 1)]
+    soon = [(1, 0)]
     before = [along(x, (0, 1)) for x in prod]
-    shapes = [square] * 3 + [(2, 2 * (order // 3), order), (2, rows, order)] + [(1, rows, order)] * (count - 1)
-    sym, g0, g1, pack, own, *firsts = local_call(
+    shapes = [square] * 4 + [(2, 2 * (order // 3), order), (2, rows, order)] + [(1, rows, order)] * (count - 1)
+    sym, g0, g1, whole, pack, own, *firsts = local_call(
         lambda *r: local_kernel(CHUNKS, *r), shapes, (a0, *prod, current_op),
         outside=(CHUNKS + 1,),
     )
+    last_step = along(whole, (count - 2, count - 1))
     ahead = along(pack, [(j, j - 1) for j in range(2, count)])
     keep(own, 0, [0, 1], 0)
     for to in range(1, count):
         keep(along(firsts[to - 1], (0, to)), to, [0], 1 if to == 1 else 5)
-    for place in range(1, count):
+    for place in range(1, count - 1):
         after = []
-        for x in before if place + 1 < count else ():
+        for x in before:
             after += local_call(lambda *r, p=place: hop_kernel(p, *r), [chunk], (x, *prod))
-        if place + 1 < count:
-            following = [along(x, (place, place + 1)) for x in after]
+        passed = after if place < count - 2 else before
+        following = [along(x, (place, place + 1)) for x in passed]
         for receivers in heis_groups(place, count):
             outs = local_call(
                 lambda *r, p=place, w=receivers: heis_kernel(p, w, count, CHUNKS, *r),
-                [(len(heis_slices(place, to)), rows, order) for to in receivers],
+                [(len(heis_slices(place, to, count)), rows, order) for to in receivers],
                 (sym, g0, g1, *before), scratch=scratch,
             )
             for to, x in zip(receivers, outs):
-                ts = heis_slices(place, to)
+                ts = heis_slices(place, to, count)
                 if to == place:
                     keep(x, to, ts, 0)
                 else:
                     keep(along(x, (place, to)), to, ts, 1 if (place, to) in soon else 3)
-        if place + 1 < count:
-            outs = local_call(
-                lambda *r, p=place: ahead_kernel(p, count, CHUNKS, *r),
-                [(2, rows, order)] * (place + 1), (ahead, *after), scratch=scratch,
-            )
-            for to, x in enumerate(outs):
-                ts = [2 * place + 2, 2 * place + 3]
-                if to == place:
-                    keep(x, to, ts, 2)
-                else:
-                    keep(along(x, (place, to)), to, ts, 4)
-            before = following
+        outs = local_call(
+            lambda *r, p=place: ahead_kernel(p, count, CHUNKS, *r),
+            [(2, rows, order)] * (place + 1), (ahead, *after), scratch=scratch,
+        )
+        for to, x in enumerate(outs):
+            ts = [2 * place + 2, 2 * place + 3]
+            if to == place:
+                keep(x, to, ts, 2)
+            else:
+                keep(along(x, (place, to)), to, ts, 4)
+        before = following
+    last_slices = heis_slices(count - 1, count - 1, count)
+    outs = local_call(
+        lambda *r: last_kernel(count, CHUNKS, *r), [(len(last_slices), rows, order)],
+        (sym, g0, g1, last_step, *before), scratch=scratch,
+    )
+    keep(outs[0], count - 1, last_slices, 0)
     width = order // 2
     length = count * slices
     half = length // 2

time: 81.2 us -> 84.9 us (1.046)
  the two profiles are of different devices: /device:TPU:11 before, /device:TPU:9 now
where the time goes in v5:
time: 84.9 us; the launch traced here: 84.5 us
  starting transfers between devices  37.9 us (45%)
  waiting for transfers between devices  31.1 us (37%)
  Pallas kernels  14.8 us (17%)
    ppermute x21, starting transfers between devices, along(): return lax.ppermute(x, 'tm', [hop] if isinstance(hop, tuple) else hop)  32.9 us
    ppermute x21, waiting for transfers between devices, along(): return lax.ppermute(x, 'tm', [hop] if isinstance(hop, tuple) else hop)  30.6 us
    pallas_call x17, Pallas kernels, local_call(): pl.pallas_call(kernel, out_shape=[pltpu.VMEM(s, jnp.float32) for s in out...  9.58 us
    ppermute x2, starting transfers between devices, paired_body(): taken.append(lax.ppermute(give, 'col', swap))  4.3 us
    pallas_call x2, Pallas kernels, spectrum(): pl.pallas_call(lambda *r: spectrum_kernel(own, tables, *r), out_shape=jax...  2.83 us
    pallas_call x2, Pallas kernels, pick(): pl.pallas_call(lambda *r: pick_kernel(own, *r), out_shape=pltpu.VMEM((sli...  2.41 us
  transfers between devices with their start and end apart: 24, of which 5 were waited for; matrix products, arithmetic and copies ran while one was open for 0% of the time, Pallas kernels for 11%

profile of v5, /device:TPU:9, one launch (start us, length us, event | category | flops | bytes accessed | tf_op | source)
XLA Modules:
  0.0 84.5 jit_solution(15545108668843745622)
XLA Ops:
  0.0 1.3 %shard_map.29 = f32[2,192,384]{2,1,0:T(8,128)S(1)} custom-call(f32[2,2,192,384]{3,2,1,0:T(8,128)} %bitcast.1), custom_call_target="tpu_custom_call" | custom-call | tf_op jit(solution)/shard_map/pallas_call | solution.py:370
  1.3 0.7 collective-permute-start
  2.0 1.2 %shard_map.28.mine_ref = f32[2,192,384]{2,1,0:T(8,128)S(1)} custom-call(f32[2,2,192,384]{3,2,1,0:T(8,128)} %bitcast.2), custom_call_target="tpu_custom_call" | custom-call | tf_op jit(solution)/shard_map/pallas_call | solution.py:370
  3.6 0.8 shard_map.30
  4.5 2.3 %shard_map.31 = (f32[384,384]{1,0:T(8,128)S(1)}, f32[384,384]{1,0:T(8,128)S(1)}, f32[384,384]{1,0:T(8,128)S(1)}, f32[384,384]{1,0:T(8,128)S(1)}, f32[2,256,384]{...) custom-call(f32[384,384]{1,0:T(8,128)S(1)} %get-tuple-element.30.r_0, ...), custom_call_target="tpu_custom_call" | custom-call | tf_op jit(solution)/shard_map/pallas_call | solution.py:115
  6.8 1.3 %collective-permute-start.9 = (f32[2,256,384]{2,1,0:T(8,128)S(1)}, f32[2,256,384]{2,1,0:T(8,128)S(1)}, u32[]{:S(2)}, u32[]{:S(2)}) collective-permute-start(f32[2,256,384]{2,1,0:T(8,128)S(1)} %get-tuple-element.40), channel_id=1, source_target_pairs={{8,4},{12,8},{9,5},{13,9},{10,6},{14,10},{11,7},{15,11},{24,20},{2... | collective-permute-start | bytes 2359304 | tf_op jit(solution)/shard_map/ppermute | solution.py:387
  8.1 1.3 %collective-permute-start.4 = (f32[128,384]{1,0:T(8,128)S(1)}, f32[128,384]{1,0:T(8,128)S(1)}, u32[]{:S(2)}, u32[]{:S(2)}) collective-permute-start(f32[128,384]{1,0:T(8,128)S(1)} %get-tuple-element.33.r_3_), channel_id=1, source_target_pairs={{0,4},{1,5},{2,6},{3,7},{16,20},{17,21},{18,22},{19,23}} | collective-permute-start | bytes 589832 | tf_op jit(solution)/shard_map/ppermute | solution.py:387
  9.4 1.3 %collective-permute-start.3 = (f32[128,384]{1,0:T(8,128)S(1)}, f32[128,384]{1,0:T(8,128)S(1)}, u32[]{:S(2)}, u32[]{:S(2)}) collective-permute-start(f32[128,384]{1,0:T(8,128)S(1)} %get-tuple-element.32.r_2_), channel_id=1, source_target_pairs={{0,4},{1,5},{2,6},{3,7},{16,20},{17,21},{18,22},{19,23}} | collective-permute-start | bytes 589832 | tf_op jit(solution)/shard_map/ppermute | solution.py:387
  11.4 1.3 %collective-permute-start.2 = (f32[128,384]{1,0:T(8,128)S(1)}, f32[128,384]{1,0:T(8,128)S(1)}, u32[]{:S(2)}, u32[]{:S(2)}) collective-permute-start(f32[128,384]{1,0:T(8,128)S(1)} %get-tuple-element.31.r_1_), channel_id=1, source_target_pairs={{0,4},{1,5},{2,6},{3,7},{16,20},{17,21},{18,22},{19,23}} | collective-permute-start | bytes 589832 | tf_op jit(solution)/shard_map/ppermute | solution.py:387
  12.7 3.4 %collective-permute-done.4.r_5_.r_0_ = f32[128,384]{1,0:T(8,128)S(1)} collective-permute-done((f32[128,384]{1,0:T(8,128)S(1)}, f32[128,384]{1,0:T(8,128)S(1)}, u32[]{:S(2)}, u32[]{:S(2)}) %collective-permute-start.4) | collective-permute-done | bytes 196640 | tf_op jit(solution)/shard_map/ppermute | solution.py:387
  17.1 9.4 %collective-permute-start.8 = (f32[128,384]{1,0:T(8,128)S(1)}, f32[128,384]{1,0:T(8,128)S(1)}, u32[]{:S(2)}, u32[]{:S(2)}) collective-permute-start(f32[128,384]{1,0:T(8,128)S(1)} %shard_map.36.r_3_), channel_id=1, source_target_pairs={{4,8},{5,9},{6,10},{7,11},{20,24},{21,25},{22,26},{23,27}} | collective-permute-start | bytes 589832 | tf_op jit(solution)/shard_map/ppermute | solution.py:387
  26.5 1.3 %collective-permute-start.1 = (f32[1,96,384]{2,1,0:T(8,128)S(1)}, f32[1,96,384]{2,1,0:T(8,128)S(1)}, u32[]{:S(2)}, u32[]{:S(2)}) collective-permute-start(f32[1,96,384]{2,1,0:T(8,128)S(1)} %get-tuple-element.35), channel_id=1, source_target_pairs={{0,4},{1,5},{2,6},{3,7},{16,20},{17,21},{18,22},{19,23}} | collective-permute-start | bytes 442376 | tf_op jit(solution)/shard_map/ppermute | solution.py:387
  28.2 1.3 %collective-permute-start.7 = (f32[128,384]{1,0:T(8,128)S(1)}, f32[128,384]{1,0:T(8,128)S(1)}, u32[]{:S(2)}, u32[]{:S(2)}) collective-permute-start(f32[128,384]{1,0:T(8,128)S(1)} %shard_map.35.r_2_), channel_id=1, source_target_pairs={{4,8},{5,9},{6,10},{7,11},{20,24},{21,25},{22,26},{23,27}} | collective-permute-start | bytes 589832 | tf_op jit(solution)/shard_map/ppermute | solution.py:387
  29.5 2.3 %shard_map.33 = (f32[3,96,384]{2,1,0:T(8,128)S(1)}, f32[2,96,384]{2,1,0:T(8,128)S(1)}, f32[2,96,384]{2,1,0:T(8,128)S(1)}) custom-call(f32[384,384]{1,0:T(8,128)S(1)} %get-tuple-element.36.r_0_, f32[384,384]{1,0:T(8,128)S(1)} %get-tuple-element.37.r_1_, f32[384,384]{1,0:T(8,128)S(1)} %get-tuple-element.38.r_2_, ...), custom_call_target="tpu_custom_call" | custom-call | tf_op jit(solution)/shard_map/pallas_call | solution.py:115
  31.8 1.3 %collective-permute-start.17 = (f32[2,96,384]{2,1,0:T(8,128)S(1)}, f32[2,96,384]{2,1,0:T(8,128)S(1)}, u32[]{:S(2)}, u32[]{:S(2)}) collective-permute-start(f32[2,96,384]{2,1,0:T(8,128)S(1)} %get-tuple-element.46), channel_id=1, source_target_pairs={{4,8},{5,9},{6,10},{7,11},{20,24},{21,25},{22,26},{23,27}} | collective-permute-start | bytes 884744 | tf_op jit(solution)/shard_map/ppermute | solution.py:387
  33.2 0.7 collective-permute-start.10
  34.2 3.6 %collective-permute-start.6 = (f32[128,384]{1,0:T(8,128)S(1)}, f32[128,384]{1,0:T(8,128)S(1)}, u32[]{:S(2)}, u32[]{:S(2)}) collective-permute-start(f32[128,384]{1,0:T(8,128)S(1)} %shard_map.34.r_1_), channel_id=1, source_target_pairs={{4,8},{5,9},{6,10},{7,11},{20,24},{21,25},{22,26},{23,27}} | collective-permute-start | bytes 589832 | tf_op jit(solution)/shard_map/ppermute | solution.py:387
  37.8 1.2 %shard_map.32 = f32[2,96,384]{2,1,0:T(8,128)S(1)} custom-call(f32[384,384]{1,0:T(8,128)S(1)} %get-tuple-element.36.r_0_, f32[384,384]{1,0:T(8,128)S(1)} %get-tuple-element.37.r_1_, f32[384,384]{1,0:T(8,128)S(1)} %get-tuple-element.38.r_2_, f32[128,384]{1,0:T(8,128)S(1)} %collective-permute-done.2.r_3_.r_0_, f32[128,384]{1,0:T(8,128)S(1)} %collective-permute-done.3.r_4_.r_0_, ...), custom_call_target="tpu_custom_call" | custom-call | tf_op jit(solution)/shard_map/pallas_call | solution.py:115
  39.0 1.3 %collective-permute-start.5 = (f32[2,96,384]{2,1,0:T(8,128)S(1)}, f32[2,96,384]{2,1,0:T(8,128)S(1)}, u32[]{:S(2)}, u32[]{:S(2)}) collective-permute-start(f32[2,96,384]{2,1,0:T(8,128)S(1)} %shard_map.32), channel_id=1, source_target_pairs={{4,0},{5,1},{6,2},{7,3},{20,16},{21,17},{22,18},{23,19}} | collective-permute-start | bytes 884744 | tf_op jit(solution)/shard_map/ppermute | solution.py:387
  40.3 7.9 %collective-permute-done.6.r_3_.r_0_ = f32[128,384]{1,0:T(8,128)S(1)} collective-permute-done((f32[128,384]{1,0:T(8,128)S(1)}, f32[128,384]{1,0:T(8,128)S(1)}, u32[]{:S(2)}, u32[]{:S(2)}) %collective-permute-start.6) | collective-permute-done | bytes 196640 | tf_op jit(solution)/shard_map/ppermute | solution.py:387
  49.6 0.7 collective-permute-start.11
  50.3 1.5 %shard_map.44 = (f32[2,96,384]{2,1,0:T(8,128)S(1)}, f32[2,96,384]{2,1,0:T(8,128)S(1)}) custom-call(f32[2,256,384]{2,1,0:T(8,128)S(1)} %collective-permute-done.9.r_0_, f32[128,384]{1,0:T(8,128)S(1)} %shard_map.34.r_1_, f32[128,384]{1,0:T(8,128)S(1)} %shard_map.35.r_2_, f32[128,384]{1,0:T(8,128)S(1)} %shard_map.36.r_3_), custom_call_target="tpu_custom_call" | custom-call | tf_op jit(solution)/shard_map/pallas_call | solution.py:115
  51.9 1.3 %collective-permute-start.18 = (f32[2,96,384]{2,1,0:T(8,128)S(1)}, f32[2,96,384]{2,1,0:T(8,128)S(1)}, u32[]{:S(2)}, u32[]{:S(2)}) collective-permute-start(f32[2,96,384]{2,1,0:T(8,128)S(1)} %get-tuple-element.47), channel_id=1, source_target_pairs={{4,12},{5,13},{6,14},{7,15},{20,28},{21,29},{22,30},{23,31}} | collective-permute-start | bytes 884744 | tf_op jit(solution)/shard_map/ppermute | solution.py:387
  53.2 1.3 %collective-permute-start.19 = (f32[2,96,384]{2,1,0:T(8,128)S(1)}, f32[2,96,384]{2,1,0:T(8,128)S(1)}, u32[]{:S(2)}, u32[]{:S(2)}) collective-permute-start(f32[2,96,384]{2,1,0:T(8,128)S(1)} %get-tuple-element.48), channel_id=1, source_target_pairs={{4,0},{5,1},{6,2},{7,3},{20,16},{21,17},{22,18},{23,19}} | collective-permute-start | bytes 884744 | tf_op jit(solution)/shard_map/ppermute | solution.py:387
  54.5 0.7 collective-permute-start.21
  55.2 1.5 %collective-permute-start.22 = (f32[2,96,384]{2,1,0:T(8,128)S(1)}, f32[2,96,384]{2,1,0:T(8,128)S(1)}, u32[]{:S(2)}, u32[]{:S(2)}) collective-permute-start(f32[2,96,384]{2,1,0:T(8,128)S(1)} %get-tuple-element.51), channel_id=1, source_target_pairs={{8,4},{9,5},{10,6},{11,7},{24,20},{25,21},{26,22},{27,23}} | collective-permute-start | bytes 884744 | tf_op jit(solution)/shard_map/ppermute | solution.py:387
  57.7 1.1 %collective-permute-done.18.r_3_ = f32[2,96,384]{2,1,0:T(8,128)S(1)} collective-permute-done((f32[2,96,384]{2,1,0:T(8,128)S(1)}, f32[2,96,384]{2,1,0:T(8,128)S(1)}, u32[]{:S(2)}, u32[]{:S(2)}) %collective-permute-start.18) | collective-permute-done | bytes 294944 | tf_op jit(solution)/shard_map/ppermute | solution.py:387
  58.7 1.7 %collective-permute-start.14 = (f32[4,96,192]{2,1,0:T(8,128)S(1)}, f32[4,96,192]{2,1,0:T(8,128)S(1)}, u32[]{:S(2)}, u32[]{:S(2)}) collective-permute-start(f32[4,96,192]{2,1,0:T(8,128)S(1)} %get-tuple-element.43), channel_id=1, source_target_pairs={{0,1},{1,0},{2,3},{3,2},{4,5},{5,4},{6,7},{7,6},{8,9},{9,8},{10,11... | collective-permute-start | bytes 884744 | tf_op jit(solution)/shard_map/ppermute | solution.py:454
  60.4 18.2 %collective-permute-done.22.r_8_ = f32[2,96,384]{2,1,0:T(8,128)S(1)} collective-permute-done((f32[2,96,384]{2,1,0:T(8,128)S(1)}, f32[2,96,384]{2,1,0:T(8,128)S(1)}, u32[]{:S(2)}, u32[]{:S(2)}) %collective-permute-start.22) | collective-permute-done | bytes 294944 | tf_op jit(solution)/shard_map/ppermute | solution.py:387
  78.8 2.6 %collective-permute-start.23 = (f32[4,96,192]{2,1,0:T(8,128)S(1)}, f32[4,96,192]{2,1,0:T(8,128)S(1)}, u32[]{:S(2)}, u32[]{:S(2)}) collective-permute-start(f32[4,96,192]{2,1,0:T(8,128)S(1)} %get-tuple-element.52), channel_id=1, source_target_pairs={{0,1},{1,0},{2,3},{3,2},{4,5},{5,4},{6,7},{7,6},{8,9},{9,8},{10,11... | collective-permute-start | bytes 884744 | tf_op jit(solution)/shard_map/ppermute | solution.py:454
  81.4 1.4 %spectrum.2.r_2_ = f32[2,2,8,96,192]{4,3,2,1,0:T(8,128)} custom-call(f32[4,96,192]{2,1,0:T(8,128)S(1)} %get-tuple-element.53.r_0_, f32[4,96,192]{2,1,0:T(8,128)S(1)} %get-tuple-element.54.r_1_), custom_call_target="tpu_custom_call" | custom-call | tf_op jit(solution)/shard_map/spectrum/pallas_call | solution.py:459
  82.9 1.4 %spectrum.3 = f32[2,2,8,96,192]{4,3,2,1,0:T(8,128)} custom-call(f32[4,96,192]{2,1,0:T(8,128)S(1)} %collective-permute-done.14.r_0_, f32[4,96,192]{2,1,0:T(8,128)S(1)} %collective-permute-done.23.r_1_, f32[2,2,8,96,192]{4,3,2,1,0:T(8,128)} %spectrum.2.r_2_), custom_call_target="tpu_custom_call", output_to_operand_aliasing={{}: (2, {})} | custom-call | tf_op jit(solution)/shard_map/spectrum/pallas_call | solution.py:459
  (39 shorter events, 5.3 us)
Async XLA Ops:
  0.0 4.4 %copy-start = (f32[2,384,384]{2,1,0:T(8,128)S(1)}, f32[2,384,384]{2,1,0:T(8,128)}, u32[]{:S(2)}) copy-start(f32[2,384,384]{2,1,0:T(8,128)} %r_4_.1) | copy-start | bytes 3538948
  1.3 2.4 %collective-permute-start = (f32[2,192,384]{2,1,0:T(8,128)S(1)}, f32[2,192,384]{2,1,0:T(8,128)S(1)}, u32[]{:S(2)}, u32[]{:S(2)}) collective-permute-start(f32[2,192,384]{2,1,0:T(8,128)S(1)} %shard_map.29), channel_id=1, source_target_pairs={{0,1},{1,0},{2,3},{3,2},{4,5},{5,4},{6,7},{7,6},{8,9},{9,8},{10,11... | collective-permute-start | bytes 1769480 | tf_op jit(solution)/shard_map/ppermute | solution.py:379
  6.8 42.8 %collective-permute-start.9 = (f32[2,256,384]{2,1,0:T(8,128)S(1)}, f32[2,256,384]{2,1,0:T(8,128)S(1)}, u32[]{:S(2)}, u32[]{:S(2)}) collective-permute-start(f32[2,256,384]{2,1,0:T(8,128)S(1)} %get-tuple-element.40), channel_id=1, source_target_pairs={{8,4},{12,8},{9,5},{13,9},{10,6},{14,10},{11,7},{15,11},{24,20},{2... | collective-permute-start | bytes 2359304 | tf_op jit(solution)/shard_map/ppermute | solution.py:387
  8.1 8.0 %collective-permute-start.4 = (f32[128,384]{1,0:T(8,128)S(1)}, f32[128,384]{1,0:T(8,128)S(1)}, u32[]{:S(2)}, u32[]{:S(2)}) collective-permute-start(f32[128,384]{1,0:T(8,128)S(1)} %get-tuple-element.33.r_3_), channel_id=1, source_target_pairs={{0,4},{1,5},{2,6},{3,7},{16,20},{17,21},{18,22},{19,23}} | collective-permute-start | bytes 589832 | tf_op jit(solution)/shard_map/ppermute | solution.py:387
  9.4 17.2 %collective-permute-start.3 = (f32[128,384]{1,0:T(8,128)S(1)}, f32[128,384]{1,0:T(8,128)S(1)}, u32[]{:S(2)}, u32[]{:S(2)}) collective-permute-start(f32[128,384]{1,0:T(8,128)S(1)} %get-tuple-element.32.r_2_), channel_id=1, source_target_pairs={{0,4},{1,5},{2,6},{3,7},{16,20},{17,21},{18,22},{19,23}} | collective-permute-start | bytes 589832 | tf_op jit(solution)/shard_map/ppermute | solution.py:387
  10.7 6.4 %collective-permute-start.15 = (f32[1,96,384]{2,1,0:T(8,128)S(1)}, f32[1,96,384]{2,1,0:T(8,128)S(1)}, u32[]{:S(2)}, u32[]{:S(2)}) collective-permute-start(f32[1,96,384]{2,1,0:T(8,128)S(1)} %get-tuple-element.44), channel_id=1, source_target_pairs={{0,8},{1,9},{2,10},{3,11},{16,24},{17,25},{18,26},{19,27}} | collective-permute-start | bytes 442376 | tf_op jit(solution)/shard_map/ppermute | solution.py:387
  11.4 16.8 %collective-permute-start.2 = (f32[128,384]{1,0:T(8,128)S(1)}, f32[128,384]{1,0:T(8,128)S(1)}, u32[]{:S(2)}, u32[]{:S(2)}) collective-permute-start(f32[128,384]{1,0:T(8,128)S(1)} %get-tuple-element.31.r_1_), channel_id=1, source_target_pairs={{0,4},{1,5},{2,6},{3,7},{16,20},{17,21},{18,22},{19,23}} | collective-permute-start | bytes 589832 | tf_op jit(solution)/shard_map/ppermute | solution.py:387
  16.1 15.8 %collective-permute-start.16 = (f32[1,96,384]{2,1,0:T(8,128)S(1)}, f32[1,96,384]{2,1,0:T(8,128)S(1)}, u32[]{:S(2)}, u32[]{:S(2)}) collective-permute-start(f32[1,96,384]{2,1,0:T(8,128)S(1)} %get-tuple-element.45), channel_id=1, source_target_pairs={{0,12},{1,13},{2,14},{3,15},{16,28},{17,29},{18,30},{19,31}} | collective-permute-start | bytes 442376 | tf_op jit(solution)/shard_map/ppermute | solution.py:387
  17.1 17.1 %collective-permute-start.8 = (f32[128,384]{1,0:T(8,128)S(1)}, f32[128,384]{1,0:T(8,128)S(1)}, u32[]{:S(2)}, u32[]{:S(2)}) collective-permute-start(f32[128,384]{1,0:T(8,128)S(1)} %shard_map.36.r_3_), channel_id=1, source_target_pairs={{4,8},{5,9},{6,10},{7,11},{20,24},{21,25},{22,26},{23,27}} | collective-permute-start | bytes 589832 | tf_op jit(solution)/shard_map/ppermute | solution.py:387
  26.5 6.6 %collective-permute-start.1 = (f32[1,96,384]{2,1,0:T(8,128)S(1)}, f32[1,96,384]{2,1,0:T(8,128)S(1)}, u32[]{:S(2)}, u32[]{:S(2)}) collective-permute-start(f32[1,96,384]{2,1,0:T(8,128)S(1)} %get-tuple-element.35), channel_id=1, source_target_pairs={{0,4},{1,5},{2,6},{3,7},{16,20},{17,21},{18,22},{19,23}} | collective-permute-start | bytes 442376 | tf_op jit(solution)/shard_map/ppermute | solution.py:387
  28.2 10.8 %collective-permute-start.7 = (f32[128,384]{1,0:T(8,128)S(1)}, f32[128,384]{1,0:T(8,128)S(1)}, u32[]{:S(2)}, u32[]{:S(2)}) collective-permute-start(f32[128,384]{1,0:T(8,128)S(1)} %shard_map.35.r_2_), channel_id=1, source_target_pairs={{4,8},{5,9},{6,10},{7,11},{20,24},{21,25},{22,26},{23,27}} | collective-permute-start | bytes 589832 | tf_op jit(solution)/shard_map/ppermute | solution.py:387
  31.8 17.0 %collective-permute-start.17 = (f32[2,96,384]{2,1,0:T(8,128)S(1)}, f32[2,96,384]{2,1,0:T(8,128)S(1)}, u32[]{:S(2)}, u32[]{:S(2)}) collective-permute-start(f32[2,96,384]{2,1,0:T(8,128)S(1)} %get-tuple-element.46), channel_id=1, source_target_pairs={{4,8},{5,9},{6,10},{7,11},{20,24},{21,25},{22,26},{23,27}} | collective-permute-start | bytes 884744 | tf_op jit(solution)/shard_map/ppermute | solution.py:387
  33.2 23.6 %collective-permute-start.10 = (f32[384,384]{1,0:T(8,128)S(1)}, f32[384,384]{1,0:T(8,128)S(1)}, u32[]{:S(2)}, u32[]{:S(2)}) collective-permute-start(f32[384,384]{1,0:T(8,128)S(1)} %get-tuple-element.42), channel_id=1, source_target_pairs={{8,12},{9,13},{10,14},{11,15},{24,28},{25,29},{26,30},{27,31}} | collective-permute-start | bytes 1769480 | tf_op jit(solution)/shard_map/ppermute | solution.py:387
  34.2 14.0 %collective-permute-start.6 = (f32[128,384]{1,0:T(8,128)S(1)}, f32[128,384]{1,0:T(8,128)S(1)}, u32[]{:S(2)}, u32[]{:S(2)}) collective-permute-start(f32[128,384]{1,0:T(8,128)S(1)} %shard_map.34.r_1_), channel_id=1, source_target_pairs={{4,8},{5,9},{6,10},{7,11},{20,24},{21,25},{22,26},{23,27}} | collective-permute-start | bytes 589832 | tf_op jit(solution)/shard_map/ppermute | solution.py:387
  39.0 12.8 %collective-permute-start.5 = (f32[2,96,384]{2,1,0:T(8,128)S(1)}, f32[2,96,384]{2,1,0:T(8,128)S(1)}, u32[]{:S(2)}, u32[]{:S(2)}) collective-permute-start(f32[2,96,384]{2,1,0:T(8,128)S(1)} %shard_map.32), channel_id=1, source_target_pairs={{4,0},{5,1},{6,2},{7,3},{20,16},{21,17},{22,18},{23,19}} | collective-permute-start | bytes 884744 | tf_op jit(solution)/shard_map/ppermute | solution.py:387
  48.2 5.0 %collective-permute-start.13 = (f32[128,384]{1,0:T(8,128)S(1)}, f32[128,384]{1,0:T(8,128)S(1)}, u32[]{:S(2)}, u32[]{:S(2)}) collective-permute-start(f32[128,384]{1,0:T(8,128)S(1)} %collective-permute-done.8.r_5_.r_0_), channel_id=1, source_target_pairs={{8,12},{9,13},{10,14},{11,15},{24,28},{25,29},{26,30},{27,31}} | collective-permute-start | bytes 589832 | tf_op jit(solution)/shard_map/ppermute | solution.py:387
  48.9 5.6 %collective-permute-start.12 = (f32[128,384]{1,0:T(8,128)S(1)}, f32[128,384]{1,0:T(8,128)S(1)}, u32[]{:S(2)}, u32[]{:S(2)}) collective-permute-start(f32[128,384]{1,0:T(8,128)S(1)} %collective-permute-done.7.r_4_.r_0_), channel_id=1, source_target_pairs={{8,12},{9,13},{10,14},{11,15},{24,28},{25,29},{26,30},{27,31}} | collective-permute-start | bytes 589832 | tf_op jit(solution)/shard_map/ppermute | solution.py:387
  49.6 5.6 %collective-permute-start.11 = (f32[128,384]{1,0:T(8,128)S(1)}, f32[128,384]{1,0:T(8,128)S(1)}, u32[]{:S(2)}, u32[]{:S(2)}) collective-permute-start(f32[128,384]{1,0:T(8,128)S(1)} %collective-permute-done.6.r_3_.r_0_), channel_id=1, source_target_pairs={{8,12},{9,13},{10,14},{11,15},{24,28},{25,29},{26,30},{27,31}} | collective-permute-start | bytes 589832 | tf_op jit(solution)/shard_map/ppermute | solution.py:387
  51.9 6.9 %collective-permute-start.18 = (f32[2,96,384]{2,1,0:T(8,128)S(1)}, f32[2,96,384]{2,1,0:T(8,128)S(1)}, u32[]{:S(2)}, u32[]{:S(2)}) collective-permute-start(f32[2,96,384]{2,1,0:T(8,128)S(1)} %get-tuple-element.47), channel_id=1, source_target_pairs={{4,12},{5,13},{6,14},{7,15},{20,28},{21,29},{22,30},{23,31}} | collective-permute-start | bytes 884744 | tf_op jit(solution)/shard_map/ppermute | solution.py:387
  53.2 7.2 %collective-permute-start.19 = (f32[2,96,384]{2,1,0:T(8,128)S(1)}, f32[2,96,384]{2,1,0:T(8,128)S(1)}, u32[]{:S(2)}, u32[]{:S(2)}) collective-permute-start(f32[2,96,384]{2,1,0:T(8,128)S(1)} %get-tuple-element.48), channel_id=1, source_target_pairs={{4,0},{5,1},{6,2},{7,3},{20,16},{21,17},{22,18},{23,19}} | collective-permute-start | bytes 884744 | tf_op jit(solution)/shard_map/ppermute | solution.py:387
  54.5 5.9 %collective-permute-start.21 = (f32[2,96,384]{2,1,0:T(8,128)S(1)}, f32[2,96,384]{2,1,0:T(8,128)S(1)}, u32[]{:S(2)}, u32[]{:S(2)}) collective-permute-start(f32[2,96,384]{2,1,0:T(8,128)S(1)} %get-tuple-element.50), channel_id=1, source_target_pairs={{8,0},{9,1},{10,2},{11,3},{24,16},{25,17},{26,18},{27,19}} | collective-permute-start | bytes 884744 | tf_op jit(solution)/shard_map/ppermute | solution.py:387
  55.2 23.4 %collective-permute-start.22 = (f32[2,96,384]{2,1,0:T(8,128)S(1)}, f32[2,96,384]{2,1,0:T(8,128)S(1)}, u32[]{:S(2)}, u32[]{:S(2)}) collective-permute-start(f32[2,96,384]{2,1,0:T(8,128)S(1)} %get-tuple-element.51), channel_id=1, source_target_pairs={{8,4},{9,5},{10,6},{11,7},{24,20},{25,21},{26,22},{27,23}} | collective-permute-start | bytes 884744 | tf_op jit(solution)/shard_map/ppermute | solution.py:387
  56.7 3.7 %collective-permute-start.20 = (f32[1,96,384]{2,1,0:T(8,128)S(1)}, f32[1,96,384]{2,1,0:T(8,128)S(1)}, u32[]{:S(2)}, u32[]{:S(2)}) collective-permute-start(f32[1,96,384]{2,1,0:T(8,128)S(1)} %shard_map.45), channel_id=1, source_target_pairs={{8,12},{9,13},{10,14},{11,15},{24,28},{25,29},{26,30},{27,31}} | collective-permute-start | bytes 442376 | tf_op jit(solution)/shard_map/ppermute | solution.py:387
  58.7 24.1 %collective-permute-start.14 = (f32[4,96,192]{2,1,0:T(8,128)S(1)}, f32[4,96,192]{2,1,0:T(8,128)S(1)}, u32[]{:S(2)}, u32[]{:S(2)}) collective-permute-start(f32[4,96,192]{2,1,0:T(8,128)S(1)} %get-tuple-element.43), channel_id=1, source_target_pairs={{0,1},{1,0},{2,3},{3,2},{4,5},{5,4},{6,7},{7,6},{8,9},{9,8},{10,11... | collective-permute-start | bytes 884744 | tf_op jit(solution)/shard_map/ppermute | solution.py:454
  78.8 4.1 %collective-permute-start.23 = (f32[4,96,192]{2,1,0:T(8,128)S(1)}, f32[4,96,192]{2,1,0:T(8,128)S(1)}, u32[]{:S(2)}, u32[]{:S(2)}) collective-permute-start(f32[4,96,192]{2,1,0:T(8,128)S(1)} %get-tuple-element.52), channel_id=1, source_target_pairs={{0,1},{1,0},{2,3},{3,2},{4,5},{5,4},{6,7},{7,6},{8,9},{9,8},{10,11... | collective-permute-start | bytes 884744 | tf_op jit(solution)/shard_map/ppermute | solution.py:454

commit v6 on v5

--- a/solution.py
+++ b/solution.py
@@ -138,7 +138,7 @@
         copy.wait()
 
 
-def start_kernel(mine_ref, got_ref, a0_ref, *refs):
+def start_kernel(mine_ref, got_ref, a0_ref, whole_ref, *refs):
     *prod_refs, a1_ref = refs
     core = lax.axis_index("col")
     part = got_ref.shape[1]
@@ -149,7 +149,9 @@
     row = 0
     for p_ref in prod_refs:
         rows = p_ref.shape[0]
-        p_ref[...] = product(as_left(a0_ref[row:row + rows, :]), right)
+        part = product(as_left(a0_ref[row:row + rows, :]), right)
+        p_ref[...] = part
+        whole_ref[row:row + rows, :] = part
         row += rows
 
 
@@ -168,18 +170,15 @@
     return jnp.concatenate([top, middle, bottom], axis=0)
 
 
-def local_kernel(chunks, *refs):
-    a0_ref, *prod_refs, op_ref = refs[:chunks + 2]
-    sym_ref, g0_ref, g1_ref, b_ref, pack_ref, own_ref, *row_refs = refs[chunks + 2:]
+def local_kernel(*refs):
+    a0_ref, b_ref, op_ref, sym_ref, g0_ref, g1_ref, pack_ref, own_ref, *row_refs = refs
     place = lax.axis_index("tm")
     op = op_ref[lax.axis_index("col")]
     sym = 0.5 * (op + op.T)
     sym_ref[...] = sym
     right = as_right(sym)
-    a0 = a0_ref[...]
-    b = jnp.concatenate([r[...] for r in prod_refs], axis=0)
-    b_ref[...] = b
-    for x, g_ref in ((a0, g0_ref), (b, g1_ref)):
+    for x_ref, g_ref in ((a0_ref, g0_ref), (b_ref, g1_ref)):
+        x = x_ref[...]
         g_ref[...] = product_t(as_left(product(as_left(x), right)), as_right_t(x))
     rows = own_ref.shape[1]
 
@@ -196,13 +195,10 @@
             row_ref[0] = g0_ref[(i + 1) * rows:(i + 2) * rows, :]
 
 
-def hop_kernel(place, in_ref, *refs):
-    *prod_refs, out_ref = refs
-
+def hop_kernel(place, in_ref, step_ref, out_ref):
     @pl.when(lax.axis_index("tm") == place)
     def _():
-        b = jnp.concatenate([r[...] for r in prod_refs], axis=0)
-        out_ref[...] = product(as_left(in_ref[...]), as_right(b))
+        out_ref[...] = product(as_left(in_ref[...]), as_right(step_ref[...]))
 
 
 def joined(out_ref, parts):
@@ -290,7 +286,7 @@
 
 def heis_groups(place, count):
     if place == 1:
-        return [[0], list(range(1, count))]
+        return [[0], list(range(2, count)), [1]]
     return [list(range(place + 1, count)), [place]] if place + 1 < count else []
 
 
@@ -378,8 +374,8 @@
 
     got = lax.ppermute(pick(False), "col", swap)
     mine = pick(True)
-    a0, *prod = local_call(
-        start_kernel, [square] + [chunk] * CHUNKS, (mine, got),
+    a0, whole, *prod = local_call(
+        start_kernel, [square] * 2 + [chunk] * CHUNKS, (mine, got),
         scratch=[pltpu.VMEM(square, jnp.float32)],
     )
 
@@ -394,11 +390,8 @@
 
     soon = [(1, 0)]
     before = [along(x, (0, 1)) for x in prod]
-    shapes = [square] * 4 + [(2, 2 * (order // 3), order), (2, rows, order)] + [(1, rows, order)] * (count - 1)
-    sym, g0, g1, whole, pack, own, *firsts = local_call(
-        lambda *r: local_kernel(CHUNKS, *r), shapes, (a0, *prod, current_op),
-        outside=(CHUNKS + 1,),
-    )
+    shapes = [square] * 3 + [(2, 2 * (order // 3), order), (2, rows, order)] + [(1, rows, order)] * (count - 1)
+    sym, g0, g1, pack, own, *firsts = local_call(local_kernel, shapes, (a0, whole, current_op), outside=(2,))
     last_step = along(whole, (count - 2, count - 1))
     ahead = along(pack, [(j, j - 1) for j in range(2, count)])
     keep(own, 0, [0, 1], 0)
@@ -407,7 +400,7 @@
     for place in range(1, count - 1):
         after = []
         for x in before:
-            after += local_call(lambda *r, p=place: hop_kernel(p, *r), [chunk], (x, *prod))
+            after += local_call(lambda *r, p=place: hop_kernel(p, *r), [chunk], (x, whole))
         passed = after if place < count - 2 else before
         following = [along(x, (place, place + 1)) for x in passed]
         for receivers in heis_groups(place, count):

time: 84.9 us -> 84.9 us (level)
  Pallas kernels: 14.8 us -> 15.8 us
    pallas_call x17 -> x18, Pallas kernels: 9.58 us -> 10.6 us  [local_call(): pl.pallas_call(kernel, out_shape=[pltpu.VMEM(s, jnp.float32) for s in out...]
  transfers between devices with their start and end apart: 24 -> 24, of which waited for: 5 -> 5; matrix products, arithmetic and copies ran while one was open for 0% -> 0% of each run, Pallas kernels for 11% -> 12%
where the time goes in v6:
time: 84.9 us; the launch traced here: 84.5 us
  starting transfers between devices  37.5 us (44%)
  waiting for transfers between devices  30.6 us (36%)
  Pallas kernels  15.8 us (19%)
    ppermute x21, starting transfers between devices, along(): return lax.ppermute(x, 'tm', [hop] if isinstance(hop, tuple) else hop)  32.9 us
    ppermute x21, waiting for transfers between devices, along(): return lax.ppermute(x, 'tm', [hop] if isinstance(hop, tuple) else hop)  30.1 us
    pallas_call x18, Pallas kernels, local_call(): pl.pallas_call(kernel, out_shape=[pltpu.VMEM(s, jnp.float32) for s in out...  10.6 us
    ppermute x2, starting transfers between devices, paired_body(): taken.append(lax.ppermute(give, 'col', swap))  3.83 us
    pallas_call x2, Pallas kernels, spectrum(): pl.pallas_call(lambda *r: spectrum_kernel(own, tables, *r), out_shape=jax...  2.83 us
    pallas_call x2, Pallas kernels, pick(): pl.pallas_call(lambda *r: pick_kernel(own, *r), out_shape=pltpu.VMEM((sli...  2.41 us
  transfers between devices with their start and end apart: 24, of which 5 were waited for; matrix products, arithmetic and copies ran while one was open for 0% of the time, Pallas kernels for 12%

profile of v6, /device:TPU:9, one launch (start us, length us, event | category | flops | bytes accessed | tf_op | source)
XLA Modules:
  0.0 84.5 jit_solution(10601595118238093081)
XLA Ops:
  0.0 1.3 %shard_map.29 = f32[2,192,384]{2,1,0:T(8,128)S(1)} custom-call(f32[2,2,192,384]{3,2,1,0:T(8,128)} %bitcast.1), custom_call_target="tpu_custom_call" | custom-call | tf_op jit(solution)/shard_map/pallas_call | solution.py:366
  1.3 0.7 collective-permute-start
  2.0 1.2 %shard_map.28.mine_ref = f32[2,192,384]{2,1,0:T(8,128)S(1)} custom-call(f32[2,2,192,384]{3,2,1,0:T(8,128)} %bitcast.2), custom_call_target="tpu_custom_call" | custom-call | tf_op jit(solution)/shard_map/pallas_call | solution.py:366
  3.6 0.8 shard_map.30
  4.5 2.3 %shard_map.31 = (f32[384,384]{1,0:T(8,128)S(1)}, f32[384,384]{1,0:T(8,128)S(1)}, f32[384,384]{1,0:T(8,128)S(1)}, f32[2,256,384]{2,1,0:T(8,128)S(1)}, f32[2,96,38...) custom-call(f32[384,384]{1,0:T(8,128)S(1)} %get-tuple-element.29.refs_0_, ...), custom_call_target="tpu_custom_call" | custom-call | tf_op jit(solution)/shard_map/pallas_call | solution.py:115
  6.8 1.3 %collective-permute-start.9 = (f32[2,256,384]{2,1,0:T(8,128)S(1)}, f32[2,256,384]{2,1,0:T(8,128)S(1)}, u32[]{:S(2)}, u32[]{:S(2)}) collective-permute-start(f32[2,256,384]{2,1,0:T(8,128)S(1)} %get-tuple-element.39), channel_id=1, source_target_pairs={{8,4},{12,8},{9,5},{13,9},{10,6},{14,10},{11,7},{15,11},{24,20},{2... | collective-permute-start | bytes 2359304 | tf_op jit(solution)/shard_map/ppermute | solution.py:383
  8.1 1.3 %collective-permute-start.2 = (f32[128,384]{1,0:T(8,128)S(1)}, f32[128,384]{1,0:T(8,128)S(1)}, u32[]{:S(2)}, u32[]{:S(2)}) collective-permute-start(f32[128,384]{1,0:T(8,128)S(1)} %get-tuple-element.36), channel_id=1, source_target_pairs={{0,4},{1,5},{2,6},{3,7},{16,20},{17,21},{18,22},{19,23}} | collective-permute-start | bytes 589832 | tf_op jit(solution)/shard_map/ppermute | solution.py:383
  9.4 1.3 %collective-permute-start.3 = (f32[128,384]{1,0:T(8,128)S(1)}, f32[128,384]{1,0:T(8,128)S(1)}, u32[]{:S(2)}, u32[]{:S(2)}) collective-permute-start(f32[128,384]{1,0:T(8,128)S(1)} %get-tuple-element.37), channel_id=1, source_target_pairs={{0,4},{1,5},{2,6},{3,7},{16,20},{17,21},{18,22},{19,23}} | collective-permute-start | bytes 589832 | tf_op jit(solution)/shard_map/ppermute | solution.py:383
  11.4 1.3 %collective-permute-start.4 = (f32[128,384]{1,0:T(8,128)S(1)}, f32[128,384]{1,0:T(8,128)S(1)}, u32[]{:S(2)}, u32[]{:S(2)}) collective-permute-start(f32[128,384]{1,0:T(8,128)S(1)} %get-tuple-element.38), channel_id=1, source_target_pairs={{0,4},{1,5},{2,6},{3,7},{16,20},{17,21},{18,22},{19,23}} | collective-permute-start | bytes 589832 | tf_op jit(solution)/shard_map/ppermute | solution.py:383
  12.7 3.4 %collective-permute-done.2.r_3_.r_0_ = f32[128,384]{1,0:T(8,128)S(1)} collective-permute-done((f32[128,384]{1,0:T(8,128)S(1)}, f32[128,384]{1,0:T(8,128)S(1)}, u32[]{:S(2)}, u32[]{:S(2)}) %collective-permute-start.2) | collective-permute-done | bytes 196640 | tf_op jit(solution)/shard_map/ppermute | solution.py:383
  17.1 9.4 %collective-permute-start.6 = (f32[128,384]{1,0:T(8,128)S(1)}, f32[128,384]{1,0:T(8,128)S(1)}, u32[]{:S(2)}, u32[]{:S(2)}) collective-permute-start(f32[128,384]{1,0:T(8,128)S(1)} %shard_map.34.r_1_), channel_id=1, source_target_pairs={{4,8},{5,9},{6,10},{7,11},{20,24},{21,25},{22,26},{23,27}} | collective-permute-start | bytes 589832 | tf_op jit(solution)/shard_map/ppermute | solution.py:383
  26.5 1.3 %collective-permute-start.1 = (f32[1,96,384]{2,1,0:T(8,128)S(1)}, f32[1,96,384]{2,1,0:T(8,128)S(1)}, u32[]{:S(2)}, u32[]{:S(2)}) collective-permute-start(f32[1,96,384]{2,1,0:T(8,128)S(1)} %get-tuple-element.32), channel_id=1, source_target_pairs={{0,4},{1,5},{2,6},{3,7},{16,20},{17,21},{18,22},{19,23}} | collective-permute-start | bytes 442376 | tf_op jit(solution)/shard_map/ppermute | solution.py:383
  28.2 1.3 %collective-permute-start.7 = (f32[128,384]{1,0:T(8,128)S(1)}, f32[128,384]{1,0:T(8,128)S(1)}, u32[]{:S(2)}, u32[]{:S(2)}) collective-permute-start(f32[128,384]{1,0:T(8,128)S(1)} %shard_map.35.r_2_), channel_id=1, source_target_pairs={{4,8},{5,9},{6,10},{7,11},{20,24},{21,25},{22,26},{23,27}} | collective-permute-start | bytes 589832 | tf_op jit(solution)/shard_map/ppermute | solution.py:383
  29.5 1.4 %shard_map.44 = (f32[2,96,384]{2,1,0:T(8,128)S(1)}, f32[2,96,384]{2,1,0:T(8,128)S(1)}) custom-call(f32[384,384]{1,0:T(8,128)S(1)} %get-tuple-element.33.r_0_, f32[384,384]{1,0:T(8,128)S(1)} %get-tuple-element.34.r_1_, f32[384,384]{1,0:T(8,128)S(1)} %get-tuple-element.35.r_2_, f32[128,384]{1,0:T(8,128)S(1)} %collective-permute-done.2.r_3_.r_0_, ...), custom_call_target="tpu_custom_call" | custom-call | tf_op jit(solution)/shard_map/pallas_call | solution.py:115
  30.9 1.3 %collective-permute-start.17 = (f32[2,96,384]{2,1,0:T(8,128)S(1)}, f32[2,96,384]{2,1,0:T(8,128)S(1)}, u32[]{:S(2)}, u32[]{:S(2)}) collective-permute-start(f32[2,96,384]{2,1,0:T(8,128)S(1)} %get-tuple-element.44), channel_id=1, source_target_pairs={{4,8},{5,9},{6,10},{7,11},{20,24},{21,25},{22,26},{23,27}} | collective-permute-start | bytes 884744 | tf_op jit(solution)/shard_map/ppermute | solution.py:383
  32.3 0.7 collective-permute-done.1.r_1_
  33.0 0.7 collective-permute-start.10
  34.0 3.8 %collective-permute-start.8 = (f32[128,384]{1,0:T(8,128)S(1)}, f32[128,384]{1,0:T(8,128)S(1)}, u32[]{:S(2)}, u32[]{:S(2)}) collective-permute-start(f32[128,384]{1,0:T(8,128)S(1)} %shard_map.36.r_3_), channel_id=1, source_target_pairs={{4,8},{5,9},{6,10},{7,11},{20,24},{21,25},{22,26},{23,27}} | collective-permute-start | bytes 589832 | tf_op jit(solution)/shard_map/ppermute | solution.py:383
  37.8 1.2 %shard_map.32 = f32[2,96,384]{2,1,0:T(8,128)S(1)} custom-call(f32[384,384]{1,0:T(8,128)S(1)} %get-tuple-element.33.r_0_, f32[384,384]{1,0:T(8,128)S(1)} %get-tuple-element.34.r_1_, f32[384,384]{1,0:T(8,128)S(1)} %get-tuple-element.35.r_2_, f32[128,384]{1,0:T(8,128)S(1)} %collective-permute-done.2.r_3_.r_0_, f32[128,384]{1,0:T(8,128)S(1)} %collective-permute-done.3.r_4_.r_0_, ...), custom_call_target="tpu_custom_call" | custom-call | tf_op jit(solution)/shard_map/pallas_call | solution.py:115
  39.0 1.3 %collective-permute-start.5 = (f32[2,96,384]{2,1,0:T(8,128)S(1)}, f32[2,96,384]{2,1,0:T(8,128)S(1)}, u32[]{:S(2)}, u32[]{:S(2)}) collective-permute-start(f32[2,96,384]{2,1,0:T(8,128)S(1)} %shard_map.32), channel_id=1, source_target_pairs={{4,0},{5,1},{6,2},{7,3},{20,16},{21,17},{22,18},{23,19}} | collective-permute-start | bytes 884744 | tf_op jit(solution)/shard_map/ppermute | solution.py:383
  40.3 7.9 %collective-permute-done.8.r_5_.r_0_ = f32[128,384]{1,0:T(8,128)S(1)} collective-permute-done((f32[128,384]{1,0:T(8,128)S(1)}, f32[128,384]{1,0:T(8,128)S(1)}, u32[]{:S(2)}, u32[]{:S(2)}) %collective-permute-start.8) | collective-permute-done | bytes 196640 | tf_op jit(solution)/shard_map/ppermute | solution.py:383
  50.3 1.5 %shard_map.45 = (f32[2,96,384]{2,1,0:T(8,128)S(1)}, f32[2,96,384]{2,1,0:T(8,128)S(1)}) custom-call(f32[2,256,384]{2,1,0:T(8,128)S(1)} %collective-permute-done.9.r_0_, f32[128,384]{1,0:T(8,128)S(1)} %shard_map.34.r_1_, f32[128,384]{1,0:T(8,128)S(1)} %shard_map.35.r_2_, f32[128,384]{1,0:T(8,128)S(1)} %shard_map.36.r_3_), custom_call_target="tpu_custom_call" | custom-call | tf_op jit(solution)/shard_map/pallas_call | solution.py:115
  51.9 1.3 %collective-permute-start.18 = (f32[2,96,384]{2,1,0:T(8,128)S(1)}, f32[2,96,384]{2,1,0:T(8,128)S(1)}, u32[]{:S(2)}, u32[]{:S(2)}) collective-permute-start(f32[2,96,384]{2,1,0:T(8,128)S(1)} %get-tuple-element.45), channel_id=1, source_target_pairs={{4,12},{5,13},{6,14},{7,15},{20,28},{21,29},{22,30},{23,31}} | collective-permute-start | bytes 884744 | tf_op jit(solution)/shard_map/ppermute | solution.py:383
  53.2 1.3 %collective-permute-start.19 = (f32[2,96,384]{2,1,0:T(8,128)S(1)}, f32[2,96,384]{2,1,0:T(8,128)S(1)}, u32[]{:S(2)}, u32[]{:S(2)}) collective-permute-start(f32[2,96,384]{2,1,0:T(8,128)S(1)} %get-tuple-element.46), channel_id=1, source_target_pairs={{4,0},{5,1},{6,2},{7,3},{20,16},{21,17},{22,18},{23,19}} | collective-permute-start | bytes 884744 | tf_op jit(solution)/shard_map/ppermute | solution.py:383
  54.5 0.7 collective-permute-start.21
  55.2 1.3 %collective-permute-start.22 = (f32[2,96,384]{2,1,0:T(8,128)S(1)}, f32[2,96,384]{2,1,0:T(8,128)S(1)}, u32[]{:S(2)}, u32[]{:S(2)}) collective-permute-start(f32[2,96,384]{2,1,0:T(8,128)S(1)} %get-tuple-element.49), channel_id=1, source_target_pairs={{8,4},{9,5},{10,6},{11,7},{24,20},{25,21},{26,22},{27,23}} | collective-permute-start | bytes 884744 | tf_op jit(solution)/shard_map/ppermute | solution.py:383
  57.4 1.7 %shard_map.33.r_3_ = f32[3,96,384]{2,1,0:T(8,128)S(1)} custom-call(f32[384,384]{1,0:T(8,128)S(1)} %get-tuple-element.33.r_0_, f32[384,384]{1,0:T(8,128)S(1)} %get-tuple-element.34.r_1_, f32[384,384]{1,0:T(8,128)S(1)} %get-tuple-element.35.r_2_, f32[128,384]{1,0:T(8,128)S(1)} %collective-permute-done.2.r_3_.r_0_, ...), custom_call_target="tpu_custom_call" | custom-call | tf_op jit(solution)/shard_map/pallas_call | solution.py:115
  59.4 1.2 %collective-permute-start.14 = (f32[4,96,192]{2,1,0:T(8,128)S(1)}, f32[4,96,192]{2,1,0:T(8,128)S(1)}, u32[]{:S(2)}, u32[]{:S(2)}) collective-permute-start(f32[4,96,192]{2,1,0:T(8,128)S(1)} %get-tuple-element.41), channel_id=1, source_target_pairs={{0,1},{1,0},{2,3},{3,2},{4,5},{5,4},{6,7},{7,6},{8,9},{9,8},{10,11... | collective-permute-start | bytes 884744 | tf_op jit(solution)/shard_map/ppermute | solution.py:447
  60.6 18.1 %collective-permute-done.22.r_8_ = f32[2,96,384]{2,1,0:T(8,128)S(1)} collective-permute-done((f32[2,96,384]{2,1,0:T(8,128)S(1)}, f32[2,96,384]{2,1,0:T(8,128)S(1)}, u32[]{:S(2)}, u32[]{:S(2)}) %collective-permute-start.22) | collective-permute-done | bytes 294944 | tf_op jit(solution)/shard_map/ppermute | solution.py:383
  78.8 2.6 %collective-permute-start.23 = (f32[4,96,192]{2,1,0:T(8,128)S(1)}, f32[4,96,192]{2,1,0:T(8,128)S(1)}, u32[]{:S(2)}, u32[]{:S(2)}) collective-permute-start(f32[4,96,192]{2,1,0:T(8,128)S(1)} %get-tuple-element.50), channel_id=1, source_target_pairs={{0,1},{1,0},{2,3},{3,2},{4,5},{5,4},{6,7},{7,6},{8,9},{9,8},{10,11... | collective-permute-start | bytes 884744 | tf_op jit(solution)/shard_map/ppermute | solution.py:447
  81.4 1.4 %spectrum.2.r_2_ = f32[2,2,8,96,192]{4,3,2,1,0:T(8,128)} custom-call(f32[4,96,192]{2,1,0:T(8,128)S(1)} %get-tuple-element.51.r_0_, f32[4,96,192]{2,1,0:T(8,128)S(1)} %get-tuple-element.52.r_1_), custom_call_target="tpu_custom_call" | custom-call | tf_op jit(solution)/shard_map/spectrum/pallas_call | solution.py:452
  82.9 1.4 %spectrum.3 = f32[2,2,8,96,192]{4,3,2,1,0:T(8,128)} custom-call(f32[4,96,192]{2,1,0:T(8,128)S(1)} %collective-permute-done.14.r_0_, f32[4,96,192]{2,1,0:T(8,128)S(1)} %collective-permute-done.23.r_1_, f32[2,2,8,96,192]{4,3,2,1,0:T(8,128)} %spectrum.2.r_2_), custom_call_target="tpu_custom_call", output_to_operand_aliasing={{}: (2, {})} | custom-call | tf_op jit(solution)/shard_map/spectrum/pallas_call | solution.py:452
  (40 shorter events, 6.2 us)
Async XLA Ops:
  0.0 4.4 %copy-start = (f32[2,384,384]{2,1,0:T(8,128)S(1)}, f32[2,384,384]{2,1,0:T(8,128)}, u32[]{:S(2)}) copy-start(f32[2,384,384]{2,1,0:T(8,128)} %refs_2_.1) | copy-start | bytes 3538948
  1.3 2.4 %collective-permute-start = (f32[2,192,384]{2,1,0:T(8,128)S(1)}, f32[2,192,384]{2,1,0:T(8,128)S(1)}, u32[]{:S(2)}, u32[]{:S(2)}) collective-permute-start(f32[2,192,384]{2,1,0:T(8,128)S(1)} %shard_map.29), channel_id=1, source_target_pairs={{0,1},{1,0},{2,3},{3,2},{4,5},{5,4},{6,7},{7,6},{8,9},{9,8},{10,11... | collective-permute-start | bytes 1769480 | tf_op jit(solution)/shard_map/ppermute | solution.py:375
  6.8 42.8 %collective-permute-start.9 = (f32[2,256,384]{2,1,0:T(8,128)S(1)}, f32[2,256,384]{2,1,0:T(8,128)S(1)}, u32[]{:S(2)}, u32[]{:S(2)}) collective-permute-start(f32[2,256,384]{2,1,0:T(8,128)S(1)} %get-tuple-element.39), channel_id=1, source_target_pairs={{8,4},{12,8},{9,5},{13,9},{10,6},{14,10},{11,7},{15,11},{24,20},{2... | collective-permute-start | bytes 2359304 | tf_op jit(solution)/shard_map/ppermute | solution.py:383
  8.1 8.0 %collective-permute-start.2 = (f32[128,384]{1,0:T(8,128)S(1)}, f32[128,384]{1,0:T(8,128)S(1)}, u32[]{:S(2)}, u32[]{:S(2)}) collective-permute-start(f32[128,384]{1,0:T(8,128)S(1)} %get-tuple-element.36), channel_id=1, source_target_pairs={{0,4},{1,5},{2,6},{3,7},{16,20},{17,21},{18,22},{19,23}} | collective-permute-start | bytes 589832 | tf_op jit(solution)/shard_map/ppermute | solution.py:383
  9.4 17.2 %collective-permute-start.3 = (f32[128,384]{1,0:T(8,128)S(1)}, f32[128,384]{1,0:T(8,128)S(1)}, u32[]{:S(2)}, u32[]{:S(2)}) collective-permute-start(f32[128,384]{1,0:T(8,128)S(1)} %get-tuple-element.37), channel_id=1, source_target_pairs={{0,4},{1,5},{2,6},{3,7},{16,20},{17,21},{18,22},{19,23}} | collective-permute-start | bytes 589832 | tf_op jit(solution)/shard_map/ppermute | solution.py:383
  10.7 6.4 %collective-permute-start.15 = (f32[1,96,384]{2,1,0:T(8,128)S(1)}, f32[1,96,384]{2,1,0:T(8,128)S(1)}, u32[]{:S(2)}, u32[]{:S(2)}) collective-permute-start(f32[1,96,384]{2,1,0:T(8,128)S(1)} %get-tuple-element.42), channel_id=1, source_target_pairs={{0,8},{1,9},{2,10},{3,11},{16,24},{17,25},{18,26},{19,27}} | collective-permute-start | bytes 442376 | tf_op jit(solution)/shard_map/ppermute | solution.py:383
  11.4 16.8 %collective-permute-start.4 = (f32[128,384]{1,0:T(8,128)S(1)}, f32[128,384]{1,0:T(8,128)S(1)}, u32[]{:S(2)}, u32[]{:S(2)}) collective-permute-start(f32[128,384]{1,0:T(8,128)S(1)} %get-tuple-element.38), channel_id=1, source_target_pairs={{0,4},{1,5},{2,6},{3,7},{16,20},{17,21},{18,22},{19,23}} | collective-permute-start | bytes 589832 | tf_op jit(solution)/shard_map/ppermute | solution.py:383
  16.1 14.9 %collective-permute-start.16 = (f32[1,96,384]{2,1,0:T(8,128)S(1)}, f32[1,96,384]{2,1,0:T(8,128)S(1)}, u32[]{:S(2)}, u32[]{:S(2)}) collective-permute-start(f32[1,96,384]{2,1,0:T(8,128)S(1)} %get-tuple-element.43), channel_id=1, source_target_pairs={{0,12},{1,13},{2,14},{3,15},{16,28},{17,29},{18,30},{19,31}} | collective-permute-start | bytes 442376 | tf_op jit(solution)/shard_map/ppermute | solution.py:383
  17.1 16.9 %collective-permute-start.6 = (f32[128,384]{1,0:T(8,128)S(1)}, f32[128,384]{1,0:T(8,128)S(1)}, u32[]{:S(2)}, u32[]{:S(2)}) collective-permute-start(f32[128,384]{1,0:T(8,128)S(1)} %shard_map.34.r_1_), channel_id=1, source_target_pairs={{4,8},{5,9},{6,10},{7,11},{20,24},{21,25},{22,26},{23,27}} | collective-permute-start | bytes 589832 | tf_op jit(solution)/shard_map/ppermute | solution.py:383
  26.5 6.4 %collective-permute-start.1 = (f32[1,96,384]{2,1,0:T(8,128)S(1)}, f32[1,96,384]{2,1,0:T(8,128)S(1)}, u32[]{:S(2)}, u32[]{:S(2)}) collective-permute-start(f32[1,96,384]{2,1,0:T(8,128)S(1)} %get-tuple-element.32), channel_id=1, source_target_pairs={{0,4},{1,5},{2,6},{3,7},{16,20},{17,21},{18,22},{19,23}} | collective-permute-start | bytes 442376 | tf_op jit(solution)/shard_map/ppermute | solution.py:383
  28.2 10.8 %collective-permute-start.7 = (f32[128,384]{1,0:T(8,128)S(1)}, f32[128,384]{1,0:T(8,128)S(1)}, u32[]{:S(2)}, u32[]{:S(2)}) collective-permute-start(f32[128,384]{1,0:T(8,128)S(1)} %shard_map.35.r_2_), channel_id=1, source_target_pairs={{4,8},{5,9},{6,10},{7,11},{20,24},{21,25},{22,26},{23,27}} | collective-permute-start | bytes 589832 | tf_op jit(solution)/shard_map/ppermute | solution.py:383
  30.9 17.9 %collective-permute-start.17 = (f32[2,96,384]{2,1,0:T(8,128)S(1)}, f32[2,96,384]{2,1,0:T(8,128)S(1)}, u32[]{:S(2)}, u32[]{:S(2)}) collective-permute-start(f32[2,96,384]{2,1,0:T(8,128)S(1)} %get-tuple-element.44), channel_id=1, source_target_pairs={{4,8},{5,9},{6,10},{7,11},{20,24},{21,25},{22,26},{23,27}} | collective-permute-start | bytes 884744 | tf_op jit(solution)/shard_map/ppermute | solution.py:383
  33.0 23.7 %collective-permute-start.10 = (f32[384,384]{1,0:T(8,128)S(1)}, f32[384,384]{1,0:T(8,128)S(1)}, u32[]{:S(2)}, u32[]{:S(2)}) collective-permute-start(f32[384,384]{1,0:T(8,128)S(1)} %get-tuple-element.30.refs_1_.r_1_), channel_id=1, source_target_pairs={{8,12},{9,13},{10,14},{11,15},{24,28},{25,29},{26,30},{27,31}} | collective-permute-start | bytes 1769480 | tf_op jit(solution)/shard_map/ppermute | solution.py:383
  34.0 14.2 %collective-permute-start.8 = (f32[128,384]{1,0:T(8,128)S(1)}, f32[128,384]{1,0:T(8,128)S(1)}, u32[]{:S(2)}, u32[]{:S(2)}) collective-permute-start(f32[128,384]{1,0:T(8,128)S(1)} %shard_map.36.r_3_), channel_id=1, source_target_pairs={{4,8},{5,9},{6,10},{7,11},{20,24},{21,25},{22,26},{23,27}} | collective-permute-start | bytes 589832 | tf_op jit(solution)/shard_map/ppermute | solution.py:383
  39.0 12.8 %collective-permute-start.5 = (f32[2,96,384]{2,1,0:T(8,128)S(1)}, f32[2,96,384]{2,1,0:T(8,128)S(1)}, u32[]{:S(2)}, u32[]{:S(2)}) collective-permute-start(f32[2,96,384]{2,1,0:T(8,128)S(1)} %shard_map.32), channel_id=1, source_target_pairs={{4,0},{5,1},{6,2},{7,3},{20,16},{21,17},{22,18},{23,19}} | collective-permute-start | bytes 884744 | tf_op jit(solution)/shard_map/ppermute | solution.py:383
  48.2 5.0 %collective-permute-start.11 = (f32[128,384]{1,0:T(8,128)S(1)}, f32[128,384]{1,0:T(8,128)S(1)}, u32[]{:S(2)}, u32[]{:S(2)}) collective-permute-start(f32[128,384]{1,0:T(8,128)S(1)} %collective-permute-done.6.r_3_.r_0_), channel_id=1, source_target_pairs={{8,12},{9,13},{10,14},{11,15},{24,28},{25,29},{26,30},{27,31}} | collective-permute-start | bytes 589832 | tf_op jit(solution)/shard_map/ppermute | solution.py:383
  48.9 5.6 %collective-permute-start.12 = (f32[128,384]{1,0:T(8,128)S(1)}, f32[128,384]{1,0:T(8,128)S(1)}, u32[]{:S(2)}, u32[]{:S(2)}) collective-permute-start(f32[128,384]{1,0:T(8,128)S(1)} %collective-permute-done.7.r_4_.r_0_), channel_id=1, source_target_pairs={{8,12},{9,13},{10,14},{11,15},{24,28},{25,29},{26,30},{27,31}} | collective-permute-start | bytes 589832 | tf_op jit(solution)/shard_map/ppermute | solution.py:383
  49.6 5.6 %collective-permute-start.13 = (f32[128,384]{1,0:T(8,128)S(1)}, f32[128,384]{1,0:T(8,128)S(1)}, u32[]{:S(2)}, u32[]{:S(2)}) collective-permute-start(f32[128,384]{1,0:T(8,128)S(1)} %collective-permute-done.8.r_5_.r_0_), channel_id=1, source_target_pairs={{8,12},{9,13},{10,14},{11,15},{24,28},{25,29},{26,30},{27,31}} | collective-permute-start | bytes 589832 | tf_op jit(solution)/shard_map/ppermute | solution.py:383
  51.9 7.5 %collective-permute-start.18 = (f32[2,96,384]{2,1,0:T(8,128)S(1)}, f32[2,96,384]{2,1,0:T(8,128)S(1)}, u32[]{:S(2)}, u32[]{:S(2)}) collective-permute-start(f32[2,96,384]{2,1,0:T(8,128)S(1)} %get-tuple-element.45), channel_id=1, source_target_pairs={{4,12},{5,13},{6,14},{7,15},{20,28},{21,29},{22,30},{23,31}} | collective-permute-start | bytes 884744 | tf_op jit(solution)/shard_map/ppermute | solution.py:383
  53.2 7.4 %collective-permute-start.19 = (f32[2,96,384]{2,1,0:T(8,128)S(1)}, f32[2,96,384]{2,1,0:T(8,128)S(1)}, u32[]{:S(2)}, u32[]{:S(2)}) collective-permute-start(f32[2,96,384]{2,1,0:T(8,128)S(1)} %get-tuple-element.46), channel_id=1, source_target_pairs={{4,0},{5,1},{6,2},{7,3},{20,16},{21,17},{22,18},{23,19}} | collective-permute-start | bytes 884744 | tf_op jit(solution)/shard_map/ppermute | solution.py:383
  54.5 6.1 %collective-permute-start.21 = (f32[2,96,384]{2,1,0:T(8,128)S(1)}, f32[2,96,384]{2,1,0:T(8,128)S(1)}, u32[]{:S(2)}, u32[]{:S(2)}) collective-permute-start(f32[2,96,384]{2,1,0:T(8,128)S(1)} %get-tuple-element.48), channel_id=1, source_target_pairs={{8,0},{9,1},{10,2},{11,3},{24,16},{25,17},{26,18},{27,19}} | collective-permute-start | bytes 884744 | tf_op jit(solution)/shard_map/ppermute | solution.py:383
  55.2 23.4 %collective-permute-start.22 = (f32[2,96,384]{2,1,0:T(8,128)S(1)}, f32[2,96,384]{2,1,0:T(8,128)S(1)}, u32[]{:S(2)}, u32[]{:S(2)}) collective-permute-start(f32[2,96,384]{2,1,0:T(8,128)S(1)} %get-tuple-element.49), channel_id=1, source_target_pairs={{8,4},{9,5},{10,6},{11,7},{24,20},{25,21},{26,22},{27,23}} | collective-permute-start | bytes 884744 | tf_op jit(solution)/shard_map/ppermute | solution.py:383
  56.7 3.8 %collective-permute-start.20 = (f32[1,96,384]{2,1,0:T(8,128)S(1)}, f32[1,96,384]{2,1,0:T(8,128)S(1)}, u32[]{:S(2)}, u32[]{:S(2)}) collective-permute-start(f32[1,96,384]{2,1,0:T(8,128)S(1)} %shard_map.46), channel_id=1, source_target_pairs={{8,12},{9,13},{10,14},{11,15},{24,28},{25,29},{26,30},{27,31}} | collective-permute-start | bytes 442376 | tf_op jit(solution)/shard_map/ppermute | solution.py:383
  59.4 23.5 %collective-permute-start.14 = (f32[4,96,192]{2,1,0:T(8,128)S(1)}, f32[4,96,192]{2,1,0:T(8,128)S(1)}, u32[]{:S(2)}, u32[]{:S(2)}) collective-permute-start(f32[4,96,192]{2,1,0:T(8,128)S(1)} %get-tuple-element.41), channel_id=1, source_target_pairs={{0,1},{1,0},{2,3},{3,2},{4,5},{5,4},{6,7},{7,6},{8,9},{9,8},{10,11... | collective-permute-start | bytes 884744 | tf_op jit(solution)/shard_map/ppermute | solution.py:447
  78.8 4.1 %collective-permute-start.23 = (f32[4,96,192]{2,1,0:T(8,128)S(1)}, f32[4,96,192]{2,1,0:T(8,128)S(1)}, u32[]{:S(2)}, u32[]{:S(2)}) collective-permute-start(f32[4,96,192]{2,1,0:T(8,128)S(1)} %get-tuple-element.50), channel_id=1, source_target_pairs={{0,1},{1,0},{2,3},{3,2},{4,5},{5,4},{6,7},{7,6},{8,9},{9,8},{10,11... | collective-permute-start | bytes 884744 | tf_op jit(solution)/shard_map/ppermute | solution.py:447
